TPU v7x, 128 devices: a whole 4x4x4 slice. The times are simulated.
128 devices in a mesh: ctx: 128 (over z, y, x, core).
Axes of the slice: x: 4, y: 4, z: 4, core: 2. Of those that a mesh axis runs over, the one named last changes fastest.
Arguments:
- normed_input: bfloat16 [32768, 5120], P('ctx'), may hold values from -6 to 6
- frozen_query_output: bfloat16 [32768, 5120], P('ctx'), may hold values from -6 to 6
- key_base: bfloat16 [32768, 1024], P('ctx'), may hold values from -6 to 6
- frozen_value_output: bfloat16 [32768, 1024], P('ctx'), may hold values from -6 to 6
- out_grad: bfloat16 [32768, 5120], P('ctx'), may hold values from -6 to 6
- query_down_factor: bfloat16 [5120, 64], replicated, may hold values from -0.078125 to 0.078125
- query_up_factor: bfloat16 [64, 5120], replicated, may hold values from -0.375 to 0.375
- value_down_factor: bfloat16 [5120, 64], replicated, may hold values from -0.078125 to 0.078125
- value_up_factor: bfloat16 [64, 1024], replicated, may hold values from -0.375 to 0.375
- doc_lengths: int32 [64], replicated, may hold values from 1 to 1024, 32768 in all
- stretch_map: int32 [128], replicated, may hold values from 0 to 127, as said below
Outputs:
- attended: bfloat16 [32768, 5120], P('ctx')
- key_grad: bfloat16 [32768, 1024], P('ctx')
- grad_down_q: float32 [5120, 64], replicated
- query_up_gradient: float32 [64, 5120], replicated
- grad_down_v: float32 [5120, 64], replicated
- value_up_gradient: float32 [64, 1024], replicated
Inputs may be any that keep to these rules, and one draw needn't show every extreme that they name: stretch_map is a permutation in which entry i is i or i with its lowest bit flipped; entries 0 and 1, and entries 128 / 2 and 65, are always flipped. `doc_lengths`: the lengths sum to 32768 and the longest is exactly 1024.
All inputs are finite; a program needn't handle non-finite values.
Results may differ from a plain program's by a relative error of at most 0.013.
The roundings to bfloat16 on the way count: a program that leaves them out, or rounds other values in their place, can miss the bound.
Values may be sent and summed in bfloat16 or wider, within the bound.
No kernel may reach another device: no remote copies, remote signals or barrier semaphores. Data moves between devices by JAX's collectives and lax.ppermute only.
A program may use at most 192 MiB of HBM per device.

v0:
```python
import jax
import jax.numpy as jnp
from jax import lax
from jax.sharding import PartitionSpec as P

HD = 128
SPAN = 4


THETA = 1000000.0
ADAPTER_SCALE = 2.0
NEG_FILL = -1e30


def shifted(block, axis, distance):
    devices = range(lax.axis_size(axis))
    route = [(i - distance, i) for i in devices if i - distance in devices]
    return lax.ppermute(block, axis, route)


def rotate(field, places, turning):
    half_width = field.shape[-1] // 2
    inverse = THETA ** (-jnp.arange(half_width, dtype=jnp.float32) * 2.0 / field.shape[-1])
    angles = places.astype(jnp.float32)[:, None] * inverse[None, :]
    cosine = jnp.cos(angles)[:, None, :]
    sine_part = turning * jnp.sin(angles)[:, None, :]
    first = field[..., :half_width]
    second = field[..., half_width:]
    return jnp.concatenate(
        [first * cosine - second * sine_part, second * cosine + first * sine_part], axis=-1
    )


def document_of(places, doc_lengths):
    doc_ends = jnp.cumsum(doc_lengths)
    doc_starts = doc_ends - doc_lengths
    doc_index = jnp.sum((places[:, None] >= doc_ends[None, :]).astype(jnp.int32), axis=1)
    picked = (
        doc_index[:, None] == jnp.arange(doc_lengths.shape[0], dtype=jnp.int32)[None, :]
    ).astype(jnp.int32)
    offset = jnp.sum(picked * doc_starts[None, :], axis=1)
    return (doc_index, places - offset)


def group_attention(query_rows, key_block, value_block, grad_rows, allowed, scaling):
    scores = (
        jnp.einsum("tgd,sd->gts", query_rows, key_block, preferred_element_type=jnp.float32)
        * scaling
    )
    scores = jnp.where(allowed[None], scores, NEG_FILL)
    peak_score = jnp.max(scores, axis=-1, keepdims=True)
    weights = jnp.exp(scores - peak_score)
    attention = weights / jnp.sum(weights, axis=-1, keepdims=True)
    attention_low = attention.astype(jnp.bfloat16)
    attended = jnp.einsum(
        "gts,sd->tgd", attention_low, value_block, preferred_element_type=jnp.float32
    ).astype(jnp.bfloat16)
    row_dot = jnp.sum(grad_rows.astype(jnp.float32) * attended.astype(jnp.float32), axis=-1)
    attention_grad = jnp.einsum(
        "tgd,sd->gts", grad_rows, value_block, preferred_element_type=jnp.float32
    )
    score_grad = (attention * (attention_grad - jnp.transpose(row_dot)[:, :, None])).astype(
        jnp.bfloat16
    )
    query_gradient = (
        jnp.einsum("gts,sd->tgd", score_grad, key_block, preferred_element_type=jnp.float32)
        * scaling
    )
    key_part = (
        jnp.einsum("gts,tgd->sd", score_grad, query_rows, preferred_element_type=jnp.float32)
        * scaling
    )
    value_part = jnp.einsum(
        "gts,tgd->sd", attention_low, grad_rows, preferred_element_type=jnp.float32
    )
    return (attended, query_gradient, key_part, value_part)


def on_device(
    normed_input,
    frozen_query_output,
    key_base,
    frozen_value_output,
    out_grad,
    query_down_factor,
    query_up_factor,
    value_down_factor,
    value_up_factor,
    doc_lengths,
    stretch_map,
):
    row_count = normed_input.shape[0]
    cycle_size = lax.axis_size("ctx")
    my_index = lax.axis_index("ctx")
    groups = key_base.shape[1] // HD
    share = frozen_query_output.shape[1] // key_base.shape[1]
    scaling = HD ** (-0.5)
    row_steps = jnp.arange(row_count, dtype=jnp.int32)
    places = stretch_map[my_index] * row_count + row_steps
    doc_query, local_place = document_of(places, doc_lengths)
    query_adapter_output = jnp.dot(
        normed_input, query_down_factor, preferred_element_type=jnp.float32
    ).astype(jnp.bfloat16)
    value_adapter_output = jnp.dot(
        normed_input, value_down_factor, preferred_element_type=jnp.float32
    ).astype(jnp.bfloat16)
    complete_query = frozen_query_output.astype(jnp.float32) + ADAPTER_SCALE * jnp.dot(
        query_adapter_output, query_up_factor, preferred_element_type=jnp.float32
    )
    query_rot = rotate(
        complete_query.reshape(row_count, groups * share, HD), local_place, 1.0
    ).astype(jnp.bfloat16)
    key_rot = rotate(
        key_base.astype(jnp.float32).reshape(row_count, groups, HD), local_place, 1.0
    ).astype(jnp.bfloat16)
    key_rot = key_rot.reshape(row_count, groups * HD)
    value_row_matrix = (
        frozen_value_output.astype(jnp.float32)
        + ADAPTER_SCALE
        * jnp.dot(value_adapter_output, value_up_factor, preferred_element_type=jnp.float32)
    ).astype(jnp.bfloat16)
    own_pair = jnp.stack([key_rot, value_row_matrix])
    ahead = shifted(own_pair, "ctx", -1)
    behind = []
    for distance in range(1, SPAN + 2):
        behind.append(shifted(own_pair, "ctx", distance))
    pairs = [ahead, own_pair] + behind
    sources = [my_index + 1, my_index] + [my_index - distance for distance in range(1, SPAN + 2)]
    key_places = jnp.concatenate(
        [
            stretch_map[jnp.clip(source, 0, cycle_size - 1)] * row_count + row_steps
            for source in sources
        ]
    )
    present = jnp.concatenate(
        [
            jnp.broadcast_to((source >= 0) & (source < cycle_size), (row_count,))
            for source in sources
        ]
    )
    doc_key, unused_place = document_of(key_places, doc_lengths)
    allowed = (
        (doc_key[None, :] == doc_query[:, None])
        & (key_places[None, :] <= places[:, None])
        & present[None, :]
    )
    gathered = jnp.concatenate(pairs, axis=1)
    span_rows = gathered.shape[1]
    key_groups = jnp.transpose(gathered[0].reshape(span_rows, groups, HD), (1, 0, 2))
    value_groups = jnp.transpose(gathered[1].reshape(span_rows, groups, HD), (1, 0, 2))
    query_groups = jnp.transpose(query_rot.reshape(row_count, groups, share, HD), (1, 0, 2, 3))
    grad_groups = jnp.transpose(out_grad.reshape(row_count, groups, share, HD), (1, 0, 2, 3))

    def one_group(pieces):
        return group_attention(pieces[0], pieces[1], pieces[2], pieces[3], allowed, scaling)

    attended_all, query_all, key_all, value_all = lax.map(
        one_group, (query_groups, key_groups, value_groups, grad_groups)
    )
    attended = jnp.transpose(attended_all, (1, 0, 2, 3)).reshape(row_count, groups * share * HD)
    query_gradient = rotate(
        jnp.transpose(query_all, (1, 0, 2, 3)).reshape(row_count, groups * share, HD),
        local_place,
        -1.0,
    )
    query_gradient = query_gradient.astype(jnp.bfloat16).reshape(row_count, groups * share * HD)
    key_parts = jnp.transpose(key_all, (1, 0, 2)).reshape(span_rows, groups * HD)
    value_parts = jnp.transpose(value_all, (1, 0, 2)).reshape(span_rows, groups * HD)
    grad_pairs = jnp.stack([key_parts, value_parts])

    def block_at(position):
        return grad_pairs[:, position * row_count : (position + 1) * row_count]

    returned = shifted(block_at(0).astype(jnp.bfloat16), "ctx", 1).astype(jnp.float32)
    totals = block_at(1) + returned
    for distance in range(1, SPAN + 2):
        totals = totals + shifted(
            block_at(distance + 1).astype(jnp.bfloat16), "ctx", -distance
        ).astype(jnp.float32)
    key_grad = rotate(totals[0].reshape(row_count, groups, HD), local_place, -1.0).astype(
        jnp.bfloat16
    )
    key_grad = key_grad.reshape(row_count, groups * HD)
    value_gradient = totals[1].astype(jnp.bfloat16)
    query_lifted = (
        ADAPTER_SCALE
        * jnp.dot(query_gradient, query_up_factor.T, preferred_element_type=jnp.float32)
    ).astype(jnp.bfloat16)
    value_lifted = (
        ADAPTER_SCALE
        * jnp.dot(value_gradient, value_up_factor.T, preferred_element_type=jnp.float32)
    ).astype(jnp.bfloat16)
    term_down_q = jnp.einsum(
        "td,tr->dr", normed_input, query_lifted, preferred_element_type=jnp.float32
    )
    query_up_term = ADAPTER_SCALE * jnp.einsum(
        "qp,qs->ps", query_adapter_output, query_gradient, preferred_element_type=jnp.float32
    )
    term_down_v = jnp.einsum(
        "td,tr->dr", normed_input, value_lifted, preferred_element_type=jnp.float32
    )
    value_up_term = ADAPTER_SCALE * jnp.einsum(
        "qp,qs->ps", value_adapter_output, value_gradient, preferred_element_type=jnp.float32
    )
    summed = lax.psum((term_down_q, query_up_term, term_down_v, value_up_term), "ctx")
    tokens_all = row_count * cycle_size
    return (
        attended,
        key_grad,
        summed[0] / tokens_all,
        summed[1] / tokens_all,
        summed[2] / tokens_all,
        summed[3] / tokens_all,
    )


def solution(mesh):
    return jax.shard_map(
        on_device,
        mesh=mesh,
        in_specs=(
            P("ctx", None),
            P("ctx", None),
            P("ctx", None),
            P("ctx", None),
            P("ctx", None),
            P(),
            P(),
            P(),
            P(),
            P(),
            P(),
        ),
        out_specs=(P("ctx", None), P("ctx", None), P(), P(), P(), P()),
        check_vma=False,
    )
```

profile of v0, /device:TPU:62, one launch (start us, length us, event | category | flops | bytes accessed | tf_op | source)
XLA Modules:
  0.0 765.5 jit_solution(9148768812713364856)
XLA Ops:
  26.2 4.3 collective-permute-start.4
  49.0 26.7 %collective-permute-done = bf16[2,256,1024]{2,1,0:T(8,128)(2,1)} collective-permute-done((bf16[2,256,1024]{2,1,0:T(8,128)(2,1)}, bf16[2,256,1024]{2,1,0:T(8,128)(2,1)}, u32[]{:S(2)}, u32[]{:S(2)}) %collective-permute-start) | collective-permute-done | bytes 1048608 | tf_op jit(solution)/shard_map/ppermute | solution.py:18
  75.7 7.0 collective-permute-start.5
  83.0 4.5 copy.62
  95.2 5.6 maximum_bitcast_fusion
  102.1 17.7 %collective-permute-done.1 = bf16[2,256,1024]{2,1,0:T(8,128)(2,1)} collective-permute-done((bf16[2,256,1024]{2,1,0:T(8,128)(2,1)}, bf16[2,256,1024]{2,1,0:T(8,128)(2,1)}, u32[]{:S(2)}, u32[]{:S(2)}) %collective-permute-start.1) | collective-permute-done | bytes 1048608 | tf_op jit(solution)/shard_map/ppermute | solution.py:18
  121.2 9.9 %collective-permute-done.2 = bf16[2,256,1024]{2,1,0:T(8,128)(2,1)} collective-permute-done((bf16[2,256,1024]{2,1,0:T(8,128)(2,1)}, bf16[2,256,1024]{2,1,0:T(8,128)(2,1)}, u32[]{:S(2)}, u32[]{:S(2)}) %collective-permute-start.2) | collective-permute-done | bytes 1048608 | tf_op jit(solution)/shard_map/ppermute | solution.py:18
  142.7 5.9 copy.76
  148.6 296.7 %while.17 = (s32[]{:T(128)}, bf16[8,256,5,128]{1,3,2,0:T(8,128)(2,1)}, f32[8,256,5,128]{1,3,2,0:T(8,128)}, f32[8,1792,128]{1,2,0:T(8,128)}, f32[8,1792,128]{1,2,...) while((s32[]{:T(128)}, ...), condition=%wide.region_8.9_spmd.clone, body=%wide.region_4.8_spmd.clone.sunk | while | flops 3549200896 | bytes 162076848 | solution.py:157
  150.4 7.8 %fusion.153 = (f32[5,256]{1,0:T(8,128)S(1)}, f32[5,256,1792]{1,2,0:T(8,128)}) fusion(pred[256,1792]{0,1:T(8,128)(4,1)S(1)} %and_and_fusion.2, bf16[8,1792,128]{2,1,0:T(8,128)(2,1)} %get-tuple-element.310, s32[]{:T(128)S(6)} %copy.141, bf16[8,256,5,128]{3,1,2,0:T(8,128)(2,1)} %get-tuple-element.311), kind=kOutput, calls=%fused_computation.141.clone.1 | convolution fusion | flops 596379392 | bytes 10426368 | tf_op jit(solution)/shard_map/while/body/eval_jaxpr/sub | solution.py:52
  158.2 4.5 fusion.154
  162.8 4.8 bitcast_dynamic-update-slice_fusion.2
  187.4 7.8 %fusion.153 = (f32[5,256]{1,0:T(8,128)S(1)}, f32[5,256,1792]{1,2,0:T(8,128)}) fusion(pred[256,1792]{0,1:T(8,128)(4,1)S(1)} %and_and_fusion.2, bf16[8,1792,128]{2,1,0:T(8,128)(2,1)} %get-tuple-element.310, s32[]{:T(128)S(6)} %copy.141, bf16[8,256,5,128]{3,1,2,0:T(8,128)(2,1)} %get-tuple-element.311), kind=kOutput, calls=%fused_computation.141.clone.1 | convolution fusion | flops 596379392 | bytes 10426368 | tf_op jit(solution)/shard_map/while/body/eval_jaxpr/sub | solution.py:52
  195.3 4.5 fusion.154
  199.8 4.8 bitcast_dynamic-update-slice_fusion.2
  214.0 4.3 fusion.156
  224.6 7.8 %fusion.153 = (f32[5,256]{1,0:T(8,128)S(1)}, f32[5,256,1792]{1,2,0:T(8,128)}) fusion(pred[256,1792]{0,1:T(8,128)(4,1)S(1)} %and_and_fusion.2, bf16[8,1792,128]{2,1,0:T(8,128)(2,1)} %get-tuple-element.310, s32[]{:T(128)S(6)} %copy.141, bf16[8,256,5,128]{3,1,2,0:T(8,128)(2,1)} %get-tuple-element.311), kind=kOutput, calls=%fused_computation.141.clone.1 | convolution fusion | flops 596379392 | bytes 10426368 | tf_op jit(solution)/shard_map/while/body/eval_jaxpr/sub | solution.py:52
  232.4 4.5 fusion.154
  237.0 4.8 bitcast_dynamic-update-slice_fusion.2
  261.7 7.8 %fusion.153 = (f32[5,256]{1,0:T(8,128)S(1)}, f32[5,256,1792]{1,2,0:T(8,128)}) fusion(pred[256,1792]{0,1:T(8,128)(4,1)S(1)} %and_and_fusion.2, bf16[8,1792,128]{2,1,0:T(8,128)(2,1)} %get-tuple-element.310, s32[]{:T(128)S(6)} %copy.141, bf16[8,256,5,128]{3,1,2,0:T(8,128)(2,1)} %get-tuple-element.311), kind=kOutput, calls=%fused_computation.141.clone.1 | convolution fusion | flops 596379392 | bytes 10426368 | tf_op jit(solution)/shard_map/while/body/eval_jaxpr/sub | solution.py:52
  269.5 4.5 fusion.154
  274.1 4.8 bitcast_dynamic-update-slice_fusion.2
  298.7 7.8 %fusion.153 = (f32[5,256]{1,0:T(8,128)S(1)}, f32[5,256,1792]{1,2,0:T(8,128)}) fusion(pred[256,1792]{0,1:T(8,128)(4,1)S(1)} %and_and_fusion.2, bf16[8,1792,128]{2,1,0:T(8,128)(2,1)} %get-tuple-element.310, s32[]{:T(128)S(6)} %copy.141, bf16[8,256,5,128]{3,1,2,0:T(8,128)(2,1)} %get-tuple-element.311), kind=kOutput, calls=%fused_computation.141.clone.1 | convolution fusion | flops 596379392 | bytes 10426368 | tf_op jit(solution)/shard_map/while/body/eval_jaxpr/sub | solution.py:52
  306.6 4.5 fusion.154
  311.1 4.8 bitcast_dynamic-update-slice_fusion.2
  325.3 4.3 fusion.156
  335.8 7.8 %fusion.153 = (f32[5,256]{1,0:T(8,128)S(1)}, f32[5,256,1792]{1,2,0:T(8,128)}) fusion(pred[256,1792]{0,1:T(8,128)(4,1)S(1)} %and_and_fusion.2, bf16[8,1792,128]{2,1,0:T(8,128)(2,1)} %get-tuple-element.310, s32[]{:T(128)S(6)} %copy.141, bf16[8,256,5,128]{3,1,2,0:T(8,128)(2,1)} %get-tuple-element.311), kind=kOutput, calls=%fused_computation.141.clone.1 | convolution fusion | flops 596379392 | bytes 10426368 | tf_op jit(solution)/shard_map/while/body/eval_jaxpr/sub | solution.py:52
  343.6 4.5 fusion.154
  348.2 4.8 bitcast_dynamic-update-slice_fusion.2
  372.8 7.8 %fusion.153 = (f32[5,256]{1,0:T(8,128)S(1)}, f32[5,256,1792]{1,2,0:T(8,128)}) fusion(pred[256,1792]{0,1:T(8,128)(4,1)S(1)} %and_and_fusion.2, bf16[8,1792,128]{2,1,0:T(8,128)(2,1)} %get-tuple-element.310, s32[]{:T(128)S(6)} %copy.141, bf16[8,256,5,128]{3,1,2,0:T(8,128)(2,1)} %get-tuple-element.311), kind=kOutput, calls=%fused_computation.141.clone.1 | convolution fusion | flops 596379392 | bytes 10426368 | tf_op jit(solution)/shard_map/while/body/eval_jaxpr/sub | solution.py:52
  380.7 4.5 fusion.154
  385.2 4.8 bitcast_dynamic-update-slice_fusion.2
  409.9 7.8 %fusion.153 = (f32[5,256]{1,0:T(8,128)S(1)}, f32[5,256,1792]{1,2,0:T(8,128)}) fusion(pred[256,1792]{0,1:T(8,128)(4,1)S(1)} %and_and_fusion.2, bf16[8,1792,128]{2,1,0:T(8,128)(2,1)} %get-tuple-element.310, s32[]{:T(128)S(6)} %copy.141, bf16[8,256,5,128]{3,1,2,0:T(8,128)(2,1)} %get-tuple-element.311), kind=kOutput, calls=%fused_computation.141.clone.1 | convolution fusion | flops 596379392 | bytes 10426368 | tf_op jit(solution)/shard_map/while/body/eval_jaxpr/sub | solution.py:52
  417.8 4.5 fusion.154
  422.3 4.8 bitcast_dynamic-update-slice_fusion.2
  445.3 9.1 %fusion.59 = bf16[2,1792,1024]{1,2,0:T(8,128)(2,1)} fusion(f32[1,1792,1024]{1,2,0:T(8,128)} %bitcast.225, f32[1,1792,1024]{1,2,0:T(8,128)} %bitcast.227), kind=kLoop, calls=%fused_computation.60 | loop fusion | flops 3670016 | bytes 22020096 | tf_op jit(solution)/shard_map/convert.11
  454.4 5.8 fusion.103
  466.4 6.2 copy.86
  472.6 6.1 copy.85
  484.7 7.1 collective-permute-start.9
  498.2 4.8 subtract_convert_fusion
  507.5 4.8 convolution_bitcast_fusion.3
  512.3 4.5 collective-permute-done.11
  516.9 7.9 %collective-permute-done.10 = bf16[2,256,1024]{1,2,0:T(8,128)(2,1)} collective-permute-done((bf16[2,256,1024]{1,2,0:T(8,128)(2,1)}, bf16[2,256,1024]{1,2,0:T(8,128)(2,1)}, u32[]{:S(2)}, u32[]{:S(2)}) %collective-permute-start.10) | collective-permute-done | bytes 1048608 | tf_op jit(solution)/shard_map/ppermute | solution.py:18
  524.8 42.2 %collective-permute-done.9 = bf16[2,256,1024]{1,2,0:T(8,128)(2,1)} collective-permute-done((bf16[2,256,1024]{1,2,0:T(8,128)(2,1)}, bf16[2,256,1024]{1,2,0:T(8,128)(2,1)}, u32[]{:S(2)}, u32[]{:S(2)}) %collective-permute-start.9) | collective-permute-done | bytes 1048608 | tf_op jit(solution)/shard_map/ppermute | solution.py:18
  567.2 6.8 collective-permute-done.7
  583.7 4.4 copy.69
  597.0 154.8 %all-reduce.3.cloned.1.call-done = (f32[5120,64]{0,1:T(8,128)}, f32[64,5120]{1,0:T(8,128)}, f32[5120,64]{0,1:T(8,128)}, f32[64,1024]{1,0:T(8,128)}) async-done(((f32[5120,64]{0,1:T(8,128)}, f32[64,5120]{1,0:T(8,128)}, f32[5120,64]{0,1:T(8,128)}, f32[64,1024]{1,0:T(8,128)}), (f32[5120,64]{0,1:T(8,128)}, f32[64,5120]{1,0:T(8,128)}, f32[5120,64]{0,1:T(8,128)}, ...) | async-done | bytes 4194320 | tf_op jit(solution)/shard_map/psum | solution.py:205
  (357 shorter events, 252.6 us)
Async XLA Ops:
  7.2 13.7 %copy-start = (bf16[256,5120]{1,0:T(8,128)(2,1)S(1)}, bf16[256,5120]{1,0:T(8,128)(2,1)}, u32[]{:S(2)}) copy-start(bf16[256,5120]{1,0:T(8,128)(2,1)} %param.13) | copy-start | bytes 7864324
  7.2 744.6 %all-reduce.3.cloned.1.call-start = ((), (), s32[]{:S(2)}) async-start(), calls=%async_computation | async-start | bytes 8388608 | tf_op jit(solution)/shard_map/psum | solution.py:205
  19.0 26.4 %copy-start.12 = (f32[256,64]{1,0:T(8,128)}, f32[256,64]{1,0:T(8,128)S(1)}, u32[]{:S(2)}) copy-start(f32[256,64]{1,0:T(8,128)S(1)} %get-tuple-element.170) | copy-start | bytes 196612
  20.8 21.2 %copy-start.20 = (bf16[5120,64]{0,1:T(8,128)(2,1)S(1)}, bf16[5120,64]{0,1:T(8,128)(2,1)}, u32[]{:S(2)}) copy-start(bf16[5120,64]{0,1:T(8,128)(2,1)} %param.18) | copy-start | bytes 1966084
  23.6 20.0 %copy-start.14 = (bf16[64,5120]{1,0:T(8,128)(2,1)S(1)}, bf16[64,5120]{1,0:T(8,128)(2,1)}, u32[]{:S(2)}) copy-start(bf16[64,5120]{1,0:T(8,128)(2,1)} %param.19) | copy-start | bytes 1966084
  23.6 20.0 %copy-start.16 = (bf16[256,5120]{1,0:T(8,128)(2,1)S(1)}, bf16[256,5120]{1,0:T(8,128)(2,1)}, u32[]{:S(2)}) copy-start(bf16[256,5120]{1,0:T(8,128)(2,1)} %param.14) | copy-start | bytes 7864324
  26.2 107.5 %collective-permute-start.4 = (bf16[2,256,1024]{2,1,0:T(8,128)(2,1)}, bf16[2,256,1024]{2,1,0:T(8,128)(2,1)}, u32[]{:S(2)}, u32[]{:S(2)}) collective-permute-start(bf16[2,256,1024]{2,1,0:T(8,128)(2,1)} %pad_maximum_fusion.2), channel_id=1, source_target_pairs={{0,4},{1,5},{2,6},{3,7},{4,8},{5,9},{6,10},{7,11},{8,12},{9,13},{1... | collective-permute-start | bytes 3145736 | tf_op jit(solution)/shard_map/ppermute | solution.py:18
  30.5 101.9 %collective-permute-start.3 = (bf16[2,256,1024]{2,1,0:T(8,128)(2,1)}, bf16[2,256,1024]{2,1,0:T(8,128)(2,1)}, u32[]{:S(2)}, u32[]{:S(2)}) collective-permute-start(bf16[2,256,1024]{2,1,0:T(8,128)(2,1)} %pad_maximum_fusion.2), channel_id=1, source_target_pairs={{0,3},{1,4},{2,5},{3,6},{4,7},{5,8},{6,9},{7,10},{8,11},{9,12},{10... | collective-permute-start | bytes 3145736 | tf_op jit(solution)/shard_map/ppermute | solution.py:18
  33.7 97.4 %collective-permute-start.2 = (bf16[2,256,1024]{2,1,0:T(8,128)(2,1)}, bf16[2,256,1024]{2,1,0:T(8,128)(2,1)}, u32[]{:S(2)}, u32[]{:S(2)}) collective-permute-start(bf16[2,256,1024]{2,1,0:T(8,128)(2,1)} %pad_maximum_fusion.2), channel_id=1, source_target_pairs={{0,2},{1,3},{2,4},{3,5},{4,6},{5,7},{6,8},{7,9},{8,10},{9,11},{10,... | collective-permute-start | bytes 3145736 | tf_op jit(solution)/shard_map/ppermute | solution.py:18
  36.4 83.5 %collective-permute-start.1 = (bf16[2,256,1024]{2,1,0:T(8,128)(2,1)}, bf16[2,256,1024]{2,1,0:T(8,128)(2,1)}, u32[]{:S(2)}, u32[]{:S(2)}) collective-permute-start(bf16[2,256,1024]{2,1,0:T(8,128)(2,1)} %pad_maximum_fusion.2), channel_id=1, source_target_pairs={{0,1},{1,2},{2,3},{3,4},{4,5},{5,6},{6,7},{7,8},{8,9},{9,10},{10,1... | collective-permute-start | bytes 3145736 | tf_op jit(solution)/shard_map/ppermute | solution.py:18
  39.7 36.0 %collective-permute-start = (bf16[2,256,1024]{2,1,0:T(8,128)(2,1)}, bf16[2,256,1024]{2,1,0:T(8,128)(2,1)}, u32[]{:S(2)}, u32[]{:S(2)}) collective-permute-start(bf16[2,256,1024]{2,1,0:T(8,128)(2,1)} %pad_maximum_fusion.2), channel_id=1, source_target_pairs={{1,0},{2,1},{3,2},{4,3},{5,4},{6,5},{7,6},{8,7},{9,8},{10,9},{11,1... | collective-permute-start | bytes 3145736 | tf_op jit(solution)/shard_map/ppermute | solution.py:18
  45.4 37.4 %copy-start.36 = (s32[64]{0:T(128)S(1)}, s32[64]{0:T(128)}, u32[]{:S(2)}) copy-start(s32[64]{0:T(128)} %copy-done.35) | copy-start | bytes 772
  75.7 59.3 %collective-permute-start.5 = (bf16[2,256,1024]{2,1,0:T(8,128)(2,1)}, bf16[2,256,1024]{2,1,0:T(8,128)(2,1)}, u32[]{:S(2)}, u32[]{:S(2)}) collective-permute-start(bf16[2,256,1024]{2,1,0:T(8,128)(2,1)} %pad_maximum_fusion.2), channel_id=1, source_target_pairs={{0,5},{1,6},{2,7},{3,8},{4,9},{5,10},{6,11},{7,12},{8,13},{9,14},{... | collective-permute-start | bytes 3145736 | tf_op jit(solution)/shard_map/ppermute | solution.py:18
  148.7 9.5 %copy-start.27 = (pred[1792]{0:T(1024)(128)(4,1)}, pred[1792]{0:T(1024)(128)(4,1)S(1)}, u32[]{:S(2)}) copy-start(pred[1792]{0:T(1024)(128)(4,1)S(1)} %get-tuple-element.317) | copy-start | bytes 5380 | tf_op jit(solution)/shard_map/while
  158.2 10.4 %copy-start.4 = (f32[5,256,1792]{1,2,0:T(8,128)S(1)}, f32[5,256,1792]{1,2,0:T(8,128)}, u32[]{:S(2)}) copy-start(f32[5,256,1792]{1,2,0:T(8,128)} %get-tuple-element.270) | copy-start | bytes 27525124 | tf_op jit(solution)/shard_map/while
  162.8 8.4 %copy-start.1 = (bf16[5,256,1792]{1,2,0:T(8,128)(2,1)}, bf16[5,256,1792]{1,2,0:T(8,128)(2,1)S(1)}, u32[]{:S(2)}) copy-start(bf16[5,256,1792]{1,2,0:T(8,128)(2,1)S(1)} %fusion.154) | copy-start | bytes 13762564 | tf_op jit(solution)/shard_map/while
  185.8 9.5 %copy-start.27 = (pred[1792]{0:T(1024)(128)(4,1)}, pred[1792]{0:T(1024)(128)(4,1)S(1)}, u32[]{:S(2)}) copy-start(pred[1792]{0:T(1024)(128)(4,1)S(1)} %get-tuple-element.317) | copy-start | bytes 5380 | tf_op jit(solution)/shard_map/while
  195.3 10.4 %copy-start.4 = (f32[5,256,1792]{1,2,0:T(8,128)S(1)}, f32[5,256,1792]{1,2,0:T(8,128)}, u32[]{:S(2)}) copy-start(f32[5,256,1792]{1,2,0:T(8,128)} %get-tuple-element.270) | copy-start | bytes 27525124 | tf_op jit(solution)/shard_map/while
  199.8 8.5 %copy-start.1 = (bf16[5,256,1792]{1,2,0:T(8,128)(2,1)}, bf16[5,256,1792]{1,2,0:T(8,128)(2,1)S(1)}, u32[]{:S(2)}) copy-start(bf16[5,256,1792]{1,2,0:T(8,128)(2,1)S(1)} %fusion.154) | copy-start | bytes 13762564 | tf_op jit(solution)/shard_map/while
  223.0 9.5 %copy-start.27 = (pred[1792]{0:T(1024)(128)(4,1)}, pred[1792]{0:T(1024)(128)(4,1)S(1)}, u32[]{:S(2)}) copy-start(pred[1792]{0:T(1024)(128)(4,1)S(1)} %get-tuple-element.317) | copy-start | bytes 5380 | tf_op jit(solution)/shard_map/while
  232.4 10.4 %copy-start.4 = (f32[5,256,1792]{1,2,0:T(8,128)S(1)}, f32[5,256,1792]{1,2,0:T(8,128)}, u32[]{:S(2)}) copy-start(f32[5,256,1792]{1,2,0:T(8,128)} %get-tuple-element.270) | copy-start | bytes 27525124 | tf_op jit(solution)/shard_map/while
  237.0 8.5 %copy-start.1 = (bf16[5,256,1792]{1,2,0:T(8,128)(2,1)}, bf16[5,256,1792]{1,2,0:T(8,128)(2,1)S(1)}, u32[]{:S(2)}) copy-start(bf16[5,256,1792]{1,2,0:T(8,128)(2,1)S(1)} %fusion.154) | copy-start | bytes 13762564 | tf_op jit(solution)/shard_map/while
  260.0 9.5 %copy-start.27 = (pred[1792]{0:T(1024)(128)(4,1)}, pred[1792]{0:T(1024)(128)(4,1)S(1)}, u32[]{:S(2)}) copy-start(pred[1792]{0:T(1024)(128)(4,1)S(1)} %get-tuple-element.317) | copy-start | bytes 5380 | tf_op jit(solution)/shard_map/while
  269.5 10.4 %copy-start.4 = (f32[5,256,1792]{1,2,0:T(8,128)S(1)}, f32[5,256,1792]{1,2,0:T(8,128)}, u32[]{:S(2)}) copy-start(f32[5,256,1792]{1,2,0:T(8,128)} %get-tuple-element.270) | copy-start | bytes 27525124 | tf_op jit(solution)/shard_map/while
  274.0 8.4 %copy-start.1 = (bf16[5,256,1792]{1,2,0:T(8,128)(2,1)}, bf16[5,256,1792]{1,2,0:T(8,128)(2,1)S(1)}, u32[]{:S(2)}) copy-start(bf16[5,256,1792]{1,2,0:T(8,128)(2,1)S(1)} %fusion.154) | copy-start | bytes 13762564 | tf_op jit(solution)/shard_map/while
  297.1 9.5 %copy-start.27 = (pred[1792]{0:T(1024)(128)(4,1)}, pred[1792]{0:T(1024)(128)(4,1)S(1)}, u32[]{:S(2)}) copy-start(pred[1792]{0:T(1024)(128)(4,1)S(1)} %get-tuple-element.317) | copy-start | bytes 5380 | tf_op jit(solution)/shard_map/while
  306.6 10.4 %copy-start.4 = (f32[5,256,1792]{1,2,0:T(8,128)S(1)}, f32[5,256,1792]{1,2,0:T(8,128)}, u32[]{:S(2)}) copy-start(f32[5,256,1792]{1,2,0:T(8,128)} %get-tuple-element.270) | copy-start | bytes 27525124 | tf_op jit(solution)/shard_map/while
  311.1 8.4 %copy-start.1 = (bf16[5,256,1792]{1,2,0:T(8,128)(2,1)}, bf16[5,256,1792]{1,2,0:T(8,128)(2,1)S(1)}, u32[]{:S(2)}) copy-start(bf16[5,256,1792]{1,2,0:T(8,128)(2,1)S(1)} %fusion.154) | copy-start | bytes 13762564 | tf_op jit(solution)/shard_map/while
  334.2 9.5 %copy-start.27 = (pred[1792]{0:T(1024)(128)(4,1)}, pred[1792]{0:T(1024)(128)(4,1)S(1)}, u32[]{:S(2)}) copy-start(pred[1792]{0:T(1024)(128)(4,1)S(1)} %get-tuple-element.317) | copy-start | bytes 5380 | tf_op jit(solution)/shard_map/while
  343.6 10.4 %copy-start.4 = (f32[5,256,1792]{1,2,0:T(8,128)S(1)}, f32[5,256,1792]{1,2,0:T(8,128)}, u32[]{:S(2)}) copy-start(f32[5,256,1792]{1,2,0:T(8,128)} %get-tuple-element.270) | copy-start | bytes 27525124 | tf_op jit(solution)/shard_map/while
  348.2 8.4 %copy-start.1 = (bf16[5,256,1792]{1,2,0:T(8,128)(2,1)}, bf16[5,256,1792]{1,2,0:T(8,128)(2,1)S(1)}, u32[]{:S(2)}) copy-start(bf16[5,256,1792]{1,2,0:T(8,128)(2,1)S(1)} %fusion.154) | copy-start | bytes 13762564 | tf_op jit(solution)/shard_map/while
  371.2 9.5 %copy-start.27 = (pred[1792]{0:T(1024)(128)(4,1)}, pred[1792]{0:T(1024)(128)(4,1)S(1)}, u32[]{:S(2)}) copy-start(pred[1792]{0:T(1024)(128)(4,1)S(1)} %get-tuple-element.317) | copy-start | bytes 5380 | tf_op jit(solution)/shard_map/while
  380.7 10.4 %copy-start.4 = (f32[5,256,1792]{1,2,0:T(8,128)S(1)}, f32[5,256,1792]{1,2,0:T(8,128)}, u32[]{:S(2)}) copy-start(f32[5,256,1792]{1,2,0:T(8,128)} %get-tuple-element.270) | copy-start | bytes 27525124 | tf_op jit(solution)/shard_map/while
  385.2 8.4 %copy-start.1 = (bf16[5,256,1792]{1,2,0:T(8,128)(2,1)}, bf16[5,256,1792]{1,2,0:T(8,128)(2,1)S(1)}, u32[]{:S(2)}) copy-start(bf16[5,256,1792]{1,2,0:T(8,128)(2,1)S(1)} %fusion.154) | copy-start | bytes 13762564 | tf_op jit(solution)/shard_map/while
  408.3 9.5 %copy-start.27 = (pred[1792]{0:T(1024)(128)(4,1)}, pred[1792]{0:T(1024)(128)(4,1)S(1)}, u32[]{:S(2)}) copy-start(pred[1792]{0:T(1024)(128)(4,1)S(1)} %get-tuple-element.317) | copy-start | bytes 5380 | tf_op jit(solution)/shard_map/while
  417.8 10.4 %copy-start.4 = (f32[5,256,1792]{1,2,0:T(8,128)S(1)}, f32[5,256,1792]{1,2,0:T(8,128)}, u32[]{:S(2)}) copy-start(f32[5,256,1792]{1,2,0:T(8,128)} %get-tuple-element.270) | copy-start | bytes 27525124 | tf_op jit(solution)/shard_map/while
  422.3 8.4 %copy-start.1 = (bf16[5,256,1792]{1,2,0:T(8,128)(2,1)}, bf16[5,256,1792]{1,2,0:T(8,128)(2,1)S(1)}, u32[]{:S(2)}) copy-start(bf16[5,256,1792]{1,2,0:T(8,128)(2,1)S(1)} %fusion.154) | copy-start | bytes 13762564 | tf_op jit(solution)/shard_map/while
  454.4 9.3 %copy-start.9 = (f32[8,256,5,128]{1,3,2,0:T(8,128)S(1)}, f32[8,256,5,128]{1,3,2,0:T(8,128)}, u32[]{:S(2)}) copy-start(f32[8,256,5,128]{1,3,2,0:T(8,128)} %get-tuple-element.360) | copy-start | bytes 15728644
  460.2 33.7 %collective-permute-start.6 = (bf16[2,256,1024]{1,2,0:T(8,128)(2,1)}, bf16[2,256,1024]{1,2,0:T(8,128)(2,1)}, u32[]{:S(2)}, u32[]{:S(2)}) collective-permute-start(bf16[2,256,1024]{1,2,0:T(8,128)(2,1)} %get-tuple-element.150), channel_id=1, source_target_pairs={{0,1},{1,2},{2,3},{3,4},{4,5},{5,6},{6,7},{7,8},{8,9},{9,10},{10,1... | collective-permute-start | bytes 3145736 | tf_op jit(solution)/shard_map/ppermute | solution.py:18
  472.6 25.5 %copy-start.13 = (f32[256,64]{1,0:T(8,128)S(1)}, f32[256,64]{1,0:T(8,128)}, u32[]{:S(2)}) copy-start(f32[256,64]{1,0:T(8,128)} %copy-done.12) | copy-start | bytes 196612
  472.6 25.5 %copy-start.19 = (f32[256,64]{1,0:T(8,128)S(1)}, f32[256,64]{1,0:T(8,128)}, u32[]{:S(2)}) copy-start(f32[256,64]{1,0:T(8,128)} %get-tuple-element.168) | copy-start | bytes 196612
  478.7 38.1 %collective-permute-start.11 = (bf16[2,256,1024]{1,2,0:T(8,128)(2,1)}, bf16[2,256,1024]{1,2,0:T(8,128)(2,1)}, u32[]{:S(2)}, u32[]{:S(2)}) collective-permute-start(bf16[2,256,1024]{1,2,0:T(8,128)(2,1)} %get-tuple-element.151), channel_id=1, source_target_pairs={{5,0},{6,1},{7,2},{8,3},{9,4},{10,5},{11,6},{12,7},{13,8},{14,9},{... | collective-permute-start | bytes 3145736 | tf_op jit(solution)/shard_map/ppermute | solution.py:18
  480.6 44.2 %collective-permute-start.10 = (bf16[2,256,1024]{1,2,0:T(8,128)(2,1)}, bf16[2,256,1024]{1,2,0:T(8,128)(2,1)}, u32[]{:S(2)}, u32[]{:S(2)}) collective-permute-start(bf16[2,256,1024]{1,2,0:T(8,128)(2,1)} %get-tuple-element.152), channel_id=1, source_target_pairs={{4,0},{5,1},{6,2},{7,3},{8,4},{9,5},{10,6},{11,7},{12,8},{13,9},{1... | collective-permute-start | bytes 3145736 | tf_op jit(solution)/shard_map/ppermute | solution.py:18
  484.7 82.3 %collective-permute-start.9 = (bf16[2,256,1024]{1,2,0:T(8,128)(2,1)}, bf16[2,256,1024]{1,2,0:T(8,128)(2,1)}, u32[]{:S(2)}, u32[]{:S(2)}) collective-permute-start(bf16[2,256,1024]{1,2,0:T(8,128)(2,1)} %get-tuple-element.153), channel_id=1, source_target_pairs={{3,0},{4,1},{5,2},{6,3},{7,4},{8,5},{9,6},{10,7},{11,8},{12,9},{13... | collective-permute-start | bytes 3145736 | tf_op jit(solution)/shard_map/ppermute | solution.py:18
  491.8 75.3 %collective-permute-start.8 = (bf16[2,256,1024]{1,2,0:T(8,128)(2,1)}, bf16[2,256,1024]{1,2,0:T(8,128)(2,1)}, u32[]{:S(2)}, u32[]{:S(2)}) collective-permute-start(bf16[2,256,1024]{1,2,0:T(8,128)(2,1)} %get-tuple-element.154), channel_id=1, source_target_pairs={{2,0},{3,1},{4,2},{5,3},{6,4},{7,5},{8,6},{9,7},{10,8},{11,9},{12,... | collective-permute-start | bytes 3145736 | tf_op jit(solution)/shard_map/ppermute | solution.py:18
  493.9 80.0 %collective-permute-start.7 = (bf16[2,256,1024]{1,2,0:T(8,128)(2,1)}, bf16[2,256,1024]{1,2,0:T(8,128)(2,1)}, u32[]{:S(2)}, u32[]{:S(2)}) collective-permute-start(bf16[2,256,1024]{1,2,0:T(8,128)(2,1)} %get-tuple-element.155), channel_id=1, source_target_pairs={{1,0},{2,1},{3,2},{4,3},{5,4},{6,5},{7,6},{8,7},{9,8},{10,9},{11,1... | collective-permute-start | bytes 3145736 | tf_op jit(solution)/shard_map/ppermute | solution.py:18
  512.3 67.2 %copy-start.26 = (bf16[256,64]{0,1:T(8,128)(2,1)S(1)}, bf16[256,64]{0,1:T(8,128)(2,1)}, u32[]{:S(2)}) copy-start(bf16[256,64]{0,1:T(8,128)(2,1)} %copy-done.25) | copy-start | bytes 98308
  512.3 68.2 %copy-start.22 = (bf16[64,1024]{1,0:T(8,128)(2,1)S(1)}, bf16[64,1024]{1,0:T(8,128)(2,1)}, u32[]{:S(2)}) copy-start(bf16[64,1024]{1,0:T(8,128)(2,1)} %param.21) | copy-start | bytes 393220
  (65 other events, 248.1 us)
Sparse Core Ops, SparseCore 0:
  583.8 167.9 all-reduce.2
where the time goes:
time: 778 us; the launch traced here: 765 us
  waiting for transfers between devices  271 us (35%)
  matrix products  219 us (28%)
  local copies, waits for them, and re-layouts  108 us (14%)
  other arithmetic  101 us (13%)
  starting transfers between devices  45.7 us (6%)
  between operations  20 us (3%)
    psum x1, waiting for transfers between devices, on_device(): lax.psum((term_down_q, query_up_term, term_down_v, value_up_term), 'ctx')  155 us
    ppermute x12, waiting for transfers between devices, shifted(): return lax.ppermute(block, axis, route)  116 us
    sub x8, matrix products, group_attention(): weights = jnp.exp(scores - peak_score)  62.7 us
    ppermute x12, starting transfers between devices, shifted(): return lax.ppermute(block, axis, route)  45.7 us
    unnamed x78, local copies, waits for them, and re-layouts  43.3 us
    dot_general x8, matrix products, group_attention(): jnp.einsum('gts,sd->tgd', attention_low, value_block, preferred_element_t...  38.3 us
    convert_element_type x8, other arithmetic, group_attention(): attention_low = attention.astype(jnp.bfloat16)  36.3 us
    dot_general x8, matrix products, group_attention(): jnp.einsum('gts,sd->tgd', score_grad, key_block, preferred_element_type=j...  34.1 us
  transfers between devices with their start and end apart: 13, of which 9 were waited for; matrix products, arithmetic and copies ran while one was open for 9% of the time, Pallas kernels for 0%

commit v1 on v0

v1 whole, which is shorter than its diff:
```python
import functools

import jax
import jax.numpy as jnp
from jax import lax
from jax.experimental import pallas as pl
from jax.experimental.pallas import tpu as pltpu
from jax.sharding import PartitionSpec as P

HD = 128
RANK = 64
TOK = 256
SUB = 128
REACH = 1152
SPANK = 5 * TOK
ROWS = 7 * TOK
KP = 384
HEADS = 8
SHARE = 5
COUNTS = (2, 3, 3)
THETA = 1000000.0
ADAPTER_SCALE = 2.0
LOG2E = 1.4426950408889634
NEG = -1e30
BF = jnp.bfloat16
F32 = jnp.float32


def mm(a, b):
    return lax.dot_general(a, b, (((1,), (0,)), ((), ())), preferred_element_type=F32)


def mm_nt(a, b):
    return lax.dot_general(a, b, (((1,), (1,)), ((), ())), preferred_element_type=F32)


def mm_tn(a, b):
    return lax.dot_general(a, b, (((0,), (0,)), ((), ())), preferred_element_type=F32)


def attention_kernel(share, first_call, sc, fq, og, lora, qup, vup, cos, sin, dst, *rest):
    kin, vin, lin = rest[0:6], rest[6:12], rest[12:18]
    rest = rest[18:] if first_call else rest[19:]
    att, dkm, dko, liftq, qupg, vupg, lvm, lvo = rest[0:8]
    kx, vx, kt, vt, lt, bias, ss, dp, dka, dva, qn, dn, dnt, dqn, lva = rest[8:]
    g = pl.program_id(0)
    groups = pl.num_programs(0)
    wide = share * SUB
    scale = HD ** (-0.5)
    cexp = scale * LOG2E
    shift = pl.multiple_of(sc[0], TOK)

    def place(target, refs):
        for chip in range(3):
            low = pl.multiple_of((2 - chip) * 2 * TOK + shift, TOK)
            mine, other = refs[2 * chip], refs[2 * chip + 1]

            @pl.when(sc[1 + chip] == 0)
            def _():
                target[pl.ds(low, TOK), :] = mine[...]
                target[pl.ds(low + TOK, TOK), :] = other[...]

            @pl.when(sc[1 + chip] != 0)
            def _():
                target[pl.ds(low, TOK), :] = other[...]
                target[pl.ds(low + TOK, TOK), :] = mine[...]

    def take(read, mine, other):
        for chip in range(3):
            low = pl.multiple_of((2 - chip) * 2 * TOK + shift, TOK)

            @pl.when(sc[1 + chip] == 0)
            def _():
                mine[chip] = read(pl.ds(low, TOK))
                other[chip] = read(pl.ds(low + TOK, TOK))

            @pl.when(sc[1 + chip] != 0)
            def _():
                mine[chip] = read(pl.ds(low + TOK, TOK))
                other[chip] = read(pl.ds(low, TOK))

    @pl.when(g == 0)
    def _():
        for piece in (slice(0, TOK), slice(TOK + SPANK, ROWS)):
            dka[piece, :] = jnp.zeros((TOK, HD), F32)
            dva[piece, :] = jnp.zeros((TOK, HD), F32)
        lva[...] = jnp.zeros_like(lva)
        liftq[...] = jnp.zeros_like(liftq)
        place(kx, lin)
        lt[...] = kx[TOK : TOK + SPANK, :].T
        for b in range(2):
            first = dst[0:1, b * SUB : (b + 1) * SUB]
            last = SPANK - 2 * SUB + b * SUB + lax.broadcasted_iota(jnp.int32, (1, SUB), 1)
            key_at = b * SUB + lax.broadcasted_iota(jnp.int32, (REACH, SUB), 0)
            bias[b] = jnp.where((key_at >= first) & (key_at <= last), 0.0, NEG)

    place(kx, kin)
    place(vx, vin)
    kt[...] = kx[TOK : TOK + SPANK, :].T
    vt[...] = vx[TOK : TOK + SPANK, :].T
    lora_q = lora[:, 0:RANK]
    extra = mm(lora_q, qup[...])
    for h in range(share):
        col = slice(h * HD, (h + 1) * HD)
        u = fq[:, col].astype(F32) + ADAPTER_SCALE * extra[:, col]
        qr = (u * cos[...] + pltpu.roll(u, HD // 2, 1) * sin[...]).astype(BF)
        for b in range(2):
            qn[b, h * SUB : (h + 1) * SUB, :] = qr[b * SUB : (b + 1) * SUB]
            dn[b, h * SUB : (h + 1) * SUB, :] = og[b * SUB : (b + 1) * SUB, col]
    pieces = [slice(i, i + KP) for i in range(0, REACH, KP)]

    keep = {}

    def phase_a(b):
        dnt[b] = dn[b].astype(F32).T
        at = TOK + b * SUB
        top = None
        for piece in pieces:
            s = mm_nt(kx[at + piece.start : at + piece.stop, :], qn[b])
            s = s + jnp.concatenate([bias[b, piece, :]] * share, axis=1)
            ss[b, piece, :] = s
            t = jnp.max(s.reshape(KP // 8, 8, wide), axis=0)
            top = t if top is None else jnp.maximum(top, t)
        keep["top", b] = jnp.max(top, axis=0, keepdims=True) * cexp

    def phase_p(b):
        at = TOK + b * SUB
        for piece in pieces:
            dp[b, piece, :] = mm_nt(vx[at + piece.start : at + piece.stop, :], dn[b])

    def phase_b(b):
        total = None
        for piece in pieces:
            e = jnp.exp2(ss[b, piece, :] * cexp - keep["top", b])
            ss[b, piece, :] = e
            t = jnp.sum(e.reshape(KP // 8, 8, wide), axis=0)
            total = t if total is None else total + t
        keep["inverse", b] = 1.0 / jnp.sum(total, axis=0, keepdims=True)

    def add(target, b, piece, value):
        rows = slice(TOK + b * SUB + piece.start, TOK + b * SUB + piece.stop)
        if b == 0:
            target[rows, :] = value
        elif piece.stop < REACH:
            target[rows, :] += value
        else:
            cut = KP - SUB
            target[rows.start : rows.start + cut, :] += value[:cut]
            target[rows.start + cut : rows.stop, :] = value[cut:]

    def phase_c(b):
        ot = None
        for piece in pieces:
            pb = (ss[b, piece, :] * keep["inverse", b]).astype(BF)
            t = mm(vt[:, b * SUB + piece.start : b * SUB + piece.stop], pb)
            ot = t if ot is None else ot + t
            add(dva, b, piece, mm(pb, dn[b]))
        ob = ot.astype(BF).astype(F32)
        keep["dot", b] = jnp.sum(dnt[b] * ob, axis=0, keepdims=True)
        obn = ob.T.astype(BF)
        for h in range(share):
            att[b * SUB : (b + 1) * SUB, h * HD : (h + 1) * HD] = obn[h * SUB : (h + 1) * SUB]

    def phase_d(b):
        qt = None
        for piece in pieces:
            ds = ((ss[b, piece, :] * keep["inverse", b]) * (dp[b, piece, :] - keep["dot", b])).astype(BF)
            t = mm(kt[:, b * SUB + piece.start : b * SUB + piece.stop], ds)
            qt = t if qt is None else qt + t
            add(dka, b, piece, mm(ds, qn[b]))
        dq = qt.T * scale
        rows = slice(b * SUB, (b + 1) * SUB)
        for h in range(share):
            u = dq[h * SUB : (h + 1) * SUB]
            dqn[rows, h * HD : (h + 1) * HD] = (
                u * cos[rows, :] - pltpu.roll(u, HD // 2, 1) * sin[rows, :]
            ).astype(BF)

    phase_a(0)
    phase_b(0)
    phase_a(1)
    phase_p(0)
    phase_c(0)
    phase_b(1)
    phase_p(1)
    phase_d(0)
    phase_c(1)
    phase_d(1)

    dqb = dqn[...]
    liftq[...] += mm_nt(dqb, qup[...])
    lora_t = lora[...].astype(F32).T[0:RANK].astype(BF)
    up = mm(lora_t, dqb)
    for h in range(share):
        qupg[h] = (ADAPTER_SCALE * up[:, h * HD : (h + 1) * HD]).astype(qupg.dtype)
    dvb = dva[TOK : TOK + SPANK, :].astype(BF)
    lva[TOK : TOK + SPANK, :] += mm_nt(dvb, vup[...])
    vupg[0] = (ADAPTER_SCALE * mm(lt[...], dvb)[RANK : 2 * RANK]).astype(vupg.dtype)
    take(lambda rows: (dka[rows, :] * scale).astype(BF), dkm, dko)

    @pl.when(g == groups - 1)
    def _():
        take(lambda rows: lva[rows, :], lvm, lvo)


def prepare_kernel(normed, qdown, vdown, keys, values, vup, cos, sin, *outs):
    lora_q = mm(normed[...], qdown[...]).astype(BF)
    lora_v = mm(normed[...], vdown[...]).astype(BF)
    head = 0
    for place, count in enumerate(COUNTS):
        out = outs[place]
        for c in range(count):
            col = slice((head + c) * HD, (head + c + 1) * HD)
            k = keys[:, col].astype(F32)
            k = k * cos[...] + pltpu.roll(k, HD // 2, 1) * sin[...]
            out[:, c * HD : (c + 1) * HD] = k.astype(BF)
            v = values[:, col].astype(F32) + ADAPTER_SCALE * mm(lora_v, vup[:, col])
            out[:, (count + c) * HD : (count + c + 1) * HD] = v.astype(BF)
        if place == 0:
            out[:, 2 * count * HD : 2 * count * HD + RANK] = lora_q
            out[:, 2 * count * HD + RANK : 2 * count * HD + 2 * RANK] = lora_v
        head += count


def prepare(*operands):
    vmem = pl.BlockSpec(memory_space=pltpu.VMEM)
    widths = [2 * count * HD + (HD if place == 0 else 0) for place, count in enumerate(COUNTS)]
    return pl.pallas_call(
        prepare_kernel,
        out_shape=[jax.ShapeDtypeStruct((TOK, width), BF) for width in widths],
        in_specs=[vmem] * len(operands),
        out_specs=[vmem] * len(widths),
        compiler_params=pltpu.CompilerParams(vmem_limit_bytes=40 * 2**20),
        name="prepare",
    )(*operands)


def attention(scalars, frozen, grad, own, qup, vup, cos, sin, dst, keyed, lorad, attended, first, count):
    share = SHARE
    wide = share * HD
    tail = 2 * COUNTS[0]

    def whole(shape):
        return pl.BlockSpec(shape, lambda g, s: (0,) * len(shape))

    def column(rows, width, offset):
        return pl.BlockSpec((rows, width), lambda g, s: (0, g + offset))

    lora_spec = pl.BlockSpec((TOK, HD), lambda g, s: (0, tail))
    in_specs = [
        column(TOK, wide, first), column(TOK, wide, first), lora_spec,
        column(RANK, wide, first), column(RANK, HD, first),
        whole((TOK, HD)), whole((TOK, HD)), whole((1, TOK)),
    ]
    in_specs += [column(TOK, HD, 0)] * 6 + [column(TOK, HD, count)] * 6 + [lora_spec] * 6
    operands = [scalars, frozen, grad, own, qup, vup, cos, sin, dst, *keyed, *keyed, *lorad]
    aliases = {}
    if attended is not None:
        aliases = {len(operands): 0}
        operands.append(attended)
        in_specs.append(pl.BlockSpec(memory_space=pl.ANY))
    pair = jax.ShapeDtypeStruct((3, TOK, count * HD), BF)
    lift = jax.ShapeDtypeStruct((3, TOK, RANK), F32)
    out_shape = [
        jax.ShapeDtypeStruct(frozen.shape, BF), pair, pair,
        jax.ShapeDtypeStruct((TOK, RANK), F32),
        jax.ShapeDtypeStruct((count * share, RANK, HD), BF),
        jax.ShapeDtypeStruct((count, RANK, HD), BF), lift, lift,
    ]
    pair_spec = pl.BlockSpec((3, TOK, HD), lambda g, s: (0, 0, g))
    out_specs = [
        column(TOK, wide, first), pair_spec, pair_spec, whole((TOK, RANK)),
        pl.BlockSpec((share, RANK, HD), lambda g, s: (g, 0, 0)),
        pl.BlockSpec((1, RANK, HD), lambda g, s: (g, 0, 0)),
        whole((3, TOK, RANK)), whole((3, TOK, RANK)),
    ]
    wide_rows = share * SUB
    scratch = [
        pltpu.VMEM((ROWS, HD), BF), pltpu.VMEM((ROWS, HD), BF),
        pltpu.VMEM((HD, SPANK), BF), pltpu.VMEM((HD, SPANK), BF), pltpu.VMEM((HD, SPANK), BF),
        pltpu.VMEM((2, REACH, SUB), F32),
        pltpu.VMEM((2, REACH, wide_rows), F32), pltpu.VMEM((2, REACH, wide_rows), F32),
        pltpu.VMEM((ROWS, HD), F32), pltpu.VMEM((ROWS, HD), F32),
        pltpu.VMEM((2, wide_rows, HD), BF), pltpu.VMEM((2, wide_rows, HD), BF),
        pltpu.VMEM((2, HD, wide_rows), F32), pltpu.VMEM((TOK, wide), BF),
        pltpu.VMEM((ROWS, RANK), F32),
    ]
    return pl.pallas_call(
        functools.partial(attention_kernel, share, attended is None),
        out_shape=out_shape,
        grid_spec=pltpu.PrefetchScalarGridSpec(
            num_scalar_prefetch=1, grid=(count,), in_specs=in_specs, out_specs=out_specs, scratch_shapes=scratch
        ),
        input_output_aliases=aliases,
        compiler_params=pltpu.CompilerParams(
            dimension_semantics=("arbitrary",), vmem_limit_bytes=40 * 2**20
        ),
        cost_estimate=pl.CostEstimate(
            flops=12 * 2 * REACH * SUB * share * HD * count, transcendentals=2 * REACH * SUB * share * count,
            bytes_accessed=6 * 2**20 * count // HEADS,
        ),
        name="attention",
    )(*operands)


def moved(block, step):
    devices = range(lax.axis_size("ctx"))
    route = [(i, step(i)) for i in devices if step(i) in devices]
    return lax.ppermute(block, "ctx", route)


def twin(block):
    return moved(block, lambda i: i ^ 1)


def ahead(block, chips):
    return moved(block, lambda i: i + 2 * chips)


def on_device(
    normed_input,
    frozen_query_output,
    key_base,
    frozen_value_output,
    out_grad,
    query_down_factor,
    query_up_factor,
    value_down_factor,
    value_up_factor,
    doc_lengths,
    stretch_map,
):
    devices = lax.axis_size("ctx")
    mine = lax.axis_index("ctx")
    chip, core = mine // 2, mine % 2
    stretch = stretch_map[mine]
    steps = jnp.arange(TOK, dtype=jnp.int32)
    places = stretch * TOK + steps
    documents = jnp.arange(doc_lengths.shape[0], dtype=jnp.int32)
    ends = jnp.sum(jnp.where(documents[:, None] >= documents[None, :], doc_lengths[None, :], 0), axis=1)
    starts = jnp.max(jnp.where(ends[None, :] <= places[:, None], ends[None, :], 0), axis=1)
    local = places - starts
    reach = 4 * TOK + steps - local
    half = HD // 2
    inverse = THETA ** (-jnp.arange(half, dtype=F32) * 2.0 / HD)
    angles = local.astype(F32)[:, None] * inverse[None, :]
    cosine, sine = jnp.cos(angles), jnp.sin(angles)
    cos = jnp.concatenate([cosine, cosine], axis=1)
    sin = jnp.concatenate([-sine, sine], axis=1)
    chips = chip - jnp.arange(3, dtype=jnp.int32)
    flips = (core + stretch_map[2 * jnp.maximum(chips, 0)]) % 2
    scalars = jnp.concatenate([(TOK * (1 - stretch % 2))[None], flips]).astype(jnp.int32)

    payloads = prepare(
        normed_input, query_down_factor, value_down_factor, key_base, frozen_value_output, value_up_factor, cos, sin
    )
    windows = []
    for payload in payloads:
        near, far = ahead(payload, 1), ahead(payload, 2)
        windows.append([payload, twin(payload), near, twin(near), far, twin(far)])
    attended = None
    first = 0
    key_parts, lift_q, lift_mine, lift_other, query_ups, value_ups = [], 0.0, 0.0, 0.0, [], []
    for place, count in enumerate(COUNTS):
        attended, key_mine, key_other, lq, qu, vu, lm, lo = attention(
            scalars, frozen_query_output, out_grad, payloads[0], query_up_factor, value_up_factor,
            cos, sin, reach[None, :], windows[place], windows[0], attended, first, count,
        )
        first += count
        lift_q, lift_mine, lift_other = lift_q + lq, lift_mine + lm, lift_other + lo
        query_ups.append(qu)
        value_ups.append(vu)
        if place == len(COUNTS) - 1:
            key_mine = jnp.concatenate([key_mine, lift_mine.astype(BF)], axis=2)
            key_other = jnp.concatenate([key_other, lift_other.astype(BF)], axis=2)
        both = key_mine.astype(F32) + twin(key_other).astype(F32)
        near = ahead(both[1].astype(BF), -1)
        far = ahead(both[2].astype(BF), -2)
        key_parts.append(both[0] + near.astype(F32) + far.astype(F32))
    total = jnp.concatenate(key_parts, axis=1)
    key_total = total[:, : HEADS * HD].reshape(TOK, HEADS, HD)
    swapped = jnp.concatenate([key_total[..., half:], key_total[..., :half]], axis=-1)
    key_grad = (key_total * cos[:, None, :] - swapped * sin[:, None, :]).astype(BF).reshape(TOK, HEADS * HD)
    lift_q = (ADAPTER_SCALE * lift_q).astype(BF)
    lift_v = (ADAPTER_SCALE * total[:, HEADS * HD :]).astype(BF)
    lifts = jnp.concatenate([lift_q, lift_v], axis=1)
    width = normed_input.shape[1]
    tiles = width // HD
    downs = jnp.einsum("tr,td->rd", lifts, normed_input, preferred_element_type=F32).astype(BF)
    downs = jnp.transpose(downs.reshape(2 * RANK, tiles, HD), (1, 0, 2)).reshape(-1, HD)
    terms = jnp.concatenate([downs] + [x.reshape(-1, HD) for x in query_ups + value_ups], axis=0)
    rows = terms.shape[0] // devices
    spread = lax.all_to_all(terms.reshape(devices, rows, HD), "ctx", 0, 0)
    summed = jnp.sum(spread.astype(F32), axis=0).astype(BF)
    whole = lax.all_to_all(jnp.broadcast_to(summed[None], (devices, rows, HD)), "ctx", 0, 0).reshape(-1, HD)
    whole = whole.astype(F32) / (TOK * devices)
    downs = jnp.transpose(whole[: tiles * 2 * RANK].reshape(tiles, 2 * RANK, HD), (0, 2, 1)).reshape(width, 2 * RANK)
    ups = jnp.transpose(whole[tiles * 2 * RANK :].reshape(-1, RANK, HD), (1, 0, 2)).reshape(RANK, -1)
    query_width = HEADS * SHARE * HD
    return (attended, key_grad, downs[:, :RANK], ups[:, :query_width], downs[:, RANK:], ups[:, query_width:])


def solution(mesh):
    row = P("ctx", None)
    return jax.shard_map(
        on_device,
        mesh=mesh,
        in_specs=(row, row, row, row, row, P(), P(), P(), P(), P(), P()),
        out_specs=(row, row, P(), P(), P(), P()),
        check_vma=False,
    )
```

time: 778 us -> 278 us (0.36)
  matrix products: 219 us -> 0.62 us
  waiting for transfers between devices: 271 us -> 58 us
  other arithmetic: 101 us -> 13.1 us
  Pallas kernels: 0 us -> 68.4 us
  local copies, waits for them, and re-layouts: 108 us -> 48.6 us
  starting transfers between devices: 45.7 us -> 79.8 us
  between operations: 20 us -> 4.22 us
    dot_general x48 -> x1, matrix products: 156 us -> 0.62 us  [on_device(): jnp.einsum('tr,td->rd', lifts, normed_input, preferred_element_type=F32)]
    psum x1 -> x0, waiting for transfers between devices: 155 us -> none  [on_device(): lax.psum((term_down_q, query_up_term, term_down_v, value_up_term), 'ctx')]
    ppermute x12 -> x24, waiting for transfers between devices: 116 us -> 34.3 us  [moved(): return lax.ppermute(block, 'ctx', route)]
    pallas_call x0 -> x4, Pallas kernels: none -> 68.4 us  [the longest x3 65.7 us: attention(): pl.pallas_call(functools.partial(attention_kernel, share, attended is Non...]
    sub x8 -> x0, matrix products: 62.7 us -> none  [group_attention(): weights = jnp.exp(scores - peak_score)]
    convert_element_type x9 -> x6, other arithmetic: 36.3 us -> 3.22 us  [the longest x1 1.97 us: on_device(): key_mine = jnp.concatenate([key_mine, lift_mine.astype(BF)], axis=2)]
    all_to_all x0 -> x2, waiting for transfers between devices: none -> 23.7 us  [the longest x1 23.7 us: on_device(): spread = lax.all_to_all(terms.reshape(devices, rows, HD), 'ctx', 0, 0)]
    all_to_all x0 -> x2, starting transfers between devices: none -> 20 us  [the longest x1 10.1 us: on_device(): lax.all_to_all(jnp.broadcast_to(summed[None], (devices, rows, HD)), 'ctx'...]
  transfers between devices with their start and end apart: 13 -> 26, of which waited for: 9 -> 10; matrix products, arithmetic and copies ran while one was open for 9% -> 4% of each run, Pallas kernels for 0% -> 15%
where the time goes in v1:
time: 278 us; the launch traced here: 273 us
  starting transfers between devices  79.8 us (29%)
  Pallas kernels  68.4 us (25%)
  waiting for transfers between devices  58 us (21%)
  local copies, waits for them, and re-layouts  48.6 us (17%)
  other arithmetic  13.1 us (5%)
  between operations  4.22 us (2%)
    pallas_call x3, Pallas kernels, attention(): pl.pallas_call(functools.partial(attention_kernel, share, attended is Non...  65.7 us
    ppermute x24, starting transfers between devices, moved(): return lax.ppermute(block, 'ctx', route)  59.9 us
    ppermute x24, waiting for transfers between devices, moved(): return lax.ppermute(block, 'ctx', route)  34.3 us
    unnamed x105, local copies, waits for them, and re-layouts  31.2 us
    all_to_all x1, waiting for transfers between devices, on_device(): spread = lax.all_to_all(terms.reshape(devices, rows, HD), 'ctx', 0, 0)  23.7 us
    all_to_all x1, starting transfers between devices, on_device(): lax.all_to_all(jnp.broadcast_to(summed[None], (devices, rows, HD)), 'ctx'...  10.1 us
    all_to_all x1, starting transfers between devices, on_device(): spread = lax.all_to_all(terms.reshape(devices, rows, HD), 'ctx', 0, 0)  9.88 us
  transfers between devices with their start and end apart: 26, of which 10 were waited for; matrix products, arithmetic and copies ran while one was open for 4% of the time, Pallas kernels for 15%

profile of v1, /device:TPU:62, one launch (start us, length us, event | category | flops | bytes accessed | tf_op | source)
XLA Modules:
  0.0 272.7 jit_solution(1818071015001485360)
XLA Ops:
  0.7 2.5 copy.40.qdown
  3.2 2.3 copy.41.vdown
  7.7 1.3 copy-done.1
  9.0 1.3 copy-done.2
  10.3 1.0 copy-done.5
  11.4 2.6 prepare.1
  14.7 3.4 %collective-permute-start.6 = (bf16[256,640]{1,0:T(8,128)(2,1)}, bf16[256,640]{1,0:T(8,128)(2,1)}, u32[]{:S(2)}, u32[]{:S(2)}) collective-permute-start(bf16[256,640]{1,0:T(8,128)(2,1)} %get-tuple-element.33.lora.rest_0_.rest_6_.rest_12_), channel_id=1, source_target_pairs={{0,2},{1,3},{2,4},{3,5},{4,6},{5,7},{6,8},{7,9},{8,10},{9,11},{10,... | collective-permute-start | bytes 983048 | tf_op jit(solution)/shard_map/ppermute | solution.py:309
  18.1 4.3 %collective-permute-start.8 = (bf16[256,640]{1,0:T(8,128)(2,1)}, bf16[256,640]{1,0:T(8,128)(2,1)}, u32[]{:S(2)}, u32[]{:S(2)}) collective-permute-start(bf16[256,640]{1,0:T(8,128)(2,1)} %get-tuple-element.33.lora.rest_0_.rest_6_.rest_12_), channel_id=1, source_target_pairs={{0,4},{1,5},{2,6},{3,7},{4,8},{5,9},{6,10},{7,11},{8,12},{9,13},{1... | collective-permute-start | bytes 983048 | tf_op jit(solution)/shard_map/ppermute | solution.py:309
  22.5 3.7 %collective-permute-start.11 = (bf16[256,768]{1,0:T(8,128)(2,1)}, bf16[256,768]{1,0:T(8,128)(2,1)S(1)}, u32[]{:S(2)}, u32[]{:S(2)}) collective-permute-start(bf16[256,768]{1,0:T(8,128)(2,1)} %get-tuple-element.35.rest_0_.rest_6_), channel_id=1, source_target_pairs={{0,2},{1,3},{2,4},{3,5},{4,6},{5,7},{6,8},{7,9},{8,10},{9,11},{10,... | collective-permute-start | bytes 1179656 | tf_op jit(solution)/shard_map/ppermute | solution.py:309
  26.2 3.1 %collective-permute-start.13 = (bf16[256,768]{1,0:T(8,128)(2,1)}, bf16[256,768]{1,0:T(8,128)(2,1)}, u32[]{:S(2)}, u32[]{:S(2)}) collective-permute-start(bf16[256,768]{1,0:T(8,128)(2,1)} %get-tuple-element.35.rest_0_.rest_6_), channel_id=1, source_target_pairs={{0,4},{1,5},{2,6},{3,7},{4,8},{5,9},{6,10},{7,11},{8,12},{9,13},{1... | collective-permute-start | bytes 1179656 | tf_op jit(solution)/shard_map/ppermute | solution.py:309
  32.7 9.7 %collective-permute-start.1 = (bf16[256,768]{1,0:T(8,128)(2,1)}, bf16[256,768]{1,0:T(8,128)(2,1)S(1)}, u32[]{:S(2)}, u32[]{:S(2)}) collective-permute-start(bf16[256,768]{1,0:T(8,128)(2,1)} %copy-done.35), channel_id=1, source_target_pairs={{0,2},{1,3},{2,4},{3,5},{4,6},{5,7},{6,8},{7,9},{8,10},{9,11},{10,... | collective-permute-start | bytes 1179656 | tf_op jit(solution)/shard_map/ppermute | solution.py:309
  42.8 4.3 %collective-permute-start.3 = (bf16[256,768]{1,0:T(8,128)(2,1)}, bf16[256,768]{1,0:T(8,128)(2,1)S(1)}, u32[]{:S(2)}, u32[]{:S(2)}) collective-permute-start(bf16[256,768]{1,0:T(8,128)(2,1)} %copy-done.35), channel_id=1, source_target_pairs={{0,4},{1,5},{2,6},{3,7},{4,8},{5,9},{6,10},{7,11},{8,12},{9,13},{1... | collective-permute-start | bytes 1179656 | tf_op jit(solution)/shard_map/ppermute | solution.py:309
  48.4 1.7 copy-done.29
  50.1 1.7 copy-done.31
  51.9 1.1 copy-done.32
  53.0 17.2 %attention.3 = (bf16[256,5120]{1,0:T(8,128)(2,1)}, bf16[3,256,256]{2,1,0:T(8,128)(2,1)S(1)}, bf16[3,256,256]{2,1,0:T(8,128)(2,1)S(1)}, f32[256,64]{1,0:T(8,128)S...) custom-call(s32[4]{0:T(128)S(1)} %pad_add_fusion.sc, ...), custom_call_target="tpu_custom_call" | custom-call | flops 4529848320 | bytes 1572864 | tf_op jit(solution)/shard_map/attention/pallas_call | solution.py:288
  74.8 1.0 copy-done.38
  75.8 24.1 %attention.4 = (bf16[256,5120]{1,0:T(8,128)(2,1)}, bf16[3,256,384]{2,1,0:T(8,128)(2,1)S(1)}, bf16[3,256,384]{2,1,0:T(8,128)(2,1)S(1)}, f32[256,64]{1,0:T(8,128)S...) custom-call(s32[4]{0:T(128)S(1)} %pad_add_fusion.sc, ...), custom_call_target="tpu_custom_call", output_to_operand_aliasing={{0}: (27, {})} | custom-call | flops 6794772480 | bytes 2359296 | tf_op jit(solution)/shard_map/attention/pallas_call | solution.py:288
  102.9 24.4 %attention.5 = (bf16[256,5120]{1,0:T(8,128)(2,1)}, bf16[3,256,384]{2,1,0:T(8,128)(2,1)S(1)}, bf16[3,256,384]{2,1,0:T(8,128)(2,1)S(1)}, f32[256,64]{1,0:T(8,128)S...) custom-call(s32[4]{0:T(128)S(1)} %pad_add_fusion.sc, ...), custom_call_target="tpu_custom_call", output_to_operand_aliasing={{0}: (27, {})} | custom-call | flops 6794772480 | bytes 2359296 | tf_op jit(solution)/shard_map/attention/pallas_call | solution.py:288
  129.9 2.3 copy.42
  132.3 2.0 add_convert_fusion.1
  134.7 2.3 copy.43
  136.9 1.7 fusion.19
  138.7 3.0 %collective-permute-start.23 = (bf16[256,448]{1,0:T(8,128)(2,1)S(1)}, bf16[256,448]{1,0:T(8,128)(2,1)S(1)}, u32[]{:S(2)}, u32[]{:S(2)}) collective-permute-start(bf16[256,448]{1,0:T(8,128)(2,1)S(1)} %get-tuple-element.89), channel_id=1, source_target_pairs={{4,0},{5,1},{6,2},{7,3},{8,4},{9,5},{10,6},{11,7},{12,8},{13,9},{1... | collective-permute-start | bytes 688136 | tf_op jit(solution)/shard_map/ppermute | solution.py:309
  141.7 11.1 %collective-permute-start.22 = (bf16[256,448]{1,0:T(8,128)(2,1)S(1)}, bf16[256,448]{1,0:T(8,128)(2,1)S(1)}, u32[]{:S(2)}, u32[]{:S(2)}) collective-permute-start(bf16[256,448]{1,0:T(8,128)(2,1)S(1)} %get-tuple-element.88), channel_id=1, source_target_pairs={{2,0},{3,1},{4,2},{5,3},{6,4},{7,5},{8,6},{9,7},{10,8},{11,9},{12,... | collective-permute-start | bytes 688136 | tf_op jit(solution)/shard_map/ppermute | solution.py:309
  153.5 7.8 %collective-permute-done.22 = bf16[256,448]{1,0:T(8,128)(2,1)S(1)} collective-permute-done((bf16[256,448]{1,0:T(8,128)(2,1)S(1)}, bf16[256,448]{1,0:T(8,128)(2,1)S(1)}, u32[]{:S(2)}, u32[]{:S(2)}) %collective-permute-start.22) | collective-permute-done | bytes 229408 | tf_op jit(solution)/shard_map/ppermute | solution.py:309
  164.5 1.4 copy-done.43
  165.8 9.9 %all-to-all-start = ((bf16[128,64,128]{2,1,0:T(8,128)(2,1)}), bf16[128,64,128]{2,1,0:T(8,128)(2,1)}, u32[]{:S(2)}, u32[]{:S(2)}) async-start(bf16[128,64,128]{2,1,0:T(8,128)(2,1)} %bitcast.83), calls=%async_computation | async-start | bytes 4194304 | tf_op jit(solution)/shard_map/all_to_all | solution.py:393
  177.6 23.7 %all-to-all-done = bf16[128,64,128]{2,1,0:T(8,128)(2,1)} async-done(((bf16[128,64,128]{2,1,0:T(8,128)(2,1)}), bf16[128,64,128]{2,1,0:T(8,128)(2,1)}, u32[]{:S(2)}, u32[]{:S(2)}) %all-to-all-start) | async-done | bytes 2097184 | tf_op jit(solution)/shard_map/all_to_all | solution.py:393
  201.3 2.0 reduce_sum.22
  203.3 1.9 broadcast_in_dim.30
  205.2 10.1 %all-to-all-start.1 = ((bf16[128,64,128]{2,1,0:T(8,128)(2,1)}), bf16[128,64,128]{2,1,0:T(8,128)(2,1)}, u32[]{:S(2)}, u32[]{:S(2)}) async-start(bf16[128,64,128]{2,1,0:T(8,128)(2,1)} %broadcast_in_dim.30), calls=%async_computation.1 | async-start | bytes 4194304 | tf_op jit(solution)/shard_map/all_to_all | solution.py:395
  215.3 3.3 %collective-permute-start.17 = (bf16[256,256]{1,0:T(8,128)(2,1)S(1)}, bf16[256,256]{1,0:T(8,128)(2,1)S(1)}, u32[]{:S(2)}, u32[]{:S(2)}) collective-permute-start(bf16[256,256]{1,0:T(8,128)(2,1)S(1)} %get-tuple-element.93), channel_id=1, source_target_pairs={{4,0},{5,1},{6,2},{7,3},{8,4},{9,5},{10,6},{11,7},{12,8},{13,9},{1... | collective-permute-start | bytes 393224 | tf_op jit(solution)/shard_map/ppermute | solution.py:309
  218.6 1.9 collective-permute-start.16
  220.6 1.2 fusion.18
  221.9 5.8 %collective-permute-start.20 = (bf16[256,384]{1,0:T(8,128)(2,1)S(1)}, bf16[256,384]{1,0:T(8,128)(2,1)S(1)}, u32[]{:S(2)}, u32[]{:S(2)}) collective-permute-start(bf16[256,384]{1,0:T(8,128)(2,1)S(1)} %get-tuple-element.91), channel_id=1, source_target_pairs={{4,0},{5,1},{6,2},{7,3},{8,4},{9,5},{10,6},{11,7},{12,8},{13,9},{1... | collective-permute-start | bytes 589832 | tf_op jit(solution)/shard_map/ppermute | solution.py:309
  227.7 2.5 collective-permute-start.19
  230.1 13.7 %collective-permute-done.17 = bf16[256,256]{1,0:T(8,128)(2,1)S(1)} collective-permute-done((bf16[256,256]{1,0:T(8,128)(2,1)S(1)}, bf16[256,256]{1,0:T(8,128)(2,1)S(1)}, u32[]{:S(2)}, u32[]{:S(2)}) %collective-permute-start.17) | collective-permute-done | bytes 131104 | tf_op jit(solution)/shard_map/ppermute | solution.py:309
  243.9 6.1 %collective-permute-done.16 = bf16[256,256]{1,0:T(8,128)(2,1)S(1)} collective-permute-done((bf16[256,256]{1,0:T(8,128)(2,1)S(1)}, bf16[256,256]{1,0:T(8,128)(2,1)S(1)}, u32[]{:S(2)}, u32[]{:S(2)}) %collective-permute-start.16) | collective-permute-done | bytes 131104 | tf_op jit(solution)/shard_map/ppermute | solution.py:309
  250.7 3.4 %collective-permute-done.19 = bf16[256,384]{1,0:T(8,128)(2,1)S(1)} collective-permute-done((bf16[256,384]{1,0:T(8,128)(2,1)S(1)}, bf16[256,384]{1,0:T(8,128)(2,1)S(1)}, u32[]{:S(2)}, u32[]{:S(2)}) %collective-permute-start.19) | collective-permute-done | bytes 196640 | tf_op jit(solution)/shard_map/ppermute | solution.py:309
  255.3 1.1 fusion.1
  256.4 2.2 convert_multiply_fusion
  258.6 1.6 slice.98
  260.4 1.1 slice.101
  262.2 2.1 copy.45
  264.4 3.2 %fusion.20 = (f32[5120,64]{1,0:T(8,128)}, f32[5120,64]{1,0:T(8,128)}) fusion(f32[5120,128]{1,0:T(8,128)S(1)} %bitcast.80), kind=kLoop, calls=%fused_computation.72 | loop fusion | bytes 5242880 | tf_op jit(solution)/shard_map/slice | solution.py:400
  267.6 3.1 %copy.47 = f32[5120,64]{0,1:T(8,128)} copy(f32[5120,64]{1,0:T(8,128)} %get-tuple-element.79) | data formatting | bytes 2621440
  270.6 1.8 copy.48
  (160 shorter events, 24.5 us)
Async XLA Ops:
  0.6 4.9 %copy-start.41 = (s32[128]{0:T(128)S(1)}, s32[128]{0:T(128)}, u32[]{:S(2)}) copy-start(s32[128]{0:T(128)} %param.21) | copy-start | bytes 1540
  0.6 6.1 %copy-start.46 = (s32[64]{0:T(128)S(1)}, s32[64]{0:T(128)}, u32[]{:S(2)}) copy-start(s32[64]{0:T(128)} %param.20) | copy-start | bytes 772
  0.7 7.0 %copy-start = (bf16[256,5120]{1,0:T(8,128)(2,1)S(1)}, bf16[256,5120]{1,0:T(8,128)(2,1)}, u32[]{:S(2)}) copy-start(bf16[256,5120]{1,0:T(8,128)(2,1)} %normed.1) | copy-start | bytes 7864324
  0.7 7.0 %copy-start.4 = (bf16[256,1024]{1,0:T(8,128)(2,1)S(1)}, bf16[256,1024]{1,0:T(8,128)(2,1)}, u32[]{:S(2)}) copy-start(bf16[256,1024]{1,0:T(8,128)(2,1)} %keys.1) | copy-start | bytes 1572868
  0.7 7.0 %copy-start.17 = (bf16[64,1024]{1,0:T(8,128)(2,1)S(1)}, bf16[64,1024]{1,0:T(8,128)(2,1)}, u32[]{:S(2)}) copy-start(bf16[64,1024]{1,0:T(8,128)(2,1)} %vup.7) | copy-start | bytes 393220
  7.7 1.3 copy-start.1
  14.7 17.9 %collective-permute-start.5 = (bf16[256,640]{1,0:T(8,128)(2,1)}, bf16[256,640]{1,0:T(8,128)(2,1)}, u32[]{:S(2)}, u32[]{:S(2)}) collective-permute-start(bf16[256,640]{1,0:T(8,128)(2,1)} %get-tuple-element.33.lora.rest_0_.rest_6_.rest_12_), channel_id=1, source_target_pairs={{0,1},{1,0},{2,3},{3,2},{4,5},{5,4},{6,7},{7,6},{8,9},{9,8},{10,11... | collective-permute-start | bytes 983048 | tf_op jit(solution)/shard_map/ppermute | solution.py:309
  14.7 17.2 %collective-permute-start.6 = (bf16[256,640]{1,0:T(8,128)(2,1)}, bf16[256,640]{1,0:T(8,128)(2,1)}, u32[]{:S(2)}, u32[]{:S(2)}) collective-permute-start(bf16[256,640]{1,0:T(8,128)(2,1)} %get-tuple-element.33.lora.rest_0_.rest_6_.rest_12_), channel_id=1, source_target_pairs={{0,2},{1,3},{2,4},{3,5},{4,6},{5,7},{6,8},{7,9},{8,10},{9,11},{10,... | collective-permute-start | bytes 983048 | tf_op jit(solution)/shard_map/ppermute | solution.py:309
  18.1 13.9 %collective-permute-start.8 = (bf16[256,640]{1,0:T(8,128)(2,1)}, bf16[256,640]{1,0:T(8,128)(2,1)}, u32[]{:S(2)}, u32[]{:S(2)}) collective-permute-start(bf16[256,640]{1,0:T(8,128)(2,1)} %get-tuple-element.33.lora.rest_0_.rest_6_.rest_12_), channel_id=1, source_target_pairs={{0,4},{1,5},{2,6},{3,7},{4,8},{5,9},{6,10},{7,11},{8,12},{9,13},{1... | collective-permute-start | bytes 983048 | tf_op jit(solution)/shard_map/ppermute | solution.py:309
  22.5 20.4 %collective-permute-start.11 = (bf16[256,768]{1,0:T(8,128)(2,1)}, bf16[256,768]{1,0:T(8,128)(2,1)S(1)}, u32[]{:S(2)}, u32[]{:S(2)}) collective-permute-start(bf16[256,768]{1,0:T(8,128)(2,1)} %get-tuple-element.35.rest_0_.rest_6_), channel_id=1, source_target_pairs={{0,2},{1,3},{2,4},{3,5},{4,6},{5,7},{6,8},{7,9},{8,10},{9,11},{10,... | collective-permute-start | bytes 1179656 | tf_op jit(solution)/shard_map/ppermute | solution.py:309
  26.2 21.0 %collective-permute-start.13 = (bf16[256,768]{1,0:T(8,128)(2,1)}, bf16[256,768]{1,0:T(8,128)(2,1)}, u32[]{:S(2)}, u32[]{:S(2)}) collective-permute-start(bf16[256,768]{1,0:T(8,128)(2,1)} %get-tuple-element.35.rest_0_.rest_6_), channel_id=1, source_target_pairs={{0,4},{1,5},{2,6},{3,7},{4,8},{5,9},{6,10},{7,11},{8,12},{9,13},{1... | collective-permute-start | bytes 1179656 | tf_op jit(solution)/shard_map/ppermute | solution.py:309
  32.0 15.3 %collective-permute-start.7 = (bf16[256,640]{1,0:T(8,128)(2,1)}, bf16[256,640]{1,0:T(8,128)(2,1)S(1)}, u32[]{:S(2)}, u32[]{:S(2)}) collective-permute-start(bf16[256,640]{1,0:T(8,128)(2,1)} %collective-permute-done.6.rest_2_.rest_8_.rest_14_), channel_id=1, source_target_pairs={{0,1},{1,0},{2,3},{3,2},{4,5},{5,4},{6,7},{7,6},{8,9},{9,8},{10,11... | collective-permute-start | bytes 983048 | tf_op jit(solution)/shard_map/ppermute | solution.py:309
  32.1 15.7 %collective-permute-start.9 = (bf16[256,640]{1,0:T(8,128)(2,1)}, bf16[256,640]{1,0:T(8,128)(2,1)S(1)}, u32[]{:S(2)}, u32[]{:S(2)}) collective-permute-start(bf16[256,640]{1,0:T(8,128)(2,1)} %collective-permute-done.8.rest_4_.rest_10_.rest_16_), channel_id=1, source_target_pairs={{0,1},{1,0},{2,3},{3,2},{4,5},{5,4},{6,7},{7,6},{8,9},{9,8},{10,11... | collective-permute-start | bytes 983048 | tf_op jit(solution)/shard_map/ppermute | solution.py:309
  32.7 42.1 %copy-start.18 = (bf16[64,1024]{1,0:T(8,128)(2,1)S(1)}, bf16[64,1024]{1,0:T(8,128)(2,1)}, u32[]{:S(2)}) copy-start(bf16[64,1024]{1,0:T(8,128)(2,1)} %vup.7) | copy-start | bytes 393220
  32.7 40.9 %collective-permute-start.1 = (bf16[256,768]{1,0:T(8,128)(2,1)}, bf16[256,768]{1,0:T(8,128)(2,1)S(1)}, u32[]{:S(2)}, u32[]{:S(2)}) collective-permute-start(bf16[256,768]{1,0:T(8,128)(2,1)} %copy-done.35), channel_id=1, source_target_pairs={{0,2},{1,3},{2,4},{3,5},{4,6},{5,7},{6,8},{7,9},{8,10},{9,11},{10,... | collective-permute-start | bytes 1179656 | tf_op jit(solution)/shard_map/ppermute | solution.py:309
  42.8 27.3 %copy-start.37 = (bf16[256,768]{1,0:T(8,128)(2,1)}, bf16[256,768]{1,0:T(8,128)(2,1)S(1)}, u32[]{:S(2)}) copy-start(bf16[256,768]{1,0:T(8,128)(2,1)S(1)} %collective-permute-done.11.rest_2_.rest_8_) | copy-start | bytes 1179652
  42.8 31.2 %collective-permute-start.3 = (bf16[256,768]{1,0:T(8,128)(2,1)}, bf16[256,768]{1,0:T(8,128)(2,1)S(1)}, u32[]{:S(2)}, u32[]{:S(2)}) collective-permute-start(bf16[256,768]{1,0:T(8,128)(2,1)} %copy-done.35), channel_id=1, source_target_pairs={{0,4},{1,5},{2,6},{3,7},{4,8},{5,9},{6,10},{7,11},{8,12},{9,13},{1... | collective-permute-start | bytes 1179656 | tf_op jit(solution)/shard_map/ppermute | solution.py:309
  47.2 27.0 %collective-permute-start.10 = (bf16[256,768]{1,0:T(8,128)(2,1)}, bf16[256,768]{1,0:T(8,128)(2,1)S(1)}, u32[]{:S(2)}, u32[]{:S(2)}) collective-permute-start(bf16[256,768]{1,0:T(8,128)(2,1)} %get-tuple-element.35.rest_0_.rest_6_), channel_id=1, source_target_pairs={{0,1},{1,0},{2,3},{3,2},{4,5},{5,4},{6,7},{7,6},{8,9},{9,8},{10,11... | collective-permute-start | bytes 1179656 | tf_op jit(solution)/shard_map/ppermute | solution.py:309
  47.3 27.5 %collective-permute-start.12 = (bf16[256,768]{1,0:T(8,128)(2,1)S(1)}, bf16[256,768]{1,0:T(8,128)(2,1)S(1)}, u32[]{:S(2)}, u32[]{:S(2)}) collective-permute-start(bf16[256,768]{1,0:T(8,128)(2,1)S(1)} %collective-permute-done.11.rest_2_.rest_8_), channel_id=1, source_target_pairs={{0,1},{1,0},{2,3},{3,2},{4,5},{5,4},{6,7},{7,6},{8,9},{9,8},{10,11... | collective-permute-start | bytes 1179656 | tf_op jit(solution)/shard_map/ppermute | solution.py:309
  47.8 27.0 %collective-permute-start.14 = (bf16[256,768]{1,0:T(8,128)(2,1)}, bf16[256,768]{1,0:T(8,128)(2,1)S(1)}, u32[]{:S(2)}, u32[]{:S(2)}) collective-permute-start(bf16[256,768]{1,0:T(8,128)(2,1)} %collective-permute-done.13.rest_4_.rest_10_), channel_id=1, source_target_pairs={{0,1},{1,0},{2,3},{3,2},{4,5},{5,4},{6,7},{7,6},{8,9},{9,8},{10,11... | collective-permute-start | bytes 1179656 | tf_op jit(solution)/shard_map/ppermute | solution.py:309
  48.4 1.7 copy-start.29
  50.1 1.7 copy-start.31
  52.9 20.7 %copy-start.36 = (bf16[256,768]{1,0:T(8,128)(2,1)S(1)}, bf16[256,768]{1,0:T(8,128)(2,1)}, u32[]{:S(2)}) copy-start(bf16[256,768]{1,0:T(8,128)(2,1)} %copy-done.35) | copy-start | bytes 1179652
  52.9 21.8 %copy-start.30 = (bf16[256,5120]{1,0:T(8,128)(2,1)S(1)}, bf16[256,5120]{1,0:T(8,128)(2,1)}, u32[]{:S(2)}) copy-start(bf16[256,5120]{1,0:T(8,128)(2,1)} %fq.5) | copy-start | bytes 7864324
  73.6 26.3 %copy-start.39 = (bf16[3,256,256]{2,1,0:T(8,128)(2,1)}, bf16[3,256,256]{2,1,0:T(8,128)(2,1)S(1)}, u32[]{:S(2)}) copy-start(bf16[3,256,256]{2,1,0:T(8,128)(2,1)S(1)} %get-tuple-element.40) | copy-start | bytes 1179652
  73.6 29.2 %collective-permute-start = (bf16[256,768]{1,0:T(8,128)(2,1)S(1)}, bf16[256,768]{1,0:T(8,128)(2,1)S(1)}, u32[]{:S(2)}, u32[]{:S(2)}) collective-permute-start(bf16[256,768]{1,0:T(8,128)(2,1)S(1)} %copy-done.36), channel_id=1, source_target_pairs={{0,1},{1,0},{2,3},{3,2},{4,5},{5,4},{6,7},{7,6},{8,9},{9,8},{10,11... | collective-permute-start | bytes 1179656 | tf_op jit(solution)/shard_map/ppermute | solution.py:309
  74.1 28.8 %collective-permute-start.2 = (bf16[256,768]{1,0:T(8,128)(2,1)S(1)}, bf16[256,768]{1,0:T(8,128)(2,1)S(1)}, u32[]{:S(2)}, u32[]{:S(2)}) collective-permute-start(bf16[256,768]{1,0:T(8,128)(2,1)S(1)} %collective-permute-done.1.rest_2_.rest_8_), channel_id=1, source_target_pairs={{0,1},{1,0},{2,3},{3,2},{4,5},{5,4},{6,7},{7,6},{8,9},{9,8},{10,11... | collective-permute-start | bytes 1179656 | tf_op jit(solution)/shard_map/ppermute | solution.py:309
  74.2 28.7 %collective-permute-start.4 = (bf16[256,768]{1,0:T(8,128)(2,1)S(1)}, bf16[256,768]{1,0:T(8,128)(2,1)S(1)}, u32[]{:S(2)}, u32[]{:S(2)}) collective-permute-start(bf16[256,768]{1,0:T(8,128)(2,1)S(1)} %collective-permute-done.3.rest_4_.rest_10_), channel_id=1, source_target_pairs={{0,1},{1,0},{2,3},{3,2},{4,5},{5,4},{6,7},{7,6},{8,9},{9,8},{10,11... | collective-permute-start | bytes 1179656 | tf_op jit(solution)/shard_map/ppermute | solution.py:309
  132.2 2.5 collective-permute-start.21
  136.9 15.9 %copy-start.20 = (f32[256,64]{1,0:T(8,128)S(1)}, f32[256,64]{1,0:T(8,128)}, u32[]{:S(2)}) copy-start(f32[256,64]{1,0:T(8,128)} %copy-done.19) | copy-start | bytes 196612
  136.9 15.9 %copy-start.22 = (f32[256,64]{1,0:T(8,128)S(1)}, f32[256,64]{1,0:T(8,128)}, u32[]{:S(2)}) copy-start(f32[256,64]{1,0:T(8,128)} %copy-done.21) | copy-start | bytes 196612
  136.9 15.9 %copy-start.24 = (f32[256,64]{1,0:T(8,128)S(1)}, f32[256,64]{1,0:T(8,128)}, u32[]{:S(2)}) copy-start(f32[256,64]{1,0:T(8,128)} %copy-done.23) | copy-start | bytes 196612
  138.7 14.8 %collective-permute-start.23 = (bf16[256,448]{1,0:T(8,128)(2,1)S(1)}, bf16[256,448]{1,0:T(8,128)(2,1)S(1)}, u32[]{:S(2)}, u32[]{:S(2)}) collective-permute-start(bf16[256,448]{1,0:T(8,128)(2,1)S(1)} %get-tuple-element.89), channel_id=1, source_target_pairs={{4,0},{5,1},{6,2},{7,3},{8,4},{9,5},{10,6},{11,7},{12,8},{13,9},{1... | collective-permute-start | bytes 688136 | tf_op jit(solution)/shard_map/ppermute | solution.py:309
  141.7 19.6 %collective-permute-start.22 = (bf16[256,448]{1,0:T(8,128)(2,1)S(1)}, bf16[256,448]{1,0:T(8,128)(2,1)S(1)}, u32[]{:S(2)}, u32[]{:S(2)}) collective-permute-start(bf16[256,448]{1,0:T(8,128)(2,1)S(1)} %get-tuple-element.88), channel_id=1, source_target_pairs={{2,0},{3,1},{4,2},{5,3},{6,4},{7,5},{8,6},{9,7},{10,8},{11,9},{12,... | collective-permute-start | bytes 688136 | tf_op jit(solution)/shard_map/ppermute | solution.py:309
  164.4 1.4 copy-start.43
  165.8 9.9 %copy-start.40 = (bf16[3,256,256]{2,1,0:T(8,128)(2,1)S(1)}, bf16[3,256,256]{2,1,0:T(8,128)(2,1)}, u32[]{:S(2)}) copy-start(bf16[3,256,256]{2,1,0:T(8,128)(2,1)} %copy-done.39) | copy-start | bytes 1179652
  165.8 10.1 %copy-start.34 = (bf16[3,256,384]{2,1,0:T(8,128)(2,1)S(1)}, bf16[3,256,384]{2,1,0:T(8,128)(2,1)}, u32[]{:S(2)}) copy-start(bf16[3,256,384]{2,1,0:T(8,128)(2,1)} %copy-done.33) | copy-start | bytes 1769476
  165.8 11.7 %copy-start.10 = (bf16[3,256,256]{2,1,0:T(8,128)(2,1)S(1)}, bf16[3,256,256]{2,1,0:T(8,128)(2,1)}, u32[]{:S(2)}) copy-start(bf16[3,256,256]{2,1,0:T(8,128)(2,1)} %copy-done.9) | copy-start | bytes 1179652
  165.8 35.5 %all-to-all-start = ((bf16[128,64,128]{2,1,0:T(8,128)(2,1)}), bf16[128,64,128]{2,1,0:T(8,128)(2,1)}, u32[]{:S(2)}, u32[]{:S(2)}) async-start(bf16[128,64,128]{2,1,0:T(8,128)(2,1)} %bitcast.83), calls=%async_computation | async-start | bytes 4194304 | tf_op jit(solution)/shard_map/all_to_all | solution.py:393
  175.7 1.8 collective-permute-start.15
  175.9 44.6 %collective-permute-start.18 = (bf16[3,256,384]{2,1,0:T(8,128)(2,1)S(1)}, bf16[3,256,384]{2,1,0:T(8,128)(2,1)}, u32[]{:S(2)}, u32[]{:S(2)}) collective-permute-start(bf16[3,256,384]{2,1,0:T(8,128)(2,1)S(1)} %copy-done.34), channel_id=1, source_target_pairs={{0,1},{1,0},{2,3},{3,2},{4,5},{5,4},{6,7},{7,6},{8,9},{9,8},{10,11... | collective-permute-start | bytes 1769480 | tf_op jit(solution)/shard_map/ppermute | solution.py:309
  205.2 51.3 %all-to-all-start.1 = ((bf16[128,64,128]{2,1,0:T(8,128)(2,1)}), bf16[128,64,128]{2,1,0:T(8,128)(2,1)}, u32[]{:S(2)}, u32[]{:S(2)}) async-start(bf16[128,64,128]{2,1,0:T(8,128)(2,1)} %broadcast_in_dim.30), calls=%async_computation.1 | async-start | bytes 4194304 | tf_op jit(solution)/shard_map/all_to_all | solution.py:395
  215.3 28.6 %collective-permute-start.17 = (bf16[256,256]{1,0:T(8,128)(2,1)S(1)}, bf16[256,256]{1,0:T(8,128)(2,1)S(1)}, u32[]{:S(2)}, u32[]{:S(2)}) collective-permute-start(bf16[256,256]{1,0:T(8,128)(2,1)S(1)} %get-tuple-element.93), channel_id=1, source_target_pairs={{4,0},{5,1},{6,2},{7,3},{8,4},{9,5},{10,6},{11,7},{12,8},{13,9},{1... | collective-permute-start | bytes 393224 | tf_op jit(solution)/shard_map/ppermute | solution.py:309
  218.6 31.3 %collective-permute-start.16 = (bf16[256,256]{1,0:T(8,128)(2,1)S(1)}, bf16[256,256]{1,0:T(8,128)(2,1)S(1)}, u32[]{:S(2)}, u32[]{:S(2)}) collective-permute-start(bf16[256,256]{1,0:T(8,128)(2,1)S(1)} %get-tuple-element.92), channel_id=1, source_target_pairs={{2,0},{3,1},{4,2},{5,3},{6,4},{7,5},{8,6},{9,7},{10,8},{11,9},{12,... | collective-permute-start | bytes 393224 | tf_op jit(solution)/shard_map/ppermute | solution.py:309
  221.8 32.3 %copy-start.45 = (f32[256,448]{1,0:T(8,128)S(1)}, f32[256,448]{1,0:T(8,128)}, u32[]{:S(2)}) copy-start(f32[256,448]{1,0:T(8,128)} %copy-done.44) | copy-start | bytes 1376260
  221.9 28.9 %collective-permute-start.20 = (bf16[256,384]{1,0:T(8,128)(2,1)S(1)}, bf16[256,384]{1,0:T(8,128)(2,1)S(1)}, u32[]{:S(2)}, u32[]{:S(2)}) collective-permute-start(bf16[256,384]{1,0:T(8,128)(2,1)S(1)} %get-tuple-element.91), channel_id=1, source_target_pairs={{4,0},{5,1},{6,2},{7,3},{8,4},{9,5},{10,6},{11,7},{12,8},{13,9},{1... | collective-permute-start | bytes 589832 | tf_op jit(solution)/shard_map/ppermute | solution.py:309
  227.7 26.4 %collective-permute-start.19 = (bf16[256,384]{1,0:T(8,128)(2,1)S(1)}, bf16[256,384]{1,0:T(8,128)(2,1)S(1)}, u32[]{:S(2)}, u32[]{:S(2)}) collective-permute-start(bf16[256,384]{1,0:T(8,128)(2,1)S(1)} %get-tuple-element.90), channel_id=1, source_target_pairs={{2,0},{3,1},{4,2},{5,3},{6,4},{7,5},{8,6},{9,7},{10,8},{11,9},{12,... | collective-permute-start | bytes 589832 | tf_op jit(solution)/shard_map/ppermute | solution.py:309
  267.6 3.1 %copy-start.42 = (f32[5120,64]{1,0:T(8,128)S(1)}, f32[5120,64]{1,0:T(8,128)}, u32[]{:S(2)}) copy-start(f32[5120,64]{1,0:T(8,128)} %get-tuple-element.78) | copy-start | bytes 3932164
  (25 other events, 21.7 us)

commit v2 on v1

--- a/solution.py
+++ b/solution.py
@@ -17,7 +17,10 @@
 KP = 384
 HEADS = 8
 SHARE = 5
-COUNTS = (2, 3, 3)
+COUNTS = (3, 5)
+UNIT = SHARE + 1
+EDGE = UNIT * HEADS
+VMEM_ASK = 60 * 2**20
 THETA = 1000000.0
 ADAPTER_SCALE = 2.0
 LOG2E = 1.4426950408889634
@@ -38,11 +41,11 @@
     return lax.dot_general(a, b, (((0,), (0,)), ((), ())), preferred_element_type=F32)
 
 
-def attention_kernel(share, first_call, sc, fq, og, lora, qup, vup, cos, sin, dst, *rest):
+def attention_kernel(share, first_call, sc, query, og, lora, qup, vup, cos, sin, dst, *rest):
     kin, vin, lin = rest[0:6], rest[6:12], rest[12:18]
-    rest = rest[18:] if first_call else rest[19:]
-    att, dkm, dko, liftq, qupg, vupg, lvm, lvo = rest[0:8]
-    kx, vx, kt, vt, lt, bias, ss, dp, dka, dva, qn, dn, dnt, dqn, lva = rest[8:]
+    rest = rest[18:] if first_call else rest[22:]
+    att, dkm, dko, terms, liftq, lvm, lvo = rest[0:7]
+    kx, vx, kt, vt, lt, bias, ss, dp, dka, dva, qn, dn, dnt, dqn, lva = rest[7:]
     g = pl.program_id(0)
     groups = pl.num_programs(0)
     wide = share * SUB
@@ -98,14 +101,10 @@
     place(vx, vin)
     kt[...] = kx[TOK : TOK + SPANK, :].T
     vt[...] = vx[TOK : TOK + SPANK, :].T
-    lora_q = lora[:, 0:RANK]
-    extra = mm(lora_q, qup[...])
     for h in range(share):
         col = slice(h * HD, (h + 1) * HD)
-        u = fq[:, col].astype(F32) + ADAPTER_SCALE * extra[:, col]
-        qr = (u * cos[...] + pltpu.roll(u, HD // 2, 1) * sin[...]).astype(BF)
         for b in range(2):
-            qn[b, h * SUB : (h + 1) * SUB, :] = qr[b * SUB : (b + 1) * SUB]
+            qn[b, h * SUB : (h + 1) * SUB, :] = query[b * SUB : (b + 1) * SUB, col]
             dn[b, h * SUB : (h + 1) * SUB, :] = og[b * SUB : (b + 1) * SUB, col]
     pieces = [slice(i, i + KP) for i in range(0, REACH, KP)]
 
@@ -192,10 +191,10 @@
     lora_t = lora[...].astype(F32).T[0:RANK].astype(BF)
     up = mm(lora_t, dqb)
     for h in range(share):
-        qupg[h] = (ADAPTER_SCALE * up[:, h * HD : (h + 1) * HD]).astype(qupg.dtype)
+        terms[h] = (ADAPTER_SCALE * up[:, h * HD : (h + 1) * HD]).astype(BF)
     dvb = dva[TOK : TOK + SPANK, :].astype(BF)
     lva[TOK : TOK + SPANK, :] += mm_nt(dvb, vup[...])
-    vupg[0] = (ADAPTER_SCALE * mm(lt[...], dvb)[RANK : 2 * RANK]).astype(vupg.dtype)
+    terms[share] = (ADAPTER_SCALE * mm(lt[...], dvb)[RANK : 2 * RANK]).astype(BF)
     take(lambda rows: (dka[rows, :] * scale).astype(BF), dkm, dko)
 
     @pl.when(g == groups - 1)
@@ -204,8 +203,8 @@
 
 
 def prepare_kernel(normed, qdown, vdown, keys, values, vup, cos, sin, *outs):
-    lora_q = mm(normed[...], qdown[...]).astype(BF)
-    lora_v = mm(normed[...], vdown[...]).astype(BF)
+    lora = mm_nt(normed[...], jnp.concatenate([qdown[...], vdown[...]], axis=0)).astype(BF)
+    lora_v = lora[:, RANK:]
     head = 0
     for place, count in enumerate(COUNTS):
         out = outs[place]
@@ -217,8 +216,7 @@
             v = values[:, col].astype(F32) + ADAPTER_SCALE * mm(lora_v, vup[:, col])
             out[:, (count + c) * HD : (count + c + 1) * HD] = v.astype(BF)
         if place == 0:
-            out[:, 2 * count * HD : 2 * count * HD + RANK] = lora_q
-            out[:, 2 * count * HD + RANK : 2 * count * HD + 2 * RANK] = lora_v
+            out[:, 2 * count * HD : (2 * count + 1) * HD] = lora
         head += count
 
 
@@ -230,12 +228,127 @@
         out_shape=[jax.ShapeDtypeStruct((TOK, width), BF) for width in widths],
         in_specs=[vmem] * len(operands),
         out_specs=[vmem] * len(widths),
-        compiler_params=pltpu.CompilerParams(vmem_limit_bytes=40 * 2**20),
+        compiler_params=pltpu.CompilerParams(vmem_limit_bytes=VMEM_ASK),
         name="prepare",
     )(*operands)
 
 
-def attention(scalars, frozen, grad, own, qup, vup, cos, sin, dst, keyed, lorad, attended, first, count):
+def rotate_kernel(frozen, lora, qup, cos, sin, query):
+    extra = mm(lora[:, 0:RANK], qup[...])
+    for h in range(SHARE):
+        col = slice(h * HD, (h + 1) * HD)
+        u = frozen[:, col].astype(F32) + ADAPTER_SCALE * extra[:, col]
+        query[:, col] = (u * cos[...] + pltpu.roll(u, HD // 2, 1) * sin[...]).astype(BF)
+
+
+def rotate_queries(frozen, own, qup, cos, sin):
+    wide = SHARE * HD
+    tail = 2 * COUNTS[0]
+    table = pl.BlockSpec((TOK, HD), lambda g: (0, 0))
+    return pl.pallas_call(
+        rotate_kernel,
+        out_shape=jax.ShapeDtypeStruct(frozen.shape, BF),
+        grid=(HEADS,),
+        in_specs=[
+            pl.BlockSpec((TOK, wide), lambda g: (0, g)), pl.BlockSpec((TOK, HD), lambda g: (0, tail)),
+            pl.BlockSpec((RANK, wide), lambda g: (0, g)), table, table,
+        ],
+        out_specs=pl.BlockSpec((TOK, wide), lambda g: (0, g)),
+        compiler_params=pltpu.CompilerParams(vmem_limit_bytes=VMEM_ASK),
+        name="rotate_queries",
+    )(frozen, own, qup, cos, sin)
+
+
+def gradients_kernel(core, lift_q, lift_v, normed, heads, kept, given):
+    down = mm_tn(jnp.concatenate([lift_q[...], lift_v[...]], axis=1), normed[...]).astype(BF)
+    tiles = down.shape[1] // HD
+
+    def write(low, high):
+        for place, out in enumerate((low, high)):
+            out[0 : EDGE // 2] = heads[place * EDGE // 2 : (place + 1) * EDGE // 2]
+            for i in range(tiles // 2):
+                col = slice((place * tiles // 2 + i) * HD, (place * tiles // 2 + i + 1) * HD)
+                out[EDGE // 2 + i] = down[:RANK, col]
+                out[EDGE // 2 + tiles // 2 + i] = down[RANK:, col]
+
+    @pl.when(core[0] == 0)
+    def _():
+        write(kept, given)
+
+    @pl.when(core[0] != 0)
+    def _():
+        write(given, kept)
+
+
+def gradients(core, lift_q, lift_v, normed, heads):
+    vmem = pl.BlockSpec(memory_space=pltpu.VMEM)
+    half = jax.ShapeDtypeStruct((EDGE // 2 + normed.shape[1] // HD, RANK, HD), BF)
+    return pl.pallas_call(
+        gradients_kernel,
+        out_shape=[half, half],
+        in_specs=[pl.BlockSpec(memory_space=pltpu.SMEM)] + [vmem] * 4,
+        out_specs=[vmem] * 2,
+        compiler_params=pltpu.CompilerParams(vmem_limit_bytes=24 * 2**20),
+        name="gradients",
+    )(core, lift_q, lift_v, normed, heads)
+
+
+def sum_kernel(spread, out):
+    total = jnp.zeros(out.shape[1:], F32)
+    for i in range(spread.shape[0]):
+        total = total + spread[i].astype(F32)
+    low = total.astype(BF)
+    for i in range(spread.shape[0]):
+        out[i] = low
+
+
+def sum_and_copy(spread):
+    vmem = pl.BlockSpec(memory_space=pltpu.VMEM)
+    return pl.pallas_call(
+        sum_kernel, out_shape=jax.ShapeDtypeStruct(spread.shape, BF), in_specs=[vmem], out_specs=vmem, name="sum_and_copy"
+    )(spread)
+
+
+def finish_kernel(scale, core, mine, other, down_q, up_q, down_v, up_v):
+    def write(low, high):
+        for place, half in enumerate((low, high)):
+            for i in range(HEADS // 2):
+                h = place * HEADS // 2 + i
+                for c in range(SHARE):
+                    at = (h * SHARE + c) * HD
+                    up_q[:, at : at + HD] = half[i * UNIT + c].astype(F32) * scale
+                up_v[:, h * HD : (h + 1) * HD] = half[i * UNIT + SHARE].astype(F32) * scale
+            tiles = down_q.shape[1] // HD // 2
+            for i in range(tiles):
+                col = slice((place * tiles + i) * HD, (place * tiles + i + 1) * HD)
+                down_q[:, col] = half[EDGE // 2 + i].astype(F32) * scale
+                down_v[:, col] = half[EDGE // 2 + tiles + i].astype(F32) * scale
+
+    @pl.when(core[0] == 0)
+    def _():
+        write(mine, other)
+
+    @pl.when(core[0] != 0)
+    def _():
+        write(other, mine)
+
+
+def finish(core, mine, other, tokens, width):
+    vmem = pl.BlockSpec(memory_space=pltpu.VMEM)
+    query = jax.ShapeDtypeStruct((RANK, HEADS * SHARE * HD), F32)
+    down = jax.ShapeDtypeStruct((RANK, width), F32)
+    value = jax.ShapeDtypeStruct((RANK, HEADS * HD), F32)
+    return pl.pallas_call(
+        functools.partial(finish_kernel, 1.0 / tokens),
+        out_shape=[down, query, down, value],
+        in_specs=[pl.BlockSpec(memory_space=pltpu.SMEM), vmem, vmem],
+        out_specs=[vmem] * 4,
+        compiler_params=pltpu.CompilerParams(vmem_limit_bytes=VMEM_ASK),
+        name="finish",
+    )(core, mine, other)
+
+
+def attention(scalars, query, grad, own, qup, vup, cos, sin, dst, keyed, lorad, held, first, count):
     share = SHARE
     wide = share * HD
     tail = 2 * COUNTS[0]
@@ -253,26 +366,23 @@
         whole((TOK, HD)), whole((TOK, HD)), whole((1, TOK)),
     ]
     in_specs += [column(TOK, HD, 0)] * 6 + [column(TOK, HD, count)] * 6 + [lora_spec] * 6
-    operands = [scalars, frozen, grad, own, qup, vup, cos, sin, dst, *keyed, *keyed, *lorad]
+    operands = [scalars, query, grad, own, qup, vup, cos, sin, dst, *keyed, *keyed, *lorad]
     aliases = {}
-    if attended is not None:
-        aliases = {len(operands): 0}
-        operands.append(attended)
-        in_specs.append(pl.BlockSpec(memory_space=pl.ANY))
-    pair = jax.ShapeDtypeStruct((3, TOK, count * HD), BF)
+    if held is not None:
+        aliases = {len(operands) + i: i for i in range(len(held))}
+        operands += held
+        in_specs += [pl.BlockSpec(memory_space=pl.ANY)] * len(held)
+    pair = jax.ShapeDtypeStruct((3, TOK, HEADS * HD), BF)
     lift = jax.ShapeDtypeStruct((3, TOK, RANK), F32)
     out_shape = [
-        jax.ShapeDtypeStruct(frozen.shape, BF), pair, pair,
-        jax.ShapeDtypeStruct((TOK, RANK), F32),
-        jax.ShapeDtypeStruct((count * share, RANK, HD), BF),
-        jax.ShapeDtypeStruct((count, RANK, HD), BF), lift, lift,
+        jax.ShapeDtypeStruct(query.shape, BF), pair, pair, jax.ShapeDtypeStruct((EDGE, RANK, HD), BF),
+        jax.ShapeDtypeStruct((TOK, RANK), F32), lift, lift,
     ]
-    pair_spec = pl.BlockSpec((3, TOK, HD), lambda g, s: (0, 0, g))
+    pair_spec = pl.BlockSpec((3, TOK, HD), lambda g, s: (0, 0, g + first))
     out_specs = [
-        column(TOK, wide, first), pair_spec, pair_spec, whole((TOK, RANK)),
-        pl.BlockSpec((share, RANK, HD), lambda g, s: (g, 0, 0)),
-        pl.BlockSpec((1, RANK, HD), lambda g, s: (g, 0, 0)),
-        whole((3, TOK, RANK)), whole((3, TOK, RANK)),
+        column(TOK, wide, first), pair_spec, pair_spec,
+        pl.BlockSpec((UNIT, RANK, HD), lambda g, s: (g + first, 0, 0)),
+        whole((TOK, RANK)), whole((3, TOK, RANK)), whole((3, TOK, RANK)),
     ]
     wide_rows = share * SUB
     scratch = [
@@ -286,14 +396,14 @@
         pltpu.VMEM((ROWS, RANK), F32),
     ]
     return pl.pallas_call(
-        functools.partial(attention_kernel, share, attended is None),
+        functools.partial(attention_kernel, share, held is None),
         out_shape=out_shape,
         grid_spec=pltpu.PrefetchScalarGridSpec(
             num_scalar_prefetch=1, grid=(count,), in_specs=in_specs, out_specs=out_specs, scratch_shapes=scratch
         ),
         input_output_aliases=aliases,
         compiler_params=pltpu.CompilerParams(
-            dimension_semantics=("arbitrary",), vmem_limit_bytes=40 * 2**20
+            dimension_semantics=("arbitrary",), vmem_limit_bytes=VMEM_ASK
         ),
         cost_estimate=pl.CostEstimate(
             flops=12 * 2 * REACH * SUB * share * HD * count, transcendentals=2 * REACH * SUB * share * count,
@@ -352,52 +462,50 @@
     scalars = jnp.concatenate([(TOK * (1 - stretch % 2))[None], flips]).astype(jnp.int32)
 
     payloads = prepare(
-        normed_input, query_down_factor, value_down_factor, key_base, frozen_value_output, value_up_factor, cos, sin
+        normed_input, query_down_factor.T, value_down_factor.T, key_base, frozen_value_output, value_up_factor, cos, sin
     )
-    windows = []
-    for payload in payloads:
-        near, far = ahead(payload, 1), ahead(payload, 2)
-        windows.append([payload, twin(payload), near, twin(near), far, twin(far)])
-    attended = None
+    twins = [twin(payload) for payload in payloads]
+    near = [ahead(payload, 1) for payload in payloads]
+    far = [ahead(payload, 2) for payload in payloads]
+    query = rotate_queries(frozen_query_output, payloads[0], query_up_factor, cos, sin)
+    near[0], far[0], query = lax.optimization_barrier((near[0], far[0], query))
+    lorad = held = None
     first = 0
-    key_parts, lift_q, lift_mine, lift_other, query_ups, value_ups = [], 0.0, 0.0, 0.0, [], []
+    lift_q, lift_mine, lift_other = 0.0, 0.0, 0.0
     for place, count in enumerate(COUNTS):
-        attended, key_mine, key_other, lq, qu, vu, lm, lo = attention(
-            scalars, frozen_query_output, out_grad, payloads[0], query_up_factor, value_up_factor,
-            cos, sin, reach[None, :], windows[place], windows[0], attended, first, count,
+        one, two = near[place], far[place]
+        if held is not None:
+            one, two, held[0] = lax.optimization_barrier((one, two, held[0]))
+        window = [payloads[place], twins[place], one, twin(one), two, twin(two)]
+        lorad = window if lorad is None else lorad
+        *held, lq, lm, lo = attention(
+            scalars, query, out_grad, payloads[0], query_up_factor, value_up_factor,
+            cos, sin, reach[None, :], window, lorad, held, first, count,
         )
         first += count
         lift_q, lift_mine, lift_other = lift_q + lq, lift_mine + lm, lift_other + lo
-        query_ups.append(qu)
-        value_ups.append(vu)
-        if place == len(COUNTS) - 1:
-            key_mine = jnp.concatenate([key_mine, lift_mine.astype(BF)], axis=2)
-            key_other = jnp.concatenate([key_other, lift_other.astype(BF)], axis=2)
-        both = key_mine.astype(F32) + twin(key_other).astype(F32)
-        near = ahead(both[1].astype(BF), -1)
-        far = ahead(both[2].astype(BF), -2)
-        key_parts.append(both[0] + near.astype(F32) + far.astype(F32))
-    total = jnp.concatenate(key_parts, axis=1)
-    key_total = total[:, : HEADS * HD].reshape(TOK, HEADS, HD)
+    attended, key_mine, key_other, heads = held
+    lift_q = (ADAPTER_SCALE * lift_q).astype(BF)
+    lifts = lift_mine + twin(lift_other.astype(BF)).astype(F32)
+    lift_near, lift_far = ahead(lifts[1].astype(BF), -1), ahead(lifts[2].astype(BF), -2)
+    keyed = key_mine.astype(F32) + twin(key_other).astype(F32)
+    own, one, two = keyed[0], keyed[1], keyed[2].astype(BF)
+    lift_near, lift_far, own, one, two = lax.optimization_barrier((lift_near, lift_far, own, one, two))
+    passed = ahead(two, -1)
+    lift_v = lifts[0] + (lift_near.astype(F32) + lift_far.astype(F32))
+    lift_v = (ADAPTER_SCALE * lift_v).astype(BF)
+    kept, given = gradients(core[None], lift_q, lift_v, normed_input, heads)
+    kept = (kept.astype(F32) + twin(given).astype(F32)).astype(BF)
+    cores = [list(range(c, devices, 2)) for c in range(2)]
+    spread = lax.all_to_all(kept, "ctx", 0, 0, axis_index_groups=cores, tiled=True)
+    one = (one + passed.astype(F32)).astype(BF)
+    key_total = own + ahead(one, -1).astype(F32)
+    key_total = key_total.reshape(TOK, HEADS, HD)
     swapped = jnp.concatenate([key_total[..., half:], key_total[..., :half]], axis=-1)
     key_grad = (key_total * cos[:, None, :] - swapped * sin[:, None, :]).astype(BF).reshape(TOK, HEADS * HD)
-    lift_q = (ADAPTER_SCALE * lift_q).astype(BF)
-    lift_v = (ADAPTER_SCALE * total[:, HEADS * HD :]).astype(BF)
-    lifts = jnp.concatenate([lift_q, lift_v], axis=1)
-    width = normed_input.shape[1]
-    tiles = width // HD
-    downs = jnp.einsum("tr,td->rd", lifts, normed_input, preferred_element_type=F32).astype(BF)
-    downs = jnp.transpose(downs.reshape(2 * RANK, tiles, HD), (1, 0, 2)).reshape(-1, HD)
-    terms = jnp.concatenate([downs] + [x.reshape(-1, HD) for x in query_ups + value_ups], axis=0)
-    rows = terms.shape[0] // devices
-    spread = lax.all_to_all(terms.reshape(devices, rows, HD), "ctx", 0, 0)
-    summed = jnp.sum(spread.astype(F32), axis=0).astype(BF)
-    whole = lax.all_to_all(jnp.broadcast_to(summed[None], (devices, rows, HD)), "ctx", 0, 0).reshape(-1, HD)
-    whole = whole.astype(F32) / (TOK * devices)
-    downs = jnp.transpose(whole[: tiles * 2 * RANK].reshape(tiles, 2 * RANK, HD), (0, 2, 1)).reshape(width, 2 * RANK)
-    ups = jnp.transpose(whole[tiles * 2 * RANK :].reshape(-1, RANK, HD), (1, 0, 2)).reshape(RANK, -1)
-    query_width = HEADS * SHARE * HD
-    return (attended, key_grad, downs[:, :RANK], ups[:, :query_width], downs[:, RANK:], ups[:, query_width:])
+    gathered = lax.all_to_all(sum_and_copy(spread), "ctx", 0, 0, axis_index_groups=cores, tiled=True)
+    down_q, up_q, down_v, up_v = finish(core[None], gathered, twin(gathered), TOK * devices, normed_input.shape[1])
+    return (attended, key_grad, down_q.T, up_q, down_v.T, up_v)
 
 
 def solution(mesh):

time: 278 us -> 203 us (0.73); the launches traced: 273 us -> 201 us
  local copies, waits for them, and re-layouts: 48.6 us -> 5.97 us
  starting transfers between devices: 79.8 us -> 51.2 us
  Pallas kernels: 68.4 us -> 82.1 us
  waiting for transfers between devices: 58 us -> 45.8 us
    ppermute x24 -> x18, starting transfers between devices: 59.9 us -> 31.1 us  [moved(): return lax.ppermute(block, 'ctx', route)]
    unnamed x105 -> x39, local copies, waits for them, and re-layouts: 31.2 us -> 2.66 us
    ppermute x24 -> x18, waiting for transfers between devices: 34.3 us -> 16.3 us  [moved(): return lax.ppermute(block, 'ctx', route)]
    pallas_call x3 -> x6, Pallas kernels: 65.7 us -> 77.3 us  [the longest x2 62.5 us: attention(): pl.pallas_call(functools.partial(attention_kernel, share, held is None),...]
    slice x4 -> x0, local copies, waits for them, and re-layouts: 6.68 us -> none  [the longest x1 3.17 us: on_device(): downs[:, RANK:]]
    all_to_all x2, waiting for transfers between devices: 23.7 us -> 29.6 us  [the longest x1 22.2 us: on_device(): lax.all_to_all(kept, 'ctx', 0, 0, axis_index_groups=cores, tiled=True)]
  transfers between devices with their start and end apart: 26 -> 20, of which waited for: 10 -> 10; matrix products, arithmetic and copies ran while one was open for 4% -> 6% of each run, Pallas kernels for 15% -> 17%
where the time goes in v2:
time: 203 us; the launch traced here: 201 us
  Pallas kernels  82.1 us (40%)
  starting transfers between devices  51.2 us (25%)
  waiting for transfers between devices  45.8 us (23%)
  other arithmetic  12.5 us (6%)
  local copies, waits for them, and re-layouts  5.97 us (3%)
  between operations  3.68 us (2%)
    pallas_call x2, Pallas kernels, attention(): pl.pallas_call(functools.partial(attention_kernel, share, held is None),...  62.5 us
    ppermute x18, starting transfers between devices, moved(): return lax.ppermute(block, 'ctx', route)  31.1 us
    all_to_all x1, waiting for transfers between devices, on_device(): lax.all_to_all(kept, 'ctx', 0, 0, axis_index_groups=cores, tiled=True)  22.2 us
    ppermute x18, waiting for transfers between devices, moved(): return lax.ppermute(block, 'ctx', route)  16.3 us
    all_to_all x1, starting transfers between devices, on_device(): lax.all_to_all(kept, 'ctx', 0, 0, axis_index_groups=cores, tiled=True)  10.1 us
    all_to_all x1, starting transfers between devices, on_device(): lax.all_to_all(sum_and_copy(spread), 'ctx', 0, 0, axis_index_groups=cores...  9.97 us
    pallas_call x1, Pallas kernels, rotate_queries(): pl.pallas_call(rotate_kernel, out_shape=jax.ShapeDtypeStruct(frozen.shape...  7.56 us
    all_to_all x1, waiting for transfers between devices, on_device(): lax.all_to_all(sum_and_copy(spread), 'ctx', 0, 0, axis_index_groups=cores...  7.4 us
  transfers between devices with their start and end apart: 20, of which 10 were waited for; matrix products, arithmetic and copies ran while one was open for 6% of the time, Pallas kernels for 17%

profile of v2, /device:TPU:62, one launch (start us, length us, event | category | flops | bytes accessed | tf_op | source)
XLA Modules:
  0.0 201.3 jit_solution(9401711007328139778)
XLA Ops:
  0.7 1.2 dynamic_slice.3
  2.6 0.8 select_reduce_fusion.1
  3.4 0.5 fusion.6
  4.0 0.8 pad_maximum_fusion
  4.8 4.9 %prepare.1 = (bf16[256,896]{1,0:T(8,128)(2,1)}, bf16[256,1280]{1,0:T(8,128)(2,1)}) custom-call(bf16[256,5120]{1,0:T(8,128)(2,1)} %normed.3, bf16[64,5120]{1,0:T(8,128)(2,1)} %bitcast.44, bf16[64,5120]{1,0:T(8,128)(2,1)} %bitcast.45, bf16[256,1024]{1,0:T(8,128)(2,1)} %keys.1, bf16[256,1024]{1,0:T(8,128)(2,1)} %values.1, bf16[64,1024]{1,0:T(8,128)(2,1)} %vup.5, ...), custom_call_target="tpu_custom_call" | custom-call | tf_op jit(solution)/shard_map/prepare/pallas_call | solution.py:226
  9.7 3.4 %collective-permute-start = (bf16[256,896]{1,0:T(8,128)(2,1)}, bf16[256,896]{1,0:T(8,128)(2,1)S(1)}, u32[]{:S(2)}, u32[]{:S(2)}) collective-permute-start(bf16[256,896]{1,0:T(8,128)(2,1)} %get-tuple-element.39.lora.rest_0_.rest_6_.rest_12_), channel_id=1, source_target_pairs={{0,2},{1,3},{2,4},{3,5},{4,6},{5,7},{6,8},{7,9},{8,10},{9,11},{10,... | collective-permute-start | bytes 1376264 | tf_op jit(solution)/shard_map/ppermute | solution.py:419
  13.1 4.3 %collective-permute-start.1 = (bf16[256,896]{1,0:T(8,128)(2,1)}, bf16[256,896]{1,0:T(8,128)(2,1)}, u32[]{:S(2)}, u32[]{:S(2)}) collective-permute-start(bf16[256,896]{1,0:T(8,128)(2,1)} %get-tuple-element.39.lora.rest_0_.rest_6_.rest_12_), channel_id=1, source_target_pairs={{0,4},{1,5},{2,6},{3,7},{4,8},{5,9},{6,10},{7,11},{8,12},{9,13},{1... | collective-permute-start | bytes 1376264 | tf_op jit(solution)/shard_map/ppermute | solution.py:419
  17.5 3.7 %collective-permute-start.3 = (bf16[256,1280]{1,0:T(8,128)(2,1)}, bf16[256,1280]{1,0:T(8,128)(2,1)S(1)}, u32[]{:S(2)}, u32[]{:S(2)}) collective-permute-start(bf16[256,1280]{1,0:T(8,128)(2,1)} %get-tuple-element.41.rest_0_.rest_6_), channel_id=1, source_target_pairs={{0,2},{1,3},{2,4},{3,5},{4,6},{5,7},{6,8},{7,9},{8,10},{9,11},{10,... | collective-permute-start | bytes 1966088 | tf_op jit(solution)/shard_map/ppermute | solution.py:419
  21.2 3.1 %collective-permute-start.4 = (bf16[256,1280]{1,0:T(8,128)(2,1)}, bf16[256,1280]{1,0:T(8,128)(2,1)S(1)}, u32[]{:S(2)}, u32[]{:S(2)}) collective-permute-start(bf16[256,1280]{1,0:T(8,128)(2,1)} %get-tuple-element.41.rest_0_.rest_6_), channel_id=1, source_target_pairs={{0,4},{1,5},{2,6},{3,7},{4,8},{5,9},{6,10},{7,11},{8,12},{9,13},{1... | collective-permute-start | bytes 1966088 | tf_op jit(solution)/shard_map/ppermute | solution.py:419
  26.4 0.6 gather_fusion
  27.0 7.6 %rotate_queries.1.query = bf16[256,5120]{1,0:T(8,128)(2,1)} custom-call(bf16[256,5120]{1,0:T(8,128)(2,1)} %frozen.1, bf16[256,896]{1,0:T(8,128)(2,1)} %get-tuple-element.39.lora.rest_0_.rest_6_.rest_12_, bf16[64,5120]{1,0:T(8,128)(2,1)} %qup.5, f32[256,128]{1,0:T(8,128)} %get-tuple-element.83.cos, f32[256,128]{1,0:T(8,128)} %get-tuple-element.84.sin), custom_call_target="tpu_custom_call" | custom-call | tf_op jit(solution)/shard_map/rotate_queries/pallas_call | solution.py:248
  34.7 0.5 collective-permute-start.7
  35.2 0.6 subtract_subtract_fusion.dst
  35.8 0.7 pad_add_fusion.sc
  36.5 1.0 collective-permute-done.7.rest_5_.rest_11_.rest_17_
  37.5 24.3 %attention.2 = (bf16[256,5120]{1,0:T(8,128)(2,1)}, bf16[3,256,1024]{2,1,0:T(8,128)(2,1)}, bf16[3,256,1024]{2,1,0:T(8,128)(2,1)}, bf16[48,64,128]{2,1,0:T(8,128)(...) custom-call(s32[4]{0:T(128)} %pad_add_fusion.sc, bf16[256,5120]{1,0:T(8,128)(2,1)} %rotate_queries.1.query, ...), custom_call_target="tpu_custom_call" | custom-call | flops 6794772480 | bytes 2359296 | tf_op jit(solution)/shard_map/attention/pallas_call | solution.py:398
  62.5 1.6 collective-permute-done.8.rest_3_.rest_9_
  64.0 0.9 collective-permute-done.9.rest_5_.rest_11_
  65.0 0.9 copy-done.16
  65.9 38.2 %attention.3 = (bf16[256,5120]{1,0:T(8,128)(2,1)}, bf16[3,256,1024]{2,1,0:T(8,128)(2,1)}, bf16[3,256,1024]{2,1,0:T(8,128)(2,1)}, bf16[48,64,128]{2,1,0:T(8,128)(...) custom-call(s32[4]{0:T(128)} %pad_add_fusion.sc, ...), custom_call_target="tpu_custom_call", output_to_operand_aliasing={{0}: (27, {}), {1}: (28, {}), {2}: (29, {}), {3}: (30, {})} | custom-call | flops 11324620800 | bytes 3932160 | tf_op jit(solution)/shard_map/attention/pallas_call | solution.py:398
  104.3 1.1 add_convert_fusion.2
  105.5 0.4 collective-permute-start.10
  105.8 0.9 multiply_convert_fusion.lift_q
  106.8 1.1 collective-permute-done.10
  107.9 1.1 fusion.9
  109.0 3.6 %collective-permute-start.11 = (bf16[256,64]{1,0:T(8,128)(2,1)S(1)}, bf16[256,64]{1,0:T(8,128)(2,1)S(1)}, u32[]{:S(2)}, u32[]{:S(2)}) collective-permute-start(bf16[256,64]{1,0:T(8,128)(2,1)S(1)} %get-tuple-element.79), channel_id=1, source_target_pairs={{2,0},{3,1},{4,2},{5,3},{6,4},{7,5},{8,6},{9,7},{10,8},{11,9},{12,... | collective-permute-start | bytes 98312 | tf_op jit(solution)/shard_map/ppermute | solution.py:419
  112.6 5.4 %collective-permute-start.12 = (bf16[256,64]{1,0:T(8,128)(2,1)S(1)}, bf16[256,64]{1,0:T(8,128)(2,1)S(1)}, u32[]{:S(2)}, u32[]{:S(2)}) collective-permute-start(bf16[256,64]{1,0:T(8,128)(2,1)S(1)} %get-tuple-element.78), channel_id=1, source_target_pairs={{4,0},{5,1},{6,2},{7,3},{8,4},{9,5},{10,6},{11,7},{12,8},{13,9},{1... | collective-permute-start | bytes 98312 | tf_op jit(solution)/shard_map/ppermute | solution.py:419
  118.1 0.6 convert_add_fusion
  118.9 0.9 fusion.2
  119.9 3.4 %collective-permute-done.12 = bf16[256,64]{1,0:T(8,128)(2,1)S(1)} collective-permute-done((bf16[256,64]{1,0:T(8,128)(2,1)S(1)}, bf16[256,64]{1,0:T(8,128)(2,1)S(1)}, u32[]{:S(2)}, u32[]{:S(2)}) %collective-permute-start.12) | collective-permute-done | bytes 32800 | tf_op jit(solution)/shard_map/ppermute | solution.py:419
  123.3 0.8 gradients.1
  124.2 2.6 %collective-permute-done.16 = bf16[64,64,128]{2,1,0:T(8,128)(2,1)S(1)} collective-permute-done((bf16[64,64,128]{2,1,0:T(8,128)(2,1)S(1)}, bf16[64,64,128]{2,1,0:T(8,128)(2,1)S(1)}, u32[]{:S(2)}, u32[]{:S(2)}) %collective-permute-start.16) | collective-permute-done | bytes 1048608 | tf_op jit(solution)/shard_map/ppermute | solution.py:419
  126.9 1.4 add_convert_fusion
  128.2 10.1 %all-to-all-start = ((bf16[64,64,128]{2,1,0:T(8,128)(2,1)}), bf16[64,64,128]{2,1,0:T(8,128)(2,1)S(1)}, u32[]{:S(2)}, u32[]{:S(2)}) async-start(bf16[64,64,128]{2,1,0:T(8,128)(2,1)} %add_convert_fusion), calls=%async_computation | async-start | bytes 2097152 | tf_op jit(solution)/shard_map/all_to_all | solution.py:500
  138.4 2.8 %collective-permute-start.14 = (bf16[256,1024]{1,0:T(8,128)(2,1)}, bf16[256,1024]{1,0:T(8,128)(2,1)}, u32[]{:S(2)}, u32[]{:S(2)}) collective-permute-start(bf16[256,1024]{1,0:T(8,128)(2,1)} %fusion.2), channel_id=1, source_target_pairs={{2,0},{3,1},{4,2},{5,3},{6,4},{7,5},{8,6},{9,7},{10,8},{11,9},{12,... | collective-permute-start | bytes 1572872 | tf_op jit(solution)/shard_map/ppermute | solution.py:419
  141.2 22.2 %all-to-all-done.spread = bf16[64,64,128]{2,1,0:T(8,128)(2,1)S(1)} async-done(((bf16[64,64,128]{2,1,0:T(8,128)(2,1)}), bf16[64,64,128]{2,1,0:T(8,128)(2,1)S(1)}, u32[]{:S(2)}, u32[]{:S(2)}) %all-to-all-start) | async-done | bytes 1048608 | tf_op jit(solution)/shard_map/all_to_all | solution.py:500
  163.3 1.0 copy-done.4
  164.3 2.5 %sum_and_copy.1 = bf16[64,64,128]{2,1,0:T(8,128)(2,1)} custom-call(bf16[64,64,128]{2,1,0:T(8,128)(2,1)} %copy-done.4), custom_call_target="tpu_custom_call" | custom-call | tf_op jit(solution)/shard_map/sum_and_copy/pallas_call | solution.py:307
  166.8 10.0 %all-to-all-start.1 = ((bf16[64,64,128]{2,1,0:T(8,128)(2,1)}), bf16[64,64,128]{2,1,0:T(8,128)(2,1)S(1)}, u32[]{:S(2)}, u32[]{:S(2)}) async-start(bf16[64,64,128]{2,1,0:T(8,128)(2,1)} %sum_and_copy.1), calls=%async_computation.1 | async-start | bytes 2097152 | tf_op jit(solution)/shard_map/all_to_all | solution.py:506
  176.8 2.0 add_convert_fusion.1
  178.7 2.7 %collective-permute-start.15 = (bf16[256,1024]{1,0:T(8,128)(2,1)}, bf16[256,1024]{1,0:T(8,128)(2,1)S(1)}, u32[]{:S(2)}, u32[]{:S(2)}) collective-permute-start(bf16[256,1024]{1,0:T(8,128)(2,1)} %add_convert_fusion.1), channel_id=1, source_target_pairs={{2,0},{3,1},{4,2},{5,3},{6,4},{7,5},{8,6},{9,7},{10,8},{11,9},{12,... | collective-permute-start | bytes 1572872 | tf_op jit(solution)/shard_map/ppermute | solution.py:419
  181.5 7.4 %all-to-all-done.1.mine = bf16[64,64,128]{2,1,0:T(8,128)(2,1)S(1)} async-done(((bf16[64,64,128]{2,1,0:T(8,128)(2,1)}), bf16[64,64,128]{2,1,0:T(8,128)(2,1)S(1)}, u32[]{:S(2)}, u32[]{:S(2)}) %all-to-all-start.1) | async-done | bytes 1048608 | tf_op jit(solution)/shard_map/all_to_all | solution.py:506
  188.9 5.4 %collective-permute-done.15 = bf16[256,1024]{1,0:T(8,128)(2,1)S(1)} collective-permute-done((bf16[256,1024]{1,0:T(8,128)(2,1)}, bf16[256,1024]{1,0:T(8,128)(2,1)S(1)}, u32[]{:S(2)}, u32[]{:S(2)}) %collective-permute-start.15) | collective-permute-done | bytes 524320 | tf_op jit(solution)/shard_map/ppermute | solution.py:419
  194.7 0.3 fusion.10
  195.1 0.5 copy-done.6
  195.6 0.4 maximum_multiply_fusion
  196.1 1.3 fusion
  197.4 3.9 %finish.1 = (f32[64,5120]{1,0:T(8,128)}, f32[64,5120]{1,0:T(8,128)}, f32[64,5120]{1,0:T(8,128)}, f32[64,1024]{1,0:T(8,128)}) custom-call(s32[1]{0:T(128)} %bitcast.11.core, bf16[64,64,128]{2,1,0:T(8,128)(2,1)} %copy-done.3, bf16[64,64,128]{2,1,0:T(8,128)(2,1)} %collective-permute-done.17.other), custom_call_target="tpu_custom_call" | custom-call | tf_op jit(solution)/shard_map/finish/pallas_call | solution.py:341
  (67 shorter events, 2.2 us)
Async XLA Ops:
  4.8 21.5 %copy-start.2 = (s32[128]{0:T(128)S(1)}, s32[128]{0:T(128)}, u32[]{:S(2)}) copy-start(s32[128]{0:T(128)} %param.21) | copy-start | bytes 1540
  9.7 24.9 %collective-permute-start = (bf16[256,896]{1,0:T(8,128)(2,1)}, bf16[256,896]{1,0:T(8,128)(2,1)S(1)}, u32[]{:S(2)}, u32[]{:S(2)}) collective-permute-start(bf16[256,896]{1,0:T(8,128)(2,1)} %get-tuple-element.39.lora.rest_0_.rest_6_.rest_12_), channel_id=1, source_target_pairs={{0,2},{1,3},{2,4},{3,5},{4,6},{5,7},{6,8},{7,9},{8,10},{9,11},{10,... | collective-permute-start | bytes 1376264 | tf_op jit(solution)/shard_map/ppermute | solution.py:419
  13.1 21.5 %collective-permute-start.1 = (bf16[256,896]{1,0:T(8,128)(2,1)}, bf16[256,896]{1,0:T(8,128)(2,1)}, u32[]{:S(2)}, u32[]{:S(2)}) collective-permute-start(bf16[256,896]{1,0:T(8,128)(2,1)} %get-tuple-element.39.lora.rest_0_.rest_6_.rest_12_), channel_id=1, source_target_pairs={{0,4},{1,5},{2,6},{3,7},{4,8},{5,9},{6,10},{7,11},{8,12},{9,13},{1... | collective-permute-start | bytes 1376264 | tf_op jit(solution)/shard_map/ppermute | solution.py:419
  17.4 19.0 %collective-permute-start.5 = (bf16[256,896]{1,0:T(8,128)(2,1)}, bf16[256,896]{1,0:T(8,128)(2,1)}, u32[]{:S(2)}, u32[]{:S(2)}) collective-permute-start(bf16[256,896]{1,0:T(8,128)(2,1)} %get-tuple-element.39.lora.rest_0_.rest_6_.rest_12_), channel_id=1, source_target_pairs={{0,1},{1,0},{2,3},{3,2},{4,5},{5,4},{6,7},{7,6},{8,9},{9,8},{10,11... | collective-permute-start | bytes 1376264 | tf_op jit(solution)/shard_map/ppermute | solution.py:419
  17.5 44.3 %collective-permute-start.3 = (bf16[256,1280]{1,0:T(8,128)(2,1)}, bf16[256,1280]{1,0:T(8,128)(2,1)S(1)}, u32[]{:S(2)}, u32[]{:S(2)}) collective-permute-start(bf16[256,1280]{1,0:T(8,128)(2,1)} %get-tuple-element.41.rest_0_.rest_6_), channel_id=1, source_target_pairs={{0,2},{1,3},{2,4},{3,5},{4,6},{5,7},{6,8},{7,9},{8,10},{9,11},{10,... | collective-permute-start | bytes 1966088 | tf_op jit(solution)/shard_map/ppermute | solution.py:419
  21.2 40.6 %collective-permute-start.4 = (bf16[256,1280]{1,0:T(8,128)(2,1)}, bf16[256,1280]{1,0:T(8,128)(2,1)S(1)}, u32[]{:S(2)}, u32[]{:S(2)}) collective-permute-start(bf16[256,1280]{1,0:T(8,128)(2,1)} %get-tuple-element.41.rest_0_.rest_6_), channel_id=1, source_target_pairs={{0,4},{1,5},{2,6},{3,7},{4,8},{5,9},{6,10},{7,11},{8,12},{9,13},{1... | collective-permute-start | bytes 1966088 | tf_op jit(solution)/shard_map/ppermute | solution.py:419
  27.0 9.4 %copy-start.11 = (bf16[256,1280]{1,0:T(8,128)(2,1)S(1)}, bf16[256,1280]{1,0:T(8,128)(2,1)}, u32[]{:S(2)}) copy-start(bf16[256,1280]{1,0:T(8,128)(2,1)} %get-tuple-element.41.rest_0_.rest_6_) | copy-start | bytes 1966084
  34.6 2.9 %copy-start.17 = (bf16[256,896]{1,0:T(8,128)(2,1)}, bf16[256,896]{1,0:T(8,128)(2,1)S(1)}, u32[]{:S(2)}) copy-start(bf16[256,896]{1,0:T(8,128)(2,1)S(1)} %collective-permute-done.rest_2_.rest_8_.rest_14_) | copy-start | bytes 1376260
  34.6 1.9 collective-permute-start.6
  34.7 2.8 %collective-permute-start.7 = (bf16[256,896]{1,0:T(8,128)(2,1)}, bf16[256,896]{1,0:T(8,128)(2,1)}, u32[]{:S(2)}, u32[]{:S(2)}) collective-permute-start(bf16[256,896]{1,0:T(8,128)(2,1)} %collective-permute-done.1.rest_4_.rest_10_.rest_16_), channel_id=1, source_target_pairs={{0,1},{1,0},{2,3},{3,2},{4,5},{5,4},{6,7},{7,6},{8,9},{9,8},{10,11... | collective-permute-start | bytes 1376264 | tf_op jit(solution)/shard_map/ppermute | solution.py:419
  36.4 26.0 %collective-permute-start.2 = (bf16[256,1280]{1,0:T(8,128)(2,1)S(1)}, bf16[256,1280]{1,0:T(8,128)(2,1)S(1)}, u32[]{:S(2)}, u32[]{:S(2)}) collective-permute-start(bf16[256,1280]{1,0:T(8,128)(2,1)S(1)} %copy-done.11), channel_id=1, source_target_pairs={{0,1},{1,0},{2,3},{3,2},{4,5},{5,4},{6,7},{7,6},{8,9},{9,8},{10,11... | collective-permute-start | bytes 1966088 | tf_op jit(solution)/shard_map/ppermute | solution.py:419
  36.5 1.0 copy-start.18
  61.8 4.0 %copy-start.12 = (bf16[256,1280]{1,0:T(8,128)(2,1)}, bf16[256,1280]{1,0:T(8,128)(2,1)S(1)}, u32[]{:S(2)}) copy-start(bf16[256,1280]{1,0:T(8,128)(2,1)S(1)} %collective-permute-done.3.rest_2_.rest_8_) | copy-start | bytes 1966084
  61.8 4.0 %copy-start.13 = (bf16[256,1280]{1,0:T(8,128)(2,1)}, bf16[256,1280]{1,0:T(8,128)(2,1)S(1)}, u32[]{:S(2)}) copy-start(bf16[256,1280]{1,0:T(8,128)(2,1)S(1)} %collective-permute-done.4.rest_4_.rest_10_) | copy-start | bytes 1966084
  61.9 2.2 %collective-permute-start.8 = (bf16[256,1280]{1,0:T(8,128)(2,1)S(1)}, bf16[256,1280]{1,0:T(8,128)(2,1)S(1)}, u32[]{:S(2)}, u32[]{:S(2)}) collective-permute-start(bf16[256,1280]{1,0:T(8,128)(2,1)S(1)} %collective-permute-done.3.rest_2_.rest_8_), channel_id=1, source_target_pairs={{0,1},{1,0},{2,3},{3,2},{4,5},{5,4},{6,7},{7,6},{8,9},{9,8},{10,11... | collective-permute-start | bytes 1966088 | tf_op jit(solution)/shard_map/ppermute | solution.py:419
  62.1 2.9 %collective-permute-start.9 = (bf16[256,1280]{1,0:T(8,128)(2,1)S(1)}, bf16[256,1280]{1,0:T(8,128)(2,1)S(1)}, u32[]{:S(2)}, u32[]{:S(2)}) collective-permute-start(bf16[256,1280]{1,0:T(8,128)(2,1)S(1)} %collective-permute-done.4.rest_4_.rest_10_), channel_id=1, source_target_pairs={{0,1},{1,0},{2,3},{3,2},{4,5},{5,4},{6,7},{7,6},{8,9},{9,8},{10,11... | collective-permute-start | bytes 1966088 | tf_op jit(solution)/shard_map/ppermute | solution.py:419
  62.4 3.4 %copy-start.14 = (bf16[256,1280]{1,0:T(8,128)(2,1)}, bf16[256,1280]{1,0:T(8,128)(2,1)S(1)}, u32[]{:S(2)}) copy-start(bf16[256,1280]{1,0:T(8,128)(2,1)S(1)} %collective-permute-done.2.rest_1_.rest_7_) | copy-start | bytes 1966084
  64.0 0.9 copy-start.15
  65.0 0.9 copy-start.16
  65.9 38.5 %copy-start.9 = (f32[3,256,64]{2,1,0:T(8,128)S(1)}, f32[3,256,64]{2,1,0:T(8,128)}, u32[]{:S(2)}) copy-start(f32[3,256,64]{2,1,0:T(8,128)} %get-tuple-element.54) | copy-start | bytes 589828
  65.9 40.0 %copy-start.10 = (f32[256,64]{1,0:T(8,128)S(1)}, f32[256,64]{1,0:T(8,128)}, u32[]{:S(2)}) copy-start(f32[256,64]{1,0:T(8,128)} %get-tuple-element.61) | copy-start | bytes 196612
  65.9 42.0 %copy-start.8 = (f32[3,256,64]{2,1,0:T(8,128)S(1)}, f32[3,256,64]{2,1,0:T(8,128)}, u32[]{:S(2)}) copy-start(f32[3,256,64]{2,1,0:T(8,128)} %get-tuple-element.52) | copy-start | bytes 589828
  104.1 13.9 %copy-start.7 = (bf16[3,256,1024]{2,1,0:T(8,128)(2,1)S(1)}, bf16[3,256,1024]{2,1,0:T(8,128)(2,1)}, u32[]{:S(2)}) copy-start(bf16[3,256,1024]{2,1,0:T(8,128)(2,1)} %get-tuple-element.56) | copy-start | bytes 4718596
  104.1 13.9 %collective-permute-start.13 = (bf16[3,256,1024]{2,1,0:T(8,128)(2,1)}, bf16[3,256,1024]{2,1,0:T(8,128)(2,1)S(1)}, u32[]{:S(2)}, u32[]{:S(2)}) collective-permute-start(bf16[3,256,1024]{2,1,0:T(8,128)(2,1)} %get-tuple-element.57), channel_id=1, source_target_pairs={{0,1},{1,0},{2,3},{3,2},{4,5},{5,4},{6,7},{7,6},{8,9},{9,8},{10,11... | collective-permute-start | bytes 4718600 | tf_op jit(solution)/shard_map/ppermute | solution.py:419
  105.5 2.4 %collective-permute-start.10 = (bf16[3,256,64]{2,1,0:T(8,128)(2,1)S(1)}, bf16[3,256,64]{2,1,0:T(8,128)(2,1)S(1)}, u32[]{:S(2)}, u32[]{:S(2)}) collective-permute-start(bf16[3,256,64]{2,1,0:T(8,128)(2,1)S(1)} %add_convert_fusion.2), channel_id=1, source_target_pairs={{0,1},{1,0},{2,3},{3,2},{4,5},{5,4},{6,7},{7,6},{8,9},{9,8},{10,11... | collective-permute-start | bytes 294920 | tf_op jit(solution)/shard_map/ppermute | solution.py:419
  109.0 10.9 %collective-permute-start.11 = (bf16[256,64]{1,0:T(8,128)(2,1)S(1)}, bf16[256,64]{1,0:T(8,128)(2,1)S(1)}, u32[]{:S(2)}, u32[]{:S(2)}) collective-permute-start(bf16[256,64]{1,0:T(8,128)(2,1)S(1)} %get-tuple-element.79), channel_id=1, source_target_pairs={{2,0},{3,1},{4,2},{5,3},{6,4},{7,5},{8,6},{9,7},{10,8},{11,9},{12,... | collective-permute-start | bytes 98312 | tf_op jit(solution)/shard_map/ppermute | solution.py:419
  112.6 10.7 %collective-permute-start.12 = (bf16[256,64]{1,0:T(8,128)(2,1)S(1)}, bf16[256,64]{1,0:T(8,128)(2,1)S(1)}, u32[]{:S(2)}, u32[]{:S(2)}) collective-permute-start(bf16[256,64]{1,0:T(8,128)(2,1)S(1)} %get-tuple-element.78), channel_id=1, source_target_pairs={{4,0},{5,1},{6,2},{7,3},{8,4},{9,5},{10,6},{11,7},{12,8},{13,9},{1... | collective-permute-start | bytes 98312 | tf_op jit(solution)/shard_map/ppermute | solution.py:419
  118.7 4.6 %copy-start = (bf16[256,5120]{1,0:T(8,128)(2,1)S(1)}, bf16[256,5120]{1,0:T(8,128)(2,1)}, u32[]{:S(2)}) copy-start(bf16[256,5120]{1,0:T(8,128)(2,1)} %normed.3) | copy-start | bytes 7864324
  118.7 4.6 %copy-start.1 = (bf16[48,64,128]{2,1,0:T(8,128)(2,1)S(1)}, bf16[48,64,128]{2,1,0:T(8,128)(2,1)}, u32[]{:S(2)}) copy-start(bf16[48,64,128]{2,1,0:T(8,128)(2,1)} %get-tuple-element.65.heads) | copy-start | bytes 2359300
  124.1 2.7 %collective-permute-start.16 = (bf16[64,64,128]{2,1,0:T(8,128)(2,1)S(1)}, bf16[64,64,128]{2,1,0:T(8,128)(2,1)S(1)}, u32[]{:S(2)}, u32[]{:S(2)}) collective-permute-start(bf16[64,64,128]{2,1,0:T(8,128)(2,1)S(1)} %get-tuple-element.67), channel_id=1, source_target_pairs={{0,1},{1,0},{2,3},{3,2},{4,5},{5,4},{6,7},{7,6},{8,9},{9,8},{10,11... | collective-permute-start | bytes 3145736 | tf_op jit(solution)/shard_map/ppermute | solution.py:419
  128.2 35.1 %all-to-all-start = ((bf16[64,64,128]{2,1,0:T(8,128)(2,1)}), bf16[64,64,128]{2,1,0:T(8,128)(2,1)S(1)}, u32[]{:S(2)}, u32[]{:S(2)}) async-start(bf16[64,64,128]{2,1,0:T(8,128)(2,1)} %add_convert_fusion), calls=%async_computation | async-start | bytes 2097152 | tf_op jit(solution)/shard_map/all_to_all | solution.py:500
  138.4 38.4 %collective-permute-start.14 = (bf16[256,1024]{1,0:T(8,128)(2,1)}, bf16[256,1024]{1,0:T(8,128)(2,1)}, u32[]{:S(2)}, u32[]{:S(2)}) collective-permute-start(bf16[256,1024]{1,0:T(8,128)(2,1)} %fusion.2), channel_id=1, source_target_pairs={{2,0},{3,1},{4,2},{5,3},{6,4},{7,5},{8,6},{9,7},{10,8},{11,9},{12,... | collective-permute-start | bytes 1572872 | tf_op jit(solution)/shard_map/ppermute | solution.py:419
  163.3 1.0 copy-start.4
  166.8 22.1 %all-to-all-start.1 = ((bf16[64,64,128]{2,1,0:T(8,128)(2,1)}), bf16[64,64,128]{2,1,0:T(8,128)(2,1)S(1)}, u32[]{:S(2)}, u32[]{:S(2)}) async-start(bf16[64,64,128]{2,1,0:T(8,128)(2,1)} %sum_and_copy.1), calls=%async_computation.1 | async-start | bytes 2097152 | tf_op jit(solution)/shard_map/all_to_all | solution.py:506
  178.7 15.6 %collective-permute-start.15 = (bf16[256,1024]{1,0:T(8,128)(2,1)}, bf16[256,1024]{1,0:T(8,128)(2,1)S(1)}, u32[]{:S(2)}, u32[]{:S(2)}) collective-permute-start(bf16[256,1024]{1,0:T(8,128)(2,1)} %add_convert_fusion.1), channel_id=1, source_target_pairs={{2,0},{3,1},{4,2},{5,3},{6,4},{7,5},{8,6},{9,7},{10,8},{11,9},{12,... | collective-permute-start | bytes 1572872 | tf_op jit(solution)/shard_map/ppermute | solution.py:419
  188.9 5.8 %copy-start.3 = (bf16[64,64,128]{2,1,0:T(8,128)(2,1)}, bf16[64,64,128]{2,1,0:T(8,128)(2,1)S(1)}, u32[]{:S(2)}) copy-start(bf16[64,64,128]{2,1,0:T(8,128)(2,1)S(1)} %all-to-all-done.1.mine) | copy-start | bytes 3145732
  188.9 8.5 %collective-permute-start.17 = (bf16[64,64,128]{2,1,0:T(8,128)(2,1)S(1)}, bf16[64,64,128]{2,1,0:T(8,128)(2,1)}, u32[]{:S(2)}, u32[]{:S(2)}) collective-permute-start(bf16[64,64,128]{2,1,0:T(8,128)(2,1)S(1)} %all-to-all-done.1.mine), channel_id=1, source_target_pairs={{0,1},{1,0},{2,3},{3,2},{4,5},{5,4},{6,7},{7,6},{8,9},{9,8},{10,11... | collective-permute-start | bytes 3145736 | tf_op jit(solution)/shard_map/ppermute | solution.py:419
  194.7 0.9 copy-start.6
  195.1 0.9 copy-start.5

commit v3 on v2

--- a/solution.py
+++ b/solution.py
@@ -14,7 +14,7 @@
 REACH = 1152
 SPANK = 5 * TOK
 ROWS = 7 * TOK
-KP = 384
+KP = REACH
 HEADS = 8
 SHARE = 5
 COUNTS = (3, 5)
@@ -43,9 +43,12 @@
 
 def attention_kernel(share, first_call, sc, query, og, lora, qup, vup, cos, sin, dst, *rest):
     kin, vin, lin = rest[0:6], rest[6:12], rest[12:18]
-    rest = rest[18:] if first_call else rest[22:]
-    att, dkm, dko, terms, liftq, lvm, lvo = rest[0:7]
-    kx, vx, kt, vt, lt, bias, ss, dp, dka, dva, qn, dn, dnt, dqn, lva = rest[7:]
+    before_q, before_v = (None, None) if first_call else rest[18:20]
+    rest = rest[18:] if first_call else rest[24:]
+    att, dkm, dko, terms, liftq, lifts = rest[0:6]
+    lvo = None if first_call else rest[6]
+    rest = rest[6:] if first_call else rest[7:]
+    kx, vx, kt, vt, lt, bias, ss, dka, dva, qn, dn, dnt, dqn, lva = rest
     g = pl.program_id(0)
     groups = pl.num_programs(0)
     wide = share * SUB
@@ -74,21 +77,25 @@
 
             @pl.when(sc[1 + chip] == 0)
             def _():
-                mine[chip] = read(pl.ds(low, TOK))
-                other[chip] = read(pl.ds(low + TOK, TOK))
+                mine[chip] = read(pl.ds(low, TOK)).astype(mine.dtype)
+                other[chip] = read(pl.ds(low + TOK, TOK)).astype(other.dtype)
 
             @pl.when(sc[1 + chip] != 0)
             def _():
-                mine[chip] = read(pl.ds(low + TOK, TOK))
-                other[chip] = read(pl.ds(low, TOK))
+                mine[chip] = read(pl.ds(low + TOK, TOK)).astype(mine.dtype)
+                other[chip] = read(pl.ds(low, TOK)).astype(other.dtype)
 
     @pl.when(g == 0)
     def _():
         for piece in (slice(0, TOK), slice(TOK + SPANK, ROWS)):
             dka[piece, :] = jnp.zeros((TOK, HD), F32)
             dva[piece, :] = jnp.zeros((TOK, HD), F32)
-        lva[...] = jnp.zeros_like(lva)
-        liftq[...] = jnp.zeros_like(liftq)
+        if first_call:
+            lva[...] = jnp.zeros_like(lva)
+            liftq[...] = jnp.zeros_like(liftq)
+        else:
+            lva[...] = before_v[...]
+            liftq[...] = before_q[...]
         place(kx, lin)
         lt[...] = kx[TOK : TOK + SPANK, :].T
         for b in range(2):
@@ -112,29 +119,24 @@
 
     def phase_a(b):
         dnt[b] = dn[b].astype(F32).T
+        query_t = qn[b].astype(F32).T.astype(BF)
         at = TOK + b * SUB
         top = None
         for piece in pieces:
-            s = mm_nt(kx[at + piece.start : at + piece.stop, :], qn[b])
-            s = s + jnp.concatenate([bias[b, piece, :]] * share, axis=1)
+            s = mm(kx[at + piece.start : at + piece.stop, :], query_t)
+            s = s * cexp + jnp.concatenate([bias[b, piece, :]] * share, axis=1)
             ss[b, piece, :] = s
             t = jnp.max(s.reshape(KP // 8, 8, wide), axis=0)
             top = t if top is None else jnp.maximum(top, t)
-        keep["top", b] = jnp.max(top, axis=0, keepdims=True) * cexp
-
-    def phase_p(b):
-        at = TOK + b * SUB
-        for piece in pieces:
-            dp[b, piece, :] = mm_nt(vx[at + piece.start : at + piece.stop, :], dn[b])
+        keep["top", b] = jnp.max(top, axis=0, keepdims=True)
 
     def phase_b(b):
         total = None
         for piece in pieces:
-            e = jnp.exp2(ss[b, piece, :] * cexp - keep["top", b])
-            ss[b, piece, :] = e
+            e = jnp.exp2(ss[b, piece, :] - keep["top", b])
             t = jnp.sum(e.reshape(KP // 8, 8, wide), axis=0)
             total = t if total is None else total + t
-        keep["inverse", b] = 1.0 / jnp.sum(total, axis=0, keepdims=True)
+        keep["norm", b] = keep["top", b] + jnp.log2(jnp.sum(total, axis=0, keepdims=True))
 
     def add(target, b, piece, value):
         rows = slice(TOK + b * SUB + piece.start, TOK + b * SUB + piece.stop)
@@ -150,7 +152,7 @@
     def phase_c(b):
         ot = None
         for piece in pieces:
-            pb = (ss[b, piece, :] * keep["inverse", b]).astype(BF)
+            pb = jnp.exp2(ss[b, piece, :] - keep["norm", b]).astype(BF)
             t = mm(vt[:, b * SUB + piece.start : b * SUB + piece.stop], pb)
             ot = t if ot is None else ot + t
             add(dva, b, piece, mm(pb, dn[b]))
@@ -162,8 +164,11 @@
 
     def phase_d(b):
         qt = None
+        grad_t = dnt[b].astype(BF)
         for piece in pieces:
-            ds = ((ss[b, piece, :] * keep["inverse", b]) * (dp[b, piece, :] - keep["dot", b])).astype(BF)
+            rows = slice(TOK + b * SUB + piece.start, TOK + b * SUB + piece.stop)
+            p = jnp.exp2(ss[b, piece, :] - keep["norm", b])
+            ds = (p * (mm(vx[rows, :], grad_t) - keep["dot", b])).astype(BF)
             t = mm(kt[:, b * SUB + piece.start : b * SUB + piece.stop], ds)
             qt = t if qt is None else qt + t
             add(dka, b, piece, mm(ds, qn[b]))
@@ -178,10 +183,8 @@
     phase_a(0)
     phase_b(0)
     phase_a(1)
-    phase_p(0)
     phase_c(0)
     phase_b(1)
-    phase_p(1)
     phase_d(0)
     phase_c(1)
     phase_d(1)
@@ -199,7 +202,10 @@
 
     @pl.when(g == groups - 1)
     def _():
-        take(lambda rows: lva[rows, :], lvm, lvo)
+        if first_call:
+            lifts[...] = lva[...]
+        else:
+            take(lambda rows: lva[rows, :], lifts, lvo)
 
 
 def prepare_kernel(normed, qdown, vdown, keys, values, vup, cos, sin, *outs):
@@ -259,8 +265,11 @@
     )(frozen, own, qup, cos, sin)
 
 
-def gradients_kernel(core, lift_q, lift_v, normed, heads, kept, given):
-    down = mm_tn(jnp.concatenate([lift_q[...], lift_v[...]], axis=1), normed[...]).astype(BF)
+def gradients_kernel(core, total_q, own, near, far, normed, heads, kept, given):
+    lift_q = (ADAPTER_SCALE * total_q[...]).astype(BF)
+    lift_v = own[...] + (near[...].astype(F32) + far[...].astype(F32))
+    lift_v = (ADAPTER_SCALE * lift_v).astype(BF)
+    down = mm_tn(jnp.concatenate([lift_q, lift_v], axis=1), normed[...]).astype(BF)
     tiles = down.shape[1] // HD
 
     def write(low, high):
@@ -280,17 +289,17 @@
         write(given, kept)
 
 
-def gradients(core, lift_q, lift_v, normed, heads):
+def gradients(core, total_q, own, near, far, normed, heads):
     vmem = pl.BlockSpec(memory_space=pltpu.VMEM)
     half = jax.ShapeDtypeStruct((EDGE // 2 + normed.shape[1] // HD, RANK, HD), BF)
     return pl.pallas_call(
         gradients_kernel,
         out_shape=[half, half],
-        in_specs=[pl.BlockSpec(memory_space=pltpu.SMEM)] + [vmem] * 4,
+        in_specs=[pl.BlockSpec(memory_space=pltpu.SMEM)] + [vmem] * 6,
         out_specs=[vmem] * 2,
         compiler_params=pltpu.CompilerParams(vmem_limit_bytes=24 * 2**20),
         name="gradients",
-    )(core, lift_q, lift_v, normed, heads)
+    )(core, total_q, own, near, far, normed, heads)
 
 
 def sum_kernel(spread, out):
@@ -348,7 +357,7 @@
     )(core, mine, other)
 
 
-def attention(scalars, query, grad, own, qup, vup, cos, sin, dst, keyed, lorad, held, first, count):
+def attention(scalars, query, grad, own, qup, vup, cos, sin, dst, keyed, lorad, held, lifts, first, count):
     share = SHARE
     wide = share * HD
     tail = 2 * COUNTS[0]
@@ -369,27 +378,35 @@
     operands = [scalars, query, grad, own, qup, vup, cos, sin, dst, *keyed, *keyed, *lorad]
     aliases = {}
     if held is not None:
+        operands += lifts
+        in_specs += [whole((TOK, RANK)), whole((ROWS, RANK))]
         aliases = {len(operands) + i: i for i in range(len(held))}
         operands += held
         in_specs += [pl.BlockSpec(memory_space=pl.ANY)] * len(held)
     pair = jax.ShapeDtypeStruct((3, TOK, HEADS * HD), BF)
-    lift = jax.ShapeDtypeStruct((3, TOK, RANK), F32)
+    lift = (3, TOK, RANK)
     out_shape = [
         jax.ShapeDtypeStruct(query.shape, BF), pair, pair, jax.ShapeDtypeStruct((EDGE, RANK, HD), BF),
-        jax.ShapeDtypeStruct((TOK, RANK), F32), lift, lift,
+        jax.ShapeDtypeStruct((TOK, RANK), F32),
     ]
+    if held is None:
+        out_shape += [jax.ShapeDtypeStruct((ROWS, RANK), F32)]
+        lift_specs = [whole((ROWS, RANK))]
+    else:
+        out_shape += [jax.ShapeDtypeStruct(lift, F32), jax.ShapeDtypeStruct(lift, BF)]
+        lift_specs = [whole(lift)] * 2
     pair_spec = pl.BlockSpec((3, TOK, HD), lambda g, s: (0, 0, g + first))
     out_specs = [
         column(TOK, wide, first), pair_spec, pair_spec,
         pl.BlockSpec((UNIT, RANK, HD), lambda g, s: (g + first, 0, 0)),
-        whole((TOK, RANK)), whole((3, TOK, RANK)), whole((3, TOK, RANK)),
+        whole((TOK, RANK)), *lift_specs,
     ]
     wide_rows = share * SUB
     scratch = [
         pltpu.VMEM((ROWS, HD), BF), pltpu.VMEM((ROWS, HD), BF),
         pltpu.VMEM((HD, SPANK), BF), pltpu.VMEM((HD, SPANK), BF), pltpu.VMEM((HD, SPANK), BF),
         pltpu.VMEM((2, REACH, SUB), F32),
-        pltpu.VMEM((2, REACH, wide_rows), F32), pltpu.VMEM((2, REACH, wide_rows), F32),
+        pltpu.VMEM((2, REACH, wide_rows), F32),
         pltpu.VMEM((ROWS, HD), F32), pltpu.VMEM((ROWS, HD), F32),
         pltpu.VMEM((2, wide_rows, HD), BF), pltpu.VMEM((2, wide_rows, HD), BF),
         pltpu.VMEM((2, HD, wide_rows), F32), pltpu.VMEM((TOK, wide), BF),
@@ -469,42 +486,40 @@
     far = [ahead(payload, 2) for payload in payloads]
     query = rotate_queries(frozen_query_output, payloads[0], query_up_factor, cos, sin)
     near[0], far[0], query = lax.optimization_barrier((near[0], far[0], query))
-    lorad = held = None
+    lorad = held = lifts = None
     first = 0
-    lift_q, lift_mine, lift_other = 0.0, 0.0, 0.0
     for place, count in enumerate(COUNTS):
         one, two = near[place], far[place]
         if held is not None:
             one, two, held[0] = lax.optimization_barrier((one, two, held[0]))
         window = [payloads[place], twins[place], one, twin(one), two, twin(two)]
         lorad = window if lorad is None else lorad
-        *held, lq, lm, lo = attention(
+        results = attention(
             scalars, query, out_grad, payloads[0], query_up_factor, value_up_factor,
-            cos, sin, reach[None, :], window, lorad, held, first, count,
+            cos, sin, reach[None, :], window, lorad, held, lifts, first, count,
         )
+        held, lifts = list(results[:4]), list(results[4:])
         first += count
-        lift_q, lift_mine, lift_other = lift_q + lq, lift_mine + lm, lift_other + lo
     attended, key_mine, key_other, heads = held
-    lift_q = (ADAPTER_SCALE * lift_q).astype(BF)
-    lifts = lift_mine + twin(lift_other.astype(BF)).astype(F32)
+    lift_q, lift_mine, lift_other = lifts
+    lifts = lift_mine + twin(lift_other).astype(F32)
     lift_near, lift_far = ahead(lifts[1].astype(BF), -1), ahead(lifts[2].astype(BF), -2)
     keyed = key_mine.astype(F32) + twin(key_other).astype(F32)
     own, one, two = keyed[0], keyed[1], keyed[2].astype(BF)
     lift_near, lift_far, own, one, two = lax.optimization_barrier((lift_near, lift_far, own, one, two))
     passed = ahead(two, -1)
-    lift_v = lifts[0] + (lift_near.astype(F32) + lift_far.astype(F32))
-    lift_v = (ADAPTER_SCALE * lift_v).astype(BF)
-    kept, given = gradients(core[None], lift_q, lift_v, normed_input, heads)
+    kept, given = gradients(core[None], lift_q, lifts[0], lift_near, lift_far, normed_input, heads)
     kept = (kept.astype(F32) + twin(given).astype(F32)).astype(BF)
     cores = [list(range(c, devices, 2)) for c in range(2)]
     spread = lax.all_to_all(kept, "ctx", 0, 0, axis_index_groups=cores, tiled=True)
     one = (one + passed.astype(F32)).astype(BF)
-    key_total = own + ahead(one, -1).astype(F32)
-    key_total = key_total.reshape(TOK, HEADS, HD)
+    last = ahead(one, -1)
+    gathered = lax.all_to_all(sum_and_copy(spread), "ctx", 0, 0, axis_index_groups=cores, tiled=True)
+    sums = finish(core[None], gathered, twin(gathered), TOK * devices, normed_input.shape[1])
+    key_total = (own + last.astype(F32)).reshape(TOK, HEADS, HD)
     swapped = jnp.concatenate([key_total[..., half:], key_total[..., :half]], axis=-1)
     key_grad = (key_total * cos[:, None, :] - swapped * sin[:, None, :]).astype(BF).reshape(TOK, HEADS * HD)
-    gathered = lax.all_to_all(sum_and_copy(spread), "ctx", 0, 0, axis_index_groups=cores, tiled=True)
-    down_q, up_q, down_v, up_v = finish(core[None], gathered, twin(gathered), TOK * devices, normed_input.shape[1])
+    down_q, up_q, down_v, up_v = sums
     return (attended, key_grad, down_q.T, up_q, down_v.T, up_v)
 
 

time: 203 us -> 199 us (0.980)
  Pallas kernels: 82.1 us -> 78.4 us
  other arithmetic: 12.5 us -> 10.3 us
  waiting for transfers between devices: 45.8 us -> 47.9 us
    pallas_call x2, Pallas kernels: 62.5 us -> 58.8 us  [attention(): pl.pallas_call(functools.partial(attention_kernel, share, held is None),...]
    convert_element_type x3 -> x0, other arithmetic: 2.09 us -> none  [the longest x1 1.14 us: on_device(): lifts = lift_mine + twin(lift_other.astype(BF)).astype(F32)]
    ppermute x18, waiting for transfers between devices: 16.3 us -> 18.3 us  [moved(): return lax.ppermute(block, 'ctx', route)]
  transfers between devices with their start and end apart: 20 -> 20, of which waited for: 10 -> 11; matrix products, arithmetic and copies ran while one was open for 6% -> 5% of each run, Pallas kernels for 17% -> 17%
where the time goes in v3:
time: 199 us; the launch traced here: 198 us
  Pallas kernels  78.4 us (39%)
  starting transfers between devices  51.9 us (26%)
  waiting for transfers between devices  47.9 us (24%)
  other arithmetic  10.3 us (5%)
  local copies, waits for them, and re-layouts  5.97 us (3%)
  between operations  3.67 us (2%)
    pallas_call x2, Pallas kernels, attention(): pl.pallas_call(functools.partial(attention_kernel, share, held is None),...  58.8 us
    ppermute x18, starting transfers between devices, moved(): return lax.ppermute(block, 'ctx', route)  32 us
    all_to_all x1, waiting for transfers between devices, on_device(): lax.all_to_all(kept, 'ctx', 0, 0, axis_index_groups=cores, tiled=True)  22.2 us
    ppermute x18, waiting for transfers between devices, moved(): return lax.ppermute(block, 'ctx', route)  18.3 us
    all_to_all x1, starting transfers between devices, on_device(): lax.all_to_all(kept, 'ctx', 0, 0, axis_index_groups=cores, tiled=True)  10.1 us
    all_to_all x1, starting transfers between devices, on_device(): lax.all_to_all(sum_and_copy(spread), 'ctx', 0, 0, axis_index_groups=cores...  9.75 us
    pallas_call x1, Pallas kernels, rotate_queries(): pl.pallas_call(rotate_kernel, out_shape=jax.ShapeDtypeStruct(frozen.shape...  7.6 us
    all_to_all x1, waiting for transfers between devices, on_device(): lax.all_to_all(sum_and_copy(spread), 'ctx', 0, 0, axis_index_groups=cores...  7.4 us
  transfers between devices with their start and end apart: 20, of which 11 were waited for; matrix products, arithmetic and copies ran while one was open for 5% of the time, Pallas kernels for 17%

profile of v3, /device:TPU:62, one launch (start us, length us, event | category | flops | bytes accessed | tf_op | source)
XLA Modules:
  0.0 198.1 jit_solution(7905416317859736946)
XLA Ops:
  0.7 1.2 dynamic_slice.3
  2.6 0.8 select_reduce_fusion.1
  3.4 0.5 fusion.3
  4.0 0.8 pad_maximum_fusion
  4.8 4.9 %prepare.1 = (bf16[256,896]{1,0:T(8,128)(2,1)}, bf16[256,1280]{1,0:T(8,128)(2,1)}) custom-call(bf16[256,5120]{1,0:T(8,128)(2,1)} %normed.3, bf16[64,5120]{1,0:T(8,128)(2,1)} %bitcast.38, bf16[64,5120]{1,0:T(8,128)(2,1)} %bitcast.39, bf16[256,1024]{1,0:T(8,128)(2,1)} %keys.1, bf16[256,1024]{1,0:T(8,128)(2,1)} %values.1, bf16[64,1024]{1,0:T(8,128)(2,1)} %vup.5, ...), custom_call_target="tpu_custom_call" | custom-call | tf_op jit(solution)/shard_map/prepare/pallas_call | solution.py:232
  9.7 3.4 %collective-permute-start = (bf16[256,896]{1,0:T(8,128)(2,1)}, bf16[256,896]{1,0:T(8,128)(2,1)S(1)}, u32[]{:S(2)}, u32[]{:S(2)}) collective-permute-start(bf16[256,896]{1,0:T(8,128)(2,1)} %get-tuple-element.38.lora.rest_0_.rest_6_.rest_12_), channel_id=1, source_target_pairs={{0,2},{1,3},{2,4},{3,5},{4,6},{5,7},{6,8},{7,9},{8,10},{9,11},{10,... | collective-permute-start | bytes 1376264 | tf_op jit(solution)/shard_map/ppermute | solution.py:436
  13.1 4.3 %collective-permute-start.1 = (bf16[256,896]{1,0:T(8,128)(2,1)}, bf16[256,896]{1,0:T(8,128)(2,1)S(1)}, u32[]{:S(2)}, u32[]{:S(2)}) collective-permute-start(bf16[256,896]{1,0:T(8,128)(2,1)} %get-tuple-element.38.lora.rest_0_.rest_6_.rest_12_), channel_id=1, source_target_pairs={{0,4},{1,5},{2,6},{3,7},{4,8},{5,9},{6,10},{7,11},{8,12},{9,13},{1... | collective-permute-start | bytes 1376264 | tf_op jit(solution)/shard_map/ppermute | solution.py:436
  17.5 3.7 %collective-permute-start.3 = (bf16[256,1280]{1,0:T(8,128)(2,1)}, bf16[256,1280]{1,0:T(8,128)(2,1)S(1)}, u32[]{:S(2)}, u32[]{:S(2)}) collective-permute-start(bf16[256,1280]{1,0:T(8,128)(2,1)} %get-tuple-element.40.rest_0_.rest_6_), channel_id=1, source_target_pairs={{0,2},{1,3},{2,4},{3,5},{4,6},{5,7},{6,8},{7,9},{8,10},{9,11},{10,... | collective-permute-start | bytes 1966088 | tf_op jit(solution)/shard_map/ppermute | solution.py:436
  21.2 3.1 %collective-permute-start.4 = (bf16[256,1280]{1,0:T(8,128)(2,1)}, bf16[256,1280]{1,0:T(8,128)(2,1)S(1)}, u32[]{:S(2)}, u32[]{:S(2)}) collective-permute-start(bf16[256,1280]{1,0:T(8,128)(2,1)} %get-tuple-element.40.rest_0_.rest_6_), channel_id=1, source_target_pairs={{0,4},{1,5},{2,6},{3,7},{4,8},{5,9},{6,10},{7,11},{8,12},{9,13},{1... | collective-permute-start | bytes 1966088 | tf_op jit(solution)/shard_map/ppermute | solution.py:436
  26.4 0.6 gather_fusion
  27.0 7.6 %rotate_queries.1.query = bf16[256,5120]{1,0:T(8,128)(2,1)} custom-call(bf16[256,5120]{1,0:T(8,128)(2,1)} %frozen.1, bf16[256,896]{1,0:T(8,128)(2,1)} %get-tuple-element.38.lora.rest_0_.rest_6_.rest_12_, bf16[64,5120]{1,0:T(8,128)(2,1)} %qup.5, f32[256,128]{1,0:T(8,128)} %get-tuple-element.81.cos, f32[256,128]{1,0:T(8,128)} %get-tuple-element.82.sin), custom_call_target="tpu_custom_call" | custom-call | tf_op jit(solution)/shard_map/rotate_queries/pallas_call | solution.py:254
  34.7 0.5 collective-permute-start.7
  35.2 0.5 subtract_subtract_fusion.dst
  35.8 0.6 pad_add_fusion.sc
  36.5 0.8 collective-permute-done.7.rest_5_.rest_11_.rest_17_
  37.3 22.8 %attention.2 = (bf16[256,5120]{1,0:T(8,128)(2,1)}, bf16[3,256,1024]{2,1,0:T(8,128)(2,1)}, bf16[3,256,1024]{2,1,0:T(8,128)(2,1)}, bf16[48,64,128]{2,1,0:T(8,128)(...) custom-call(s32[4]{0:T(128)} %pad_add_fusion.sc, bf16[256,5120]{1,0:T(8,128)(2,1)} %rotate_queries.1.query, ...), custom_call_target="tpu_custom_call" | custom-call | flops 6794772480 | bytes 2359296 | tf_op jit(solution)/shard_map/attention/pallas_call | solution.py:415
  60.2 0.4 collective-permute-start.8
  60.6 0.3 collective-permute-start.9
  60.9 1.5 collective-permute-done.8.rest_3_.rest_9_
  62.4 0.9 collective-permute-done.9.rest_5_.rest_11_
  63.3 0.9 copy-done.14
  64.2 35.9 %attention.3 = (bf16[256,5120]{1,0:T(8,128)(2,1)}, bf16[3,256,1024]{2,1,0:T(8,128)(2,1)}, bf16[3,256,1024]{2,1,0:T(8,128)(2,1)}, bf16[48,64,128]{2,1,0:T(8,128)(...) custom-call(s32[4]{0:T(128)} %pad_add_fusion.sc, ...), custom_call_target="tpu_custom_call", output_to_operand_aliasing={{0}: (29, {}), {1}: (30, {}), {2}: (31, {}), {3}: (32, {})} | custom-call | flops 11324620800 | bytes 3932160 | tf_op jit(solution)/shard_map/attention/pallas_call | solution.py:415
  100.2 0.4 collective-permute-start.13
  100.7 3.4 %collective-permute-done.10 = bf16[3,256,64]{2,1,0:T(8,128)(2,1)S(1)} collective-permute-done((bf16[3,256,64]{2,1,0:T(8,128)(2,1)}, bf16[3,256,64]{2,1,0:T(8,128)(2,1)S(1)}, u32[]{:S(2)}, u32[]{:S(2)}) %collective-permute-start.10) | collective-permute-done | bytes 98336 | tf_op jit(solution)/shard_map/ppermute | solution.py:436
  104.1 1.1 fusion.6
  105.2 4.5 %collective-permute-start.11 = (bf16[256,64]{1,0:T(8,128)(2,1)S(1)}, bf16[256,64]{1,0:T(8,128)(2,1)S(1)}, u32[]{:S(2)}, u32[]{:S(2)}) collective-permute-start(bf16[256,64]{1,0:T(8,128)(2,1)S(1)} %get-tuple-element.77), channel_id=1, source_target_pairs={{2,0},{3,1},{4,2},{5,3},{6,4},{7,5},{8,6},{9,7},{10,8},{11,9},{12,... | collective-permute-start | bytes 98312 | tf_op jit(solution)/shard_map/ppermute | solution.py:436
  109.7 5.4 %collective-permute-start.12 = (bf16[256,64]{1,0:T(8,128)(2,1)S(1)}, bf16[256,64]{1,0:T(8,128)(2,1)S(1)}, u32[]{:S(2)}, u32[]{:S(2)}) collective-permute-start(bf16[256,64]{1,0:T(8,128)(2,1)S(1)} %get-tuple-element.76), channel_id=1, source_target_pairs={{4,0},{5,1},{6,2},{7,3},{8,4},{9,5},{10,6},{11,7},{12,8},{13,9},{1... | collective-permute-start | bytes 98312 | tf_op jit(solution)/shard_map/ppermute | solution.py:436
  115.2 0.6 convert_add_fusion
  116.0 0.9 fusion.2
  117.0 3.4 %collective-permute-done.12.far = bf16[256,64]{1,0:T(8,128)(2,1)S(1)} collective-permute-done((bf16[256,64]{1,0:T(8,128)(2,1)S(1)}, bf16[256,64]{1,0:T(8,128)(2,1)S(1)}, u32[]{:S(2)}, u32[]{:S(2)}) %collective-permute-start.12) | collective-permute-done | bytes 32800 | tf_op jit(solution)/shard_map/ppermute | solution.py:436
  120.4 0.8 gradients.1
  121.3 2.6 %collective-permute-done.16 = bf16[64,64,128]{2,1,0:T(8,128)(2,1)S(1)} collective-permute-done((bf16[64,64,128]{2,1,0:T(8,128)(2,1)S(1)}, bf16[64,64,128]{2,1,0:T(8,128)(2,1)S(1)}, u32[]{:S(2)}, u32[]{:S(2)}) %collective-permute-start.16) | collective-permute-done | bytes 1048608 | tf_op jit(solution)/shard_map/ppermute | solution.py:436
  123.9 1.4 add_convert_fusion
  125.3 10.1 %all-to-all-start = ((bf16[64,64,128]{2,1,0:T(8,128)(2,1)}), bf16[64,64,128]{2,1,0:T(8,128)(2,1)S(1)}, u32[]{:S(2)}, u32[]{:S(2)}) async-start(bf16[64,64,128]{2,1,0:T(8,128)(2,1)} %add_convert_fusion), calls=%async_computation | async-start | bytes 2097152 | tf_op jit(solution)/shard_map/all_to_all | solution.py:514
  135.4 2.8 %collective-permute-start.14 = (bf16[256,1024]{1,0:T(8,128)(2,1)}, bf16[256,1024]{1,0:T(8,128)(2,1)}, u32[]{:S(2)}, u32[]{:S(2)}) collective-permute-start(bf16[256,1024]{1,0:T(8,128)(2,1)} %fusion.2), channel_id=1, source_target_pairs={{2,0},{3,1},{4,2},{5,3},{6,4},{7,5},{8,6},{9,7},{10,8},{11,9},{12,... | collective-permute-start | bytes 1572872 | tf_op jit(solution)/shard_map/ppermute | solution.py:436
  138.2 22.2 %all-to-all-done.spread = bf16[64,64,128]{2,1,0:T(8,128)(2,1)S(1)} async-done(((bf16[64,64,128]{2,1,0:T(8,128)(2,1)}), bf16[64,64,128]{2,1,0:T(8,128)(2,1)S(1)}, u32[]{:S(2)}, u32[]{:S(2)}) %all-to-all-start) | async-done | bytes 1048608 | tf_op jit(solution)/shard_map/all_to_all | solution.py:514
  160.4 1.0 copy-done.5
  161.3 2.5 %sum_and_copy.1 = bf16[64,64,128]{2,1,0:T(8,128)(2,1)} custom-call(bf16[64,64,128]{2,1,0:T(8,128)(2,1)} %copy-done.5), custom_call_target="tpu_custom_call" | custom-call | tf_op jit(solution)/shard_map/sum_and_copy/pallas_call | solution.py:316
  163.8 9.8 %all-to-all-start.1 = ((bf16[64,64,128]{2,1,0:T(8,128)(2,1)}), bf16[64,64,128]{2,1,0:T(8,128)(2,1)S(1)}, u32[]{:S(2)}, u32[]{:S(2)}) async-start(bf16[64,64,128]{2,1,0:T(8,128)(2,1)} %sum_and_copy.1), calls=%async_computation.1 | async-start | bytes 2097152 | tf_op jit(solution)/shard_map/all_to_all | solution.py:517
  173.6 2.0 %add_convert_fusion.1 = bf16[256,1024]{1,0:T(8,128)(2,1)} fusion(f32[256,1024]{1,0:T(8,128)S(1)} %get-tuple-element.58, bf16[256,1024]{1,0:T(8,128)(2,1)} %collective-permute-done.14), kind=kLoop, calls=%fused_computation.11 | loop fusion | flops 786432 | bytes 2097152 | tf_op jit(solution)/shard_map/convert_element_type | solution.py:515
  175.6 2.7 %collective-permute-start.15 = (bf16[256,1024]{1,0:T(8,128)(2,1)}, bf16[256,1024]{1,0:T(8,128)(2,1)S(1)}, u32[]{:S(2)}, u32[]{:S(2)}) collective-permute-start(bf16[256,1024]{1,0:T(8,128)(2,1)} %add_convert_fusion.1), channel_id=1, source_target_pairs={{2,0},{3,1},{4,2},{5,3},{6,4},{7,5},{8,6},{9,7},{10,8},{11,9},{12,... | collective-permute-start | bytes 1572872 | tf_op jit(solution)/shard_map/ppermute | solution.py:436
  178.3 7.4 %all-to-all-done.1.mine = bf16[64,64,128]{2,1,0:T(8,128)(2,1)S(1)} async-done(((bf16[64,64,128]{2,1,0:T(8,128)(2,1)}), bf16[64,64,128]{2,1,0:T(8,128)(2,1)S(1)}, u32[]{:S(2)}, u32[]{:S(2)}) %all-to-all-start.1) | async-done | bytes 1048608 | tf_op jit(solution)/shard_map/all_to_all | solution.py:517
  185.7 5.4 %collective-permute-done.15 = bf16[256,1024]{1,0:T(8,128)(2,1)S(1)} collective-permute-done((bf16[256,1024]{1,0:T(8,128)(2,1)}, bf16[256,1024]{1,0:T(8,128)(2,1)S(1)}, u32[]{:S(2)}, u32[]{:S(2)}) %collective-permute-start.15) | collective-permute-done | bytes 524320 | tf_op jit(solution)/shard_map/ppermute | solution.py:436
  191.6 0.3 fusion.7
  191.9 0.5 copy-done.7
  192.4 0.4 maximum_multiply_fusion
  192.9 1.3 fusion
  194.2 3.9 %finish.1 = (f32[64,5120]{1,0:T(8,128)}, f32[64,5120]{1,0:T(8,128)}, f32[64,5120]{1,0:T(8,128)}, f32[64,1024]{1,0:T(8,128)}) custom-call(s32[1]{0:T(128)} %bitcast.11.core, bf16[64,64,128]{2,1,0:T(8,128)(2,1)} %copy-done.4, bf16[64,64,128]{2,1,0:T(8,128)(2,1)} %collective-permute-done.17.other), custom_call_target="tpu_custom_call" | custom-call | tf_op jit(solution)/shard_map/finish/pallas_call | solution.py:350
  (63 shorter events, 1.6 us)
Async XLA Ops:
  4.8 21.5 %copy-start.3 = (s32[128]{0:T(128)S(1)}, s32[128]{0:T(128)}, u32[]{:S(2)}) copy-start(s32[128]{0:T(128)} %param.21) | copy-start | bytes 1540
  9.7 24.9 %collective-permute-start = (bf16[256,896]{1,0:T(8,128)(2,1)}, bf16[256,896]{1,0:T(8,128)(2,1)S(1)}, u32[]{:S(2)}, u32[]{:S(2)}) collective-permute-start(bf16[256,896]{1,0:T(8,128)(2,1)} %get-tuple-element.38.lora.rest_0_.rest_6_.rest_12_), channel_id=1, source_target_pairs={{0,2},{1,3},{2,4},{3,5},{4,6},{5,7},{6,8},{7,9},{8,10},{9,11},{10,... | collective-permute-start | bytes 1376264 | tf_op jit(solution)/shard_map/ppermute | solution.py:436
  13.1 21.5 %collective-permute-start.1 = (bf16[256,896]{1,0:T(8,128)(2,1)}, bf16[256,896]{1,0:T(8,128)(2,1)S(1)}, u32[]{:S(2)}, u32[]{:S(2)}) collective-permute-start(bf16[256,896]{1,0:T(8,128)(2,1)} %get-tuple-element.38.lora.rest_0_.rest_6_.rest_12_), channel_id=1, source_target_pairs={{0,4},{1,5},{2,6},{3,7},{4,8},{5,9},{6,10},{7,11},{8,12},{9,13},{1... | collective-permute-start | bytes 1376264 | tf_op jit(solution)/shard_map/ppermute | solution.py:436
  17.4 18.9 %collective-permute-start.5 = (bf16[256,896]{1,0:T(8,128)(2,1)}, bf16[256,896]{1,0:T(8,128)(2,1)}, u32[]{:S(2)}, u32[]{:S(2)}) collective-permute-start(bf16[256,896]{1,0:T(8,128)(2,1)} %get-tuple-element.38.lora.rest_0_.rest_6_.rest_12_), channel_id=1, source_target_pairs={{0,1},{1,0},{2,3},{3,2},{4,5},{5,4},{6,7},{7,6},{8,9},{9,8},{10,11... | collective-permute-start | bytes 1376264 | tf_op jit(solution)/shard_map/ppermute | solution.py:436
  17.5 42.7 %collective-permute-start.3 = (bf16[256,1280]{1,0:T(8,128)(2,1)}, bf16[256,1280]{1,0:T(8,128)(2,1)S(1)}, u32[]{:S(2)}, u32[]{:S(2)}) collective-permute-start(bf16[256,1280]{1,0:T(8,128)(2,1)} %get-tuple-element.40.rest_0_.rest_6_), channel_id=1, source_target_pairs={{0,2},{1,3},{2,4},{3,5},{4,6},{5,7},{6,8},{7,9},{8,10},{9,11},{10,... | collective-permute-start | bytes 1966088 | tf_op jit(solution)/shard_map/ppermute | solution.py:436
  21.2 39.0 %collective-permute-start.4 = (bf16[256,1280]{1,0:T(8,128)(2,1)}, bf16[256,1280]{1,0:T(8,128)(2,1)S(1)}, u32[]{:S(2)}, u32[]{:S(2)}) collective-permute-start(bf16[256,1280]{1,0:T(8,128)(2,1)} %get-tuple-element.40.rest_0_.rest_6_), channel_id=1, source_target_pairs={{0,4},{1,5},{2,6},{3,7},{4,8},{5,9},{6,10},{7,11},{8,12},{9,13},{1... | collective-permute-start | bytes 1966088 | tf_op jit(solution)/shard_map/ppermute | solution.py:436
  27.0 9.4 %copy-start.9 = (bf16[256,1280]{1,0:T(8,128)(2,1)S(1)}, bf16[256,1280]{1,0:T(8,128)(2,1)}, u32[]{:S(2)}) copy-start(bf16[256,1280]{1,0:T(8,128)(2,1)} %get-tuple-element.40.rest_0_.rest_6_) | copy-start | bytes 1966084
  34.6 2.7 %copy-start.15 = (bf16[256,896]{1,0:T(8,128)(2,1)}, bf16[256,896]{1,0:T(8,128)(2,1)S(1)}, u32[]{:S(2)}) copy-start(bf16[256,896]{1,0:T(8,128)(2,1)S(1)} %collective-permute-done.rest_2_.rest_8_.rest_14_) | copy-start | bytes 1376260
  34.6 2.7 %copy-start.16 = (bf16[256,896]{1,0:T(8,128)(2,1)}, bf16[256,896]{1,0:T(8,128)(2,1)S(1)}, u32[]{:S(2)}) copy-start(bf16[256,896]{1,0:T(8,128)(2,1)S(1)} %collective-permute-done.1.rest_4_.rest_10_.rest_16_) | copy-start | bytes 1376260
  34.6 1.9 collective-permute-start.6
  34.7 2.6 %collective-permute-start.7 = (bf16[256,896]{1,0:T(8,128)(2,1)S(1)}, bf16[256,896]{1,0:T(8,128)(2,1)}, u32[]{:S(2)}, u32[]{:S(2)}) collective-permute-start(bf16[256,896]{1,0:T(8,128)(2,1)S(1)} %collective-permute-done.1.rest_4_.rest_10_.rest_16_), channel_id=1, source_target_pairs={{0,1},{1,0},{2,3},{3,2},{4,5},{5,4},{6,7},{7,6},{8,9},{9,8},{10,11... | collective-permute-start | bytes 1376264 | tf_op jit(solution)/shard_map/ppermute | solution.py:436
  36.4 24.5 %collective-permute-start.2 = (bf16[256,1280]{1,0:T(8,128)(2,1)S(1)}, bf16[256,1280]{1,0:T(8,128)(2,1)S(1)}, u32[]{:S(2)}, u32[]{:S(2)}) collective-permute-start(bf16[256,1280]{1,0:T(8,128)(2,1)S(1)} %copy-done.9), channel_id=1, source_target_pairs={{0,1},{1,0},{2,3},{3,2},{4,5},{5,4},{6,7},{7,6},{8,9},{9,8},{10,11... | collective-permute-start | bytes 1966088 | tf_op jit(solution)/shard_map/ppermute | solution.py:436
  36.5 0.8 copy-start.17
  60.2 4.0 %copy-start.10 = (bf16[256,1280]{1,0:T(8,128)(2,1)}, bf16[256,1280]{1,0:T(8,128)(2,1)S(1)}, u32[]{:S(2)}) copy-start(bf16[256,1280]{1,0:T(8,128)(2,1)S(1)} %collective-permute-done.3.rest_2_.rest_8_) | copy-start | bytes 1966084
  60.2 4.0 %copy-start.11 = (bf16[256,1280]{1,0:T(8,128)(2,1)}, bf16[256,1280]{1,0:T(8,128)(2,1)S(1)}, u32[]{:S(2)}) copy-start(bf16[256,1280]{1,0:T(8,128)(2,1)S(1)} %collective-permute-done.4.rest_4_.rest_10_) | copy-start | bytes 1966084
  60.2 2.2 %collective-permute-start.8 = (bf16[256,1280]{1,0:T(8,128)(2,1)S(1)}, bf16[256,1280]{1,0:T(8,128)(2,1)S(1)}, u32[]{:S(2)}, u32[]{:S(2)}) collective-permute-start(bf16[256,1280]{1,0:T(8,128)(2,1)S(1)} %collective-permute-done.3.rest_2_.rest_8_), channel_id=1, source_target_pairs={{0,1},{1,0},{2,3},{3,2},{4,5},{5,4},{6,7},{7,6},{8,9},{9,8},{10,11... | collective-permute-start | bytes 1966088 | tf_op jit(solution)/shard_map/ppermute | solution.py:436
  60.6 2.7 %collective-permute-start.9 = (bf16[256,1280]{1,0:T(8,128)(2,1)S(1)}, bf16[256,1280]{1,0:T(8,128)(2,1)S(1)}, u32[]{:S(2)}, u32[]{:S(2)}) collective-permute-start(bf16[256,1280]{1,0:T(8,128)(2,1)S(1)} %collective-permute-done.4.rest_4_.rest_10_), channel_id=1, source_target_pairs={{0,1},{1,0},{2,3},{3,2},{4,5},{5,4},{6,7},{7,6},{8,9},{9,8},{10,11... | collective-permute-start | bytes 1966088 | tf_op jit(solution)/shard_map/ppermute | solution.py:436
  60.9 3.3 %copy-start.12 = (bf16[256,1280]{1,0:T(8,128)(2,1)}, bf16[256,1280]{1,0:T(8,128)(2,1)S(1)}, u32[]{:S(2)}) copy-start(bf16[256,1280]{1,0:T(8,128)(2,1)S(1)} %collective-permute-done.2.rest_1_.rest_7_) | copy-start | bytes 1966084
  62.4 1.8 copy-start.13
  63.3 0.9 copy-start.14
  100.1 15.0 %copy-start.8 = (bf16[3,256,1024]{2,1,0:T(8,128)(2,1)S(1)}, bf16[3,256,1024]{2,1,0:T(8,128)(2,1)}, u32[]{:S(2)}) copy-start(bf16[3,256,1024]{2,1,0:T(8,128)(2,1)} %get-tuple-element.55) | copy-start | bytes 4718596
  100.2 15.0 %collective-permute-start.13 = (bf16[3,256,1024]{2,1,0:T(8,128)(2,1)}, bf16[3,256,1024]{2,1,0:T(8,128)(2,1)S(1)}, u32[]{:S(2)}, u32[]{:S(2)}) collective-permute-start(bf16[3,256,1024]{2,1,0:T(8,128)(2,1)} %get-tuple-element.56), channel_id=1, source_target_pairs={{0,1},{1,0},{2,3},{3,2},{4,5},{5,4},{6,7},{7,6},{8,9},{9,8},{10,11... | collective-permute-start | bytes 4718600 | tf_op jit(solution)/shard_map/ppermute | solution.py:436
  100.6 3.6 %collective-permute-start.10 = (bf16[3,256,64]{2,1,0:T(8,128)(2,1)}, bf16[3,256,64]{2,1,0:T(8,128)(2,1)S(1)}, u32[]{:S(2)}, u32[]{:S(2)}) collective-permute-start(bf16[3,256,64]{2,1,0:T(8,128)(2,1)} %get-tuple-element.54), channel_id=1, source_target_pairs={{0,1},{1,0},{2,3},{3,2},{4,5},{5,4},{6,7},{7,6},{8,9},{9,8},{10,11... | collective-permute-start | bytes 294920 | tf_op jit(solution)/shard_map/ppermute | solution.py:436
  105.2 11.7 %collective-permute-start.11 = (bf16[256,64]{1,0:T(8,128)(2,1)S(1)}, bf16[256,64]{1,0:T(8,128)(2,1)S(1)}, u32[]{:S(2)}, u32[]{:S(2)}) collective-permute-start(bf16[256,64]{1,0:T(8,128)(2,1)S(1)} %get-tuple-element.77), channel_id=1, source_target_pairs={{2,0},{3,1},{4,2},{5,3},{6,4},{7,5},{8,6},{9,7},{10,8},{11,9},{12,... | collective-permute-start | bytes 98312 | tf_op jit(solution)/shard_map/ppermute | solution.py:436
  109.7 10.7 %collective-permute-start.12 = (bf16[256,64]{1,0:T(8,128)(2,1)S(1)}, bf16[256,64]{1,0:T(8,128)(2,1)S(1)}, u32[]{:S(2)}, u32[]{:S(2)}) collective-permute-start(bf16[256,64]{1,0:T(8,128)(2,1)S(1)} %get-tuple-element.76), channel_id=1, source_target_pairs={{4,0},{5,1},{6,2},{7,3},{8,4},{9,5},{10,6},{11,7},{12,8},{13,9},{1... | collective-permute-start | bytes 98312 | tf_op jit(solution)/shard_map/ppermute | solution.py:436
  115.8 4.6 %copy-start = (bf16[256,5120]{1,0:T(8,128)(2,1)S(1)}, bf16[256,5120]{1,0:T(8,128)(2,1)}, u32[]{:S(2)}) copy-start(bf16[256,5120]{1,0:T(8,128)(2,1)} %normed.3) | copy-start | bytes 7864324
  115.8 4.6 %copy-start.1 = (bf16[48,64,128]{2,1,0:T(8,128)(2,1)S(1)}, bf16[48,64,128]{2,1,0:T(8,128)(2,1)}, u32[]{:S(2)}) copy-start(bf16[48,64,128]{2,1,0:T(8,128)(2,1)} %get-tuple-element.63.heads) | copy-start | bytes 2359300
  115.8 4.6 %copy-start.2 = (f32[256,64]{1,0:T(8,128)S(1)}, f32[256,64]{1,0:T(8,128)}, u32[]{:S(2)}) copy-start(f32[256,64]{1,0:T(8,128)} %get-tuple-element.60.total_q) | copy-start | bytes 196612
  121.2 2.7 %collective-permute-start.16 = (bf16[64,64,128]{2,1,0:T(8,128)(2,1)S(1)}, bf16[64,64,128]{2,1,0:T(8,128)(2,1)S(1)}, u32[]{:S(2)}, u32[]{:S(2)}) collective-permute-start(bf16[64,64,128]{2,1,0:T(8,128)(2,1)S(1)} %get-tuple-element.65), channel_id=1, source_target_pairs={{0,1},{1,0},{2,3},{3,2},{4,5},{5,4},{6,7},{7,6},{8,9},{9,8},{10,11... | collective-permute-start | bytes 3145736 | tf_op jit(solution)/shard_map/ppermute | solution.py:436
  125.3 35.1 %all-to-all-start = ((bf16[64,64,128]{2,1,0:T(8,128)(2,1)}), bf16[64,64,128]{2,1,0:T(8,128)(2,1)S(1)}, u32[]{:S(2)}, u32[]{:S(2)}) async-start(bf16[64,64,128]{2,1,0:T(8,128)(2,1)} %add_convert_fusion), calls=%async_computation | async-start | bytes 2097152 | tf_op jit(solution)/shard_map/all_to_all | solution.py:514
  135.4 38.1 %collective-permute-start.14 = (bf16[256,1024]{1,0:T(8,128)(2,1)}, bf16[256,1024]{1,0:T(8,128)(2,1)}, u32[]{:S(2)}, u32[]{:S(2)}) collective-permute-start(bf16[256,1024]{1,0:T(8,128)(2,1)} %fusion.2), channel_id=1, source_target_pairs={{2,0},{3,1},{4,2},{5,3},{6,4},{7,5},{8,6},{9,7},{10,8},{11,9},{12,... | collective-permute-start | bytes 1572872 | tf_op jit(solution)/shard_map/ppermute | solution.py:436
  160.4 1.0 copy-start.5
  163.8 21.9 %all-to-all-start.1 = ((bf16[64,64,128]{2,1,0:T(8,128)(2,1)}), bf16[64,64,128]{2,1,0:T(8,128)(2,1)S(1)}, u32[]{:S(2)}, u32[]{:S(2)}) async-start(bf16[64,64,128]{2,1,0:T(8,128)(2,1)} %sum_and_copy.1), calls=%async_computation.1 | async-start | bytes 2097152 | tf_op jit(solution)/shard_map/all_to_all | solution.py:517
  175.6 15.6 %collective-permute-start.15 = (bf16[256,1024]{1,0:T(8,128)(2,1)}, bf16[256,1024]{1,0:T(8,128)(2,1)S(1)}, u32[]{:S(2)}, u32[]{:S(2)}) collective-permute-start(bf16[256,1024]{1,0:T(8,128)(2,1)} %add_convert_fusion.1), channel_id=1, source_target_pairs={{2,0},{3,1},{4,2},{5,3},{6,4},{7,5},{8,6},{9,7},{10,8},{11,9},{12,... | collective-permute-start | bytes 1572872 | tf_op jit(solution)/shard_map/ppermute | solution.py:436
  185.7 5.8 %copy-start.4 = (bf16[64,64,128]{2,1,0:T(8,128)(2,1)}, bf16[64,64,128]{2,1,0:T(8,128)(2,1)S(1)}, u32[]{:S(2)}) copy-start(bf16[64,64,128]{2,1,0:T(8,128)(2,1)S(1)} %all-to-all-done.1.mine) | copy-start | bytes 3145732
  185.7 8.5 %collective-permute-start.17 = (bf16[64,64,128]{2,1,0:T(8,128)(2,1)S(1)}, bf16[64,64,128]{2,1,0:T(8,128)(2,1)}, u32[]{:S(2)}, u32[]{:S(2)}) collective-permute-start(bf16[64,64,128]{2,1,0:T(8,128)(2,1)S(1)} %all-to-all-done.1.mine), channel_id=1, source_target_pairs={{0,1},{1,0},{2,3},{3,2},{4,5},{5,4},{6,7},{7,6},{8,9},{9,8},{10,11... | collective-permute-start | bytes 3145736 | tf_op jit(solution)/shard_map/ppermute | solution.py:436
  191.5 0.9 copy-start.7
  191.9 0.9 copy-start.6

commit v4 on v3

--- a/solution.py
+++ b/solution.py
@@ -502,21 +502,22 @@
         first += count
     attended, key_mine, key_other, heads = held
     lift_q, lift_mine, lift_other = lifts
-    lifts = lift_mine + twin(lift_other).astype(F32)
+    lift_twin, key_other = lax.optimization_barrier((twin(lift_other), key_other))
+    lifts = lift_mine + lift_twin.astype(F32)
     lift_near, lift_far = ahead(lifts[1].astype(BF), -1), ahead(lifts[2].astype(BF), -2)
     keyed = key_mine.astype(F32) + twin(key_other).astype(F32)
-    own, one, two = keyed[0], keyed[1], keyed[2].astype(BF)
+    own, one, two = keyed[0], keyed[1].astype(BF), keyed[2].astype(BF)
     lift_near, lift_far, own, one, two = lax.optimization_barrier((lift_near, lift_far, own, one, two))
-    passed = ahead(two, -1)
+    key_near = ahead(one, -1)
     kept, given = gradients(core[None], lift_q, lifts[0], lift_near, lift_far, normed_input, heads)
     kept = (kept.astype(F32) + twin(given).astype(F32)).astype(BF)
     cores = [list(range(c, devices, 2)) for c in range(2)]
     spread = lax.all_to_all(kept, "ctx", 0, 0, axis_index_groups=cores, tiled=True)
-    one = (one + passed.astype(F32)).astype(BF)
-    last = ahead(one, -1)
+    key_near, two = lax.optimization_barrier((key_near, two))
+    key_far = ahead(two, -2)
     gathered = lax.all_to_all(sum_and_copy(spread), "ctx", 0, 0, axis_index_groups=cores, tiled=True)
     sums = finish(core[None], gathered, twin(gathered), TOK * devices, normed_input.shape[1])
-    key_total = (own + last.astype(F32)).reshape(TOK, HEADS, HD)
+    key_total = (own + (key_near.astype(F32) + key_far.astype(F32))).reshape(TOK, HEADS, HD)
     swapped = jnp.concatenate([key_total[..., half:], key_total[..., :half]], axis=-1)
     key_grad = (key_total * cos[:, None, :] - swapped * sin[:, None, :]).astype(BF).reshape(TOK, HEADS * HD)
     down_q, up_q, down_v, up_v = sums

time: 199 us -> 196 us (0.985)
  waiting for transfers between devices: 47.9 us -> 45.4 us
    ppermute x18, waiting for transfers between devices: 18.3 us -> 15.9 us  [moved(): return lax.ppermute(block, 'ctx', route)]
  transfers between devices with their start and end apart: 20 -> 20, of which waited for: 11 -> 10; matrix products, arithmetic and copies ran while one was open for 5% -> 4% of each run, Pallas kernels for 17% -> 17%
where the time goes in v4:
time: 196 us; the launch traced here: 195 us
  Pallas kernels  78.4 us (40%)
  starting transfers between devices  52.6 us (27%)
  waiting for transfers between devices  45.4 us (23%)
  other arithmetic  8.75 us (4%)
  local copies, waits for them, and re-layouts  5.9 us (3%)
  between operations  3.67 us (2%)
    pallas_call x2, Pallas kernels, attention(): pl.pallas_call(functools.partial(attention_kernel, share, held is None),...  58.7 us
    ppermute x18, starting transfers between devices, moved(): return lax.ppermute(block, 'ctx', route)  32.7 us
    all_to_all x1, waiting for transfers between devices, on_device(): lax.all_to_all(kept, 'ctx', 0, 0, axis_index_groups=cores, tiled=True)  22.2 us
    ppermute x18, waiting for transfers between devices, moved(): return lax.ppermute(block, 'ctx', route)  15.9 us
    all_to_all x1, starting transfers between devices, on_device(): lax.all_to_all(kept, 'ctx', 0, 0, axis_index_groups=cores, tiled=True)  10.1 us
    all_to_all x1, starting transfers between devices, on_device(): lax.all_to_all(sum_and_copy(spread), 'ctx', 0, 0, axis_index_groups=cores...  9.75 us
    pallas_call x1, Pallas kernels, rotate_queries(): pl.pallas_call(rotate_kernel, out_shape=jax.ShapeDtypeStruct(frozen.shape...  7.58 us
    all_to_all x1, waiting for transfers between devices, on_device(): lax.all_to_all(sum_and_copy(spread), 'ctx', 0, 0, axis_index_groups=cores...  7.32 us
  transfers between devices with their start and end apart: 20, of which 10 were waited for; matrix products, arithmetic and copies ran while one was open for 4% of the time, Pallas kernels for 17%

profile of v4, /device:TPU:62, one launch (start us, length us, event | category | flops | bytes accessed | tf_op | source)
XLA Modules:
  0.0 194.7 jit_solution(12267538438119963712)
XLA Ops:
  0.7 1.2 dynamic_slice.3
  2.6 0.8 select_reduce_fusion.1
  3.4 0.5 fusion.2
  4.0 0.9 pad_maximum_fusion
  4.8 4.9 %prepare.1 = (bf16[256,896]{1,0:T(8,128)(2,1)}, bf16[256,1280]{1,0:T(8,128)(2,1)}) custom-call(bf16[256,5120]{1,0:T(8,128)(2,1)} %normed.3, bf16[64,5120]{1,0:T(8,128)(2,1)} %bitcast.38, bf16[64,5120]{1,0:T(8,128)(2,1)} %bitcast.39, bf16[256,1024]{1,0:T(8,128)(2,1)} %keys.1, bf16[256,1024]{1,0:T(8,128)(2,1)} %values.1, bf16[64,1024]{1,0:T(8,128)(2,1)} %vup.5, ...), custom_call_target="tpu_custom_call" | custom-call | tf_op jit(solution)/shard_map/prepare/pallas_call | solution.py:232
  9.7 3.4 %collective-permute-start = (bf16[256,896]{1,0:T(8,128)(2,1)}, bf16[256,896]{1,0:T(8,128)(2,1)S(1)}, u32[]{:S(2)}, u32[]{:S(2)}) collective-permute-start(bf16[256,896]{1,0:T(8,128)(2,1)} %get-tuple-element.42.lora.rest_0_.rest_6_.rest_12_), channel_id=1, source_target_pairs={{0,2},{1,3},{2,4},{3,5},{4,6},{5,7},{6,8},{7,9},{8,10},{9,11},{10,... | collective-permute-start | bytes 1376264 | tf_op jit(solution)/shard_map/ppermute | solution.py:436
  13.1 4.3 %collective-permute-start.1 = (bf16[256,896]{1,0:T(8,128)(2,1)}, bf16[256,896]{1,0:T(8,128)(2,1)S(1)}, u32[]{:S(2)}, u32[]{:S(2)}) collective-permute-start(bf16[256,896]{1,0:T(8,128)(2,1)} %get-tuple-element.42.lora.rest_0_.rest_6_.rest_12_), channel_id=1, source_target_pairs={{0,4},{1,5},{2,6},{3,7},{4,8},{5,9},{6,10},{7,11},{8,12},{9,13},{1... | collective-permute-start | bytes 1376264 | tf_op jit(solution)/shard_map/ppermute | solution.py:436
  17.5 3.7 %collective-permute-start.3 = (bf16[256,1280]{1,0:T(8,128)(2,1)}, bf16[256,1280]{1,0:T(8,128)(2,1)S(1)}, u32[]{:S(2)}, u32[]{:S(2)}) collective-permute-start(bf16[256,1280]{1,0:T(8,128)(2,1)} %get-tuple-element.44.rest_0_.rest_6_), channel_id=1, source_target_pairs={{0,2},{1,3},{2,4},{3,5},{4,6},{5,7},{6,8},{7,9},{8,10},{9,11},{10,... | collective-permute-start | bytes 1966088 | tf_op jit(solution)/shard_map/ppermute | solution.py:436
  21.2 3.1 %collective-permute-start.4 = (bf16[256,1280]{1,0:T(8,128)(2,1)}, bf16[256,1280]{1,0:T(8,128)(2,1)S(1)}, u32[]{:S(2)}, u32[]{:S(2)}) collective-permute-start(bf16[256,1280]{1,0:T(8,128)(2,1)} %get-tuple-element.44.rest_0_.rest_6_), channel_id=1, source_target_pairs={{0,4},{1,5},{2,6},{3,7},{4,8},{5,9},{6,10},{7,11},{8,12},{9,13},{1... | collective-permute-start | bytes 1966088 | tf_op jit(solution)/shard_map/ppermute | solution.py:436
  26.4 0.6 gather_fusion
  27.0 7.6 %rotate_queries.1.query = bf16[256,5120]{1,0:T(8,128)(2,1)} custom-call(bf16[256,5120]{1,0:T(8,128)(2,1)} %frozen.1, bf16[256,896]{1,0:T(8,128)(2,1)} %get-tuple-element.42.lora.rest_0_.rest_6_.rest_12_, bf16[64,5120]{1,0:T(8,128)(2,1)} %qup.5, f32[256,128]{1,0:T(8,128)} %get-tuple-element.91.cos, f32[256,128]{1,0:T(8,128)} %get-tuple-element.92.sin), custom_call_target="tpu_custom_call" | custom-call | tf_op jit(solution)/shard_map/rotate_queries/pallas_call | solution.py:254
  34.7 0.5 collective-permute-start.7
  35.2 0.5 subtract_subtract_fusion.dst
  35.8 0.7 pad_add_fusion.sc
  36.5 0.8 collective-permute-done.7.rest_5_.rest_11_.rest_17_
  37.3 22.8 %attention.2 = (bf16[256,5120]{1,0:T(8,128)(2,1)}, bf16[3,256,1024]{2,1,0:T(8,128)(2,1)}, bf16[3,256,1024]{2,1,0:T(8,128)(2,1)}, bf16[48,64,128]{2,1,0:T(8,128)(...) custom-call(s32[4]{0:T(128)} %pad_add_fusion.sc, bf16[256,5120]{1,0:T(8,128)(2,1)} %rotate_queries.1.query, ...), custom_call_target="tpu_custom_call" | custom-call | flops 6794772480 | bytes 2359296 | tf_op jit(solution)/shard_map/attention/pallas_call | solution.py:415
  60.2 0.4 collective-permute-start.8
  60.6 0.3 collective-permute-start.9
  60.9 1.5 collective-permute-done.8.rest_3_.rest_9_
  62.4 0.9 collective-permute-done.9.rest_5_.rest_11_
  63.3 0.9 copy-done.14
  64.2 35.9 %attention.3 = (bf16[256,5120]{1,0:T(8,128)(2,1)}, bf16[3,256,1024]{2,1,0:T(8,128)(2,1)}, bf16[3,256,1024]{2,1,0:T(8,128)(2,1)}, bf16[48,64,128]{2,1,0:T(8,128)(...) custom-call(s32[4]{0:T(128)} %pad_add_fusion.sc, ...), custom_call_target="tpu_custom_call", output_to_operand_aliasing={{0}: (29, {}), {1}: (30, {}), {2}: (31, {}), {3}: (32, {})} | custom-call | flops 11324620800 | bytes 3932160 | tf_op jit(solution)/shard_map/attention/pallas_call | solution.py:415
  100.1 0.5 collective-permute-start.10
  100.6 1.3 collective-permute-done.10
  101.9 0.4 collective-permute-start.13
  102.3 1.1 fusion.6
  103.3 4.2 %collective-permute-start.11 = (bf16[256,64]{1,0:T(8,128)(2,1)S(1)}, bf16[256,64]{1,0:T(8,128)(2,1)S(1)}, u32[]{:S(2)}, u32[]{:S(2)}) collective-permute-start(bf16[256,64]{1,0:T(8,128)(2,1)S(1)} %get-tuple-element.87), channel_id=1, source_target_pairs={{2,0},{3,1},{4,2},{5,3},{6,4},{7,5},{8,6},{9,7},{10,8},{11,9},{12,... | collective-permute-start | bytes 98312 | tf_op jit(solution)/shard_map/ppermute | solution.py:436
  107.6 5.4 %collective-permute-start.12 = (bf16[256,64]{1,0:T(8,128)(2,1)S(1)}, bf16[256,64]{1,0:T(8,128)(2,1)S(1)}, u32[]{:S(2)}, u32[]{:S(2)}) collective-permute-start(bf16[256,64]{1,0:T(8,128)(2,1)S(1)} %get-tuple-element.86), channel_id=1, source_target_pairs={{4,0},{5,1},{6,2},{7,3},{8,4},{9,5},{10,6},{11,7},{12,8},{13,9},{1... | collective-permute-start | bytes 98312 | tf_op jit(solution)/shard_map/ppermute | solution.py:436
  113.0 0.8 fusion.5
  114.0 0.9 slice_bitcast_fusion.1
  115.1 3.2 %collective-permute-done.12.far = bf16[256,64]{1,0:T(8,128)(2,1)S(1)} collective-permute-done((bf16[256,64]{1,0:T(8,128)(2,1)S(1)}, bf16[256,64]{1,0:T(8,128)(2,1)S(1)}, u32[]{:S(2)}, u32[]{:S(2)}) %collective-permute-start.12) | collective-permute-done | bytes 32800 | tf_op jit(solution)/shard_map/ppermute | solution.py:436
  118.3 0.8 gradients.1
  119.2 2.6 %collective-permute-done.16 = bf16[64,64,128]{2,1,0:T(8,128)(2,1)S(1)} collective-permute-done((bf16[64,64,128]{2,1,0:T(8,128)(2,1)S(1)}, bf16[64,64,128]{2,1,0:T(8,128)(2,1)S(1)}, u32[]{:S(2)}, u32[]{:S(2)}) %collective-permute-start.16) | collective-permute-done | bytes 1048608 | tf_op jit(solution)/shard_map/ppermute | solution.py:436
  121.8 1.4 add_convert_fusion
  123.2 10.1 %all-to-all-start = ((bf16[64,64,128]{2,1,0:T(8,128)(2,1)}), bf16[64,64,128]{2,1,0:T(8,128)(2,1)S(1)}, u32[]{:S(2)}, u32[]{:S(2)}) async-start(bf16[64,64,128]{2,1,0:T(8,128)(2,1)} %add_convert_fusion), calls=%async_computation | async-start | bytes 2097152 | tf_op jit(solution)/shard_map/all_to_all | solution.py:515
  133.4 2.8 %collective-permute-start.14 = (bf16[256,1024]{1,0:T(8,128)(2,1)S(1)}, bf16[256,1024]{1,0:T(8,128)(2,1)S(1)}, u32[]{:S(2)}, u32[]{:S(2)}) collective-permute-start(bf16[256,1024]{1,0:T(8,128)(2,1)S(1)} %get-tuple-element.64), channel_id=1, source_target_pairs={{2,0},{3,1},{4,2},{5,3},{6,4},{7,5},{8,6},{9,7},{10,8},{11,9},{12,... | collective-permute-start | bytes 1572872 | tf_op jit(solution)/shard_map/ppermute | solution.py:436
  136.1 22.2 %all-to-all-done.spread = bf16[64,64,128]{2,1,0:T(8,128)(2,1)S(1)} async-done(((bf16[64,64,128]{2,1,0:T(8,128)(2,1)}), bf16[64,64,128]{2,1,0:T(8,128)(2,1)S(1)}, u32[]{:S(2)}, u32[]{:S(2)}) %all-to-all-start) | async-done | bytes 1048608 | tf_op jit(solution)/shard_map/all_to_all | solution.py:515
  158.3 1.0 copy-done.5
  159.3 2.5 %sum_and_copy.1 = bf16[64,64,128]{2,1,0:T(8,128)(2,1)} custom-call(bf16[64,64,128]{2,1,0:T(8,128)(2,1)} %copy-done.5), custom_call_target="tpu_custom_call" | custom-call | tf_op jit(solution)/shard_map/sum_and_copy/pallas_call | solution.py:316
  161.7 9.8 %all-to-all-start.1 = ((bf16[64,64,128]{2,1,0:T(8,128)(2,1)}), bf16[64,64,128]{2,1,0:T(8,128)(2,1)S(1)}, u32[]{:S(2)}, u32[]{:S(2)}) async-start(bf16[64,64,128]{2,1,0:T(8,128)(2,1)} %sum_and_copy.1), calls=%async_computation.1 | async-start | bytes 2097152 | tf_op jit(solution)/shard_map/all_to_all | solution.py:518
  171.5 3.4 %collective-permute-start.15 = (bf16[256,1024]{1,0:T(8,128)(2,1)}, bf16[256,1024]{1,0:T(8,128)(2,1)S(1)}, u32[]{:S(2)}, u32[]{:S(2)}) collective-permute-start(bf16[256,1024]{1,0:T(8,128)(2,1)} %get-tuple-element.67), channel_id=1, source_target_pairs={{4,0},{5,1},{6,2},{7,3},{8,4},{9,5},{10,6},{11,7},{12,8},{13,9},{1... | collective-permute-start | bytes 1572872 | tf_op jit(solution)/shard_map/ppermute | solution.py:436
  174.9 7.3 %all-to-all-done.1.mine = bf16[64,64,128]{2,1,0:T(8,128)(2,1)S(1)} async-done(((bf16[64,64,128]{2,1,0:T(8,128)(2,1)}), bf16[64,64,128]{2,1,0:T(8,128)(2,1)S(1)}, u32[]{:S(2)}, u32[]{:S(2)}) %all-to-all-start.1) | async-done | bytes 1048608 | tf_op jit(solution)/shard_map/all_to_all | solution.py:518
  182.2 5.3 %collective-permute-done.15 = bf16[256,1024]{1,0:T(8,128)(2,1)S(1)} collective-permute-done((bf16[256,1024]{1,0:T(8,128)(2,1)}, bf16[256,1024]{1,0:T(8,128)(2,1)S(1)}, u32[]{:S(2)}, u32[]{:S(2)}) %collective-permute-start.15) | collective-permute-done | bytes 524320 | tf_op jit(solution)/shard_map/ppermute | solution.py:436
  188.0 0.3 fusion.7
  188.3 0.5 copy-done.7
  188.9 0.4 maximum_multiply_fusion
  189.3 1.5 fusion
  190.8 3.9 %finish.1 = (f32[64,5120]{1,0:T(8,128)}, f32[64,5120]{1,0:T(8,128)}, f32[64,5120]{1,0:T(8,128)}, f32[64,1024]{1,0:T(8,128)}) custom-call(s32[1]{0:T(128)} %bitcast.11.core, bf16[64,64,128]{2,1,0:T(8,128)(2,1)} %copy-done.4, bf16[64,64,128]{2,1,0:T(8,128)(2,1)} %collective-permute-done.17.other), custom_call_target="tpu_custom_call" | custom-call | tf_op jit(solution)/shard_map/finish/pallas_call | solution.py:350
  (62 shorter events, 1.4 us)
Async XLA Ops:
  4.8 21.5 %copy-start.3 = (s32[128]{0:T(128)S(1)}, s32[128]{0:T(128)}, u32[]{:S(2)}) copy-start(s32[128]{0:T(128)} %param.21) | copy-start | bytes 1540
  9.7 24.9 %collective-permute-start = (bf16[256,896]{1,0:T(8,128)(2,1)}, bf16[256,896]{1,0:T(8,128)(2,1)S(1)}, u32[]{:S(2)}, u32[]{:S(2)}) collective-permute-start(bf16[256,896]{1,0:T(8,128)(2,1)} %get-tuple-element.42.lora.rest_0_.rest_6_.rest_12_), channel_id=1, source_target_pairs={{0,2},{1,3},{2,4},{3,5},{4,6},{5,7},{6,8},{7,9},{8,10},{9,11},{10,... | collective-permute-start | bytes 1376264 | tf_op jit(solution)/shard_map/ppermute | solution.py:436
  13.1 21.5 %collective-permute-start.1 = (bf16[256,896]{1,0:T(8,128)(2,1)}, bf16[256,896]{1,0:T(8,128)(2,1)S(1)}, u32[]{:S(2)}, u32[]{:S(2)}) collective-permute-start(bf16[256,896]{1,0:T(8,128)(2,1)} %get-tuple-element.42.lora.rest_0_.rest_6_.rest_12_), channel_id=1, source_target_pairs={{0,4},{1,5},{2,6},{3,7},{4,8},{5,9},{6,10},{7,11},{8,12},{9,13},{1... | collective-permute-start | bytes 1376264 | tf_op jit(solution)/shard_map/ppermute | solution.py:436
  17.4 19.0 %collective-permute-start.5 = (bf16[256,896]{1,0:T(8,128)(2,1)}, bf16[256,896]{1,0:T(8,128)(2,1)}, u32[]{:S(2)}, u32[]{:S(2)}) collective-permute-start(bf16[256,896]{1,0:T(8,128)(2,1)} %get-tuple-element.42.lora.rest_0_.rest_6_.rest_12_), channel_id=1, source_target_pairs={{0,1},{1,0},{2,3},{3,2},{4,5},{5,4},{6,7},{7,6},{8,9},{9,8},{10,11... | collective-permute-start | bytes 1376264 | tf_op jit(solution)/shard_map/ppermute | solution.py:436
  17.5 42.6 %collective-permute-start.3 = (bf16[256,1280]{1,0:T(8,128)(2,1)}, bf16[256,1280]{1,0:T(8,128)(2,1)S(1)}, u32[]{:S(2)}, u32[]{:S(2)}) collective-permute-start(bf16[256,1280]{1,0:T(8,128)(2,1)} %get-tuple-element.44.rest_0_.rest_6_), channel_id=1, source_target_pairs={{0,2},{1,3},{2,4},{3,5},{4,6},{5,7},{6,8},{7,9},{8,10},{9,11},{10,... | collective-permute-start | bytes 1966088 | tf_op jit(solution)/shard_map/ppermute | solution.py:436
  21.2 38.9 %collective-permute-start.4 = (bf16[256,1280]{1,0:T(8,128)(2,1)}, bf16[256,1280]{1,0:T(8,128)(2,1)S(1)}, u32[]{:S(2)}, u32[]{:S(2)}) collective-permute-start(bf16[256,1280]{1,0:T(8,128)(2,1)} %get-tuple-element.44.rest_0_.rest_6_), channel_id=1, source_target_pairs={{0,4},{1,5},{2,6},{3,7},{4,8},{5,9},{6,10},{7,11},{8,12},{9,13},{1... | collective-permute-start | bytes 1966088 | tf_op jit(solution)/shard_map/ppermute | solution.py:436
  27.0 9.4 %copy-start.9 = (bf16[256,1280]{1,0:T(8,128)(2,1)S(1)}, bf16[256,1280]{1,0:T(8,128)(2,1)}, u32[]{:S(2)}) copy-start(bf16[256,1280]{1,0:T(8,128)(2,1)} %get-tuple-element.44.rest_0_.rest_6_) | copy-start | bytes 1966084
  34.6 2.7 %copy-start.15 = (bf16[256,896]{1,0:T(8,128)(2,1)}, bf16[256,896]{1,0:T(8,128)(2,1)S(1)}, u32[]{:S(2)}) copy-start(bf16[256,896]{1,0:T(8,128)(2,1)S(1)} %collective-permute-done.rest_2_.rest_8_.rest_14_) | copy-start | bytes 1376260
  34.6 2.7 %copy-start.16 = (bf16[256,896]{1,0:T(8,128)(2,1)}, bf16[256,896]{1,0:T(8,128)(2,1)S(1)}, u32[]{:S(2)}) copy-start(bf16[256,896]{1,0:T(8,128)(2,1)S(1)} %collective-permute-done.1.rest_4_.rest_10_.rest_16_) | copy-start | bytes 1376260
  34.6 1.9 collective-permute-start.6
  34.7 2.6 %collective-permute-start.7 = (bf16[256,896]{1,0:T(8,128)(2,1)S(1)}, bf16[256,896]{1,0:T(8,128)(2,1)}, u32[]{:S(2)}, u32[]{:S(2)}) collective-permute-start(bf16[256,896]{1,0:T(8,128)(2,1)S(1)} %collective-permute-done.1.rest_4_.rest_10_.rest_16_), channel_id=1, source_target_pairs={{0,1},{1,0},{2,3},{3,2},{4,5},{5,4},{6,7},{7,6},{8,9},{9,8},{10,11... | collective-permute-start | bytes 1376264 | tf_op jit(solution)/shard_map/ppermute | solution.py:436
  36.4 24.5 %collective-permute-start.2 = (bf16[256,1280]{1,0:T(8,128)(2,1)S(1)}, bf16[256,1280]{1,0:T(8,128)(2,1)S(1)}, u32[]{:S(2)}, u32[]{:S(2)}) collective-permute-start(bf16[256,1280]{1,0:T(8,128)(2,1)S(1)} %copy-done.9), channel_id=1, source_target_pairs={{0,1},{1,0},{2,3},{3,2},{4,5},{5,4},{6,7},{7,6},{8,9},{9,8},{10,11... | collective-permute-start | bytes 1966088 | tf_op jit(solution)/shard_map/ppermute | solution.py:436
  36.5 0.8 copy-start.17
  60.2 4.0 %copy-start.10 = (bf16[256,1280]{1,0:T(8,128)(2,1)}, bf16[256,1280]{1,0:T(8,128)(2,1)S(1)}, u32[]{:S(2)}) copy-start(bf16[256,1280]{1,0:T(8,128)(2,1)S(1)} %collective-permute-done.3.rest_2_.rest_8_) | copy-start | bytes 1966084
  60.2 4.0 %copy-start.11 = (bf16[256,1280]{1,0:T(8,128)(2,1)}, bf16[256,1280]{1,0:T(8,128)(2,1)S(1)}, u32[]{:S(2)}) copy-start(bf16[256,1280]{1,0:T(8,128)(2,1)S(1)} %collective-permute-done.4.rest_4_.rest_10_) | copy-start | bytes 1966084
  60.2 2.2 %collective-permute-start.8 = (bf16[256,1280]{1,0:T(8,128)(2,1)S(1)}, bf16[256,1280]{1,0:T(8,128)(2,1)S(1)}, u32[]{:S(2)}, u32[]{:S(2)}) collective-permute-start(bf16[256,1280]{1,0:T(8,128)(2,1)S(1)} %collective-permute-done.3.rest_2_.rest_8_), channel_id=1, source_target_pairs={{0,1},{1,0},{2,3},{3,2},{4,5},{5,4},{6,7},{7,6},{8,9},{9,8},{10,11... | collective-permute-start | bytes 1966088 | tf_op jit(solution)/shard_map/ppermute | solution.py:436
  60.6 2.7 %collective-permute-start.9 = (bf16[256,1280]{1,0:T(8,128)(2,1)S(1)}, bf16[256,1280]{1,0:T(8,128)(2,1)S(1)}, u32[]{:S(2)}, u32[]{:S(2)}) collective-permute-start(bf16[256,1280]{1,0:T(8,128)(2,1)S(1)} %collective-permute-done.4.rest_4_.rest_10_), channel_id=1, source_target_pairs={{0,1},{1,0},{2,3},{3,2},{4,5},{5,4},{6,7},{7,6},{8,9},{9,8},{10,11... | collective-permute-start | bytes 1966088 | tf_op jit(solution)/shard_map/ppermute | solution.py:436
  60.9 3.3 %copy-start.12 = (bf16[256,1280]{1,0:T(8,128)(2,1)}, bf16[256,1280]{1,0:T(8,128)(2,1)S(1)}, u32[]{:S(2)}) copy-start(bf16[256,1280]{1,0:T(8,128)(2,1)S(1)} %collective-permute-done.2.rest_1_.rest_7_) | copy-start | bytes 1966084
  62.4 1.8 copy-start.13
  63.3 0.9 copy-start.14
  100.1 12.9 %copy-start.8 = (bf16[3,256,1024]{2,1,0:T(8,128)(2,1)S(1)}, bf16[3,256,1024]{2,1,0:T(8,128)(2,1)}, u32[]{:S(2)}) copy-start(bf16[3,256,1024]{2,1,0:T(8,128)(2,1)} %get-tuple-element.61) | copy-start | bytes 4718596
  100.1 1.8 collective-permute-start.10
  101.9 11.1 %collective-permute-start.13 = (bf16[3,256,1024]{2,1,0:T(8,128)(2,1)}, bf16[3,256,1024]{2,1,0:T(8,128)(2,1)S(1)}, u32[]{:S(2)}, u32[]{:S(2)}) collective-permute-start(bf16[3,256,1024]{2,1,0:T(8,128)(2,1)} %get-tuple-element.62), channel_id=1, source_target_pairs={{0,1},{1,0},{2,3},{3,2},{4,5},{5,4},{6,7},{7,6},{8,9},{9,8},{10,11... | collective-permute-start | bytes 4718600 | tf_op jit(solution)/shard_map/ppermute | solution.py:436
  103.3 11.7 %collective-permute-start.11 = (bf16[256,64]{1,0:T(8,128)(2,1)S(1)}, bf16[256,64]{1,0:T(8,128)(2,1)S(1)}, u32[]{:S(2)}, u32[]{:S(2)}) collective-permute-start(bf16[256,64]{1,0:T(8,128)(2,1)S(1)} %get-tuple-element.87), channel_id=1, source_target_pairs={{2,0},{3,1},{4,2},{5,3},{6,4},{7,5},{8,6},{9,7},{10,8},{11,9},{12,... | collective-permute-start | bytes 98312 | tf_op jit(solution)/shard_map/ppermute | solution.py:436
  107.6 10.7 %collective-permute-start.12 = (bf16[256,64]{1,0:T(8,128)(2,1)S(1)}, bf16[256,64]{1,0:T(8,128)(2,1)S(1)}, u32[]{:S(2)}, u32[]{:S(2)}) collective-permute-start(bf16[256,64]{1,0:T(8,128)(2,1)S(1)} %get-tuple-element.86), channel_id=1, source_target_pairs={{4,0},{5,1},{6,2},{7,3},{8,4},{9,5},{10,6},{11,7},{12,8},{13,9},{1... | collective-permute-start | bytes 98312 | tf_op jit(solution)/shard_map/ppermute | solution.py:436
  113.8 4.4 %copy-start = (bf16[256,5120]{1,0:T(8,128)(2,1)S(1)}, bf16[256,5120]{1,0:T(8,128)(2,1)}, u32[]{:S(2)}) copy-start(bf16[256,5120]{1,0:T(8,128)(2,1)} %normed.3) | copy-start | bytes 7864324
  113.9 4.4 %copy-start.1 = (bf16[48,64,128]{2,1,0:T(8,128)(2,1)S(1)}, bf16[48,64,128]{2,1,0:T(8,128)(2,1)}, u32[]{:S(2)}) copy-start(bf16[48,64,128]{2,1,0:T(8,128)(2,1)} %get-tuple-element.71.heads) | copy-start | bytes 2359300
  113.9 4.4 %copy-start.2 = (f32[256,64]{1,0:T(8,128)S(1)}, f32[256,64]{1,0:T(8,128)}, u32[]{:S(2)}) copy-start(f32[256,64]{1,0:T(8,128)} %get-tuple-element.68.total_q) | copy-start | bytes 196612
  119.1 2.7 %collective-permute-start.16 = (bf16[64,64,128]{2,1,0:T(8,128)(2,1)S(1)}, bf16[64,64,128]{2,1,0:T(8,128)(2,1)S(1)}, u32[]{:S(2)}, u32[]{:S(2)}) collective-permute-start(bf16[64,64,128]{2,1,0:T(8,128)(2,1)S(1)} %get-tuple-element.73), channel_id=1, source_target_pairs={{0,1},{1,0},{2,3},{3,2},{4,5},{5,4},{6,7},{7,6},{8,9},{9,8},{10,11... | collective-permute-start | bytes 3145736 | tf_op jit(solution)/shard_map/ppermute | solution.py:436
  123.2 35.1 %all-to-all-start = ((bf16[64,64,128]{2,1,0:T(8,128)(2,1)}), bf16[64,64,128]{2,1,0:T(8,128)(2,1)S(1)}, u32[]{:S(2)}, u32[]{:S(2)}) async-start(bf16[64,64,128]{2,1,0:T(8,128)(2,1)} %add_convert_fusion), calls=%async_computation | async-start | bytes 2097152 | tf_op jit(solution)/shard_map/all_to_all | solution.py:515
  133.4 38.1 %collective-permute-start.14 = (bf16[256,1024]{1,0:T(8,128)(2,1)S(1)}, bf16[256,1024]{1,0:T(8,128)(2,1)S(1)}, u32[]{:S(2)}, u32[]{:S(2)}) collective-permute-start(bf16[256,1024]{1,0:T(8,128)(2,1)S(1)} %get-tuple-element.64), channel_id=1, source_target_pairs={{2,0},{3,1},{4,2},{5,3},{6,4},{7,5},{8,6},{9,7},{10,8},{11,9},{12,... | collective-permute-start | bytes 1572872 | tf_op jit(solution)/shard_map/ppermute | solution.py:436
  158.3 1.0 copy-start.5
  161.7 20.5 %all-to-all-start.1 = ((bf16[64,64,128]{2,1,0:T(8,128)(2,1)}), bf16[64,64,128]{2,1,0:T(8,128)(2,1)S(1)}, u32[]{:S(2)}, u32[]{:S(2)}) async-start(bf16[64,64,128]{2,1,0:T(8,128)(2,1)} %sum_and_copy.1), calls=%async_computation.1 | async-start | bytes 2097152 | tf_op jit(solution)/shard_map/all_to_all | solution.py:518
  171.5 16.0 %collective-permute-start.15 = (bf16[256,1024]{1,0:T(8,128)(2,1)}, bf16[256,1024]{1,0:T(8,128)(2,1)S(1)}, u32[]{:S(2)}, u32[]{:S(2)}) collective-permute-start(bf16[256,1024]{1,0:T(8,128)(2,1)} %get-tuple-element.67), channel_id=1, source_target_pairs={{4,0},{5,1},{6,2},{7,3},{8,4},{9,5},{10,6},{11,7},{12,8},{13,9},{1... | collective-permute-start | bytes 1572872 | tf_op jit(solution)/shard_map/ppermute | solution.py:436
  182.2 5.8 %copy-start.4 = (bf16[64,64,128]{2,1,0:T(8,128)(2,1)}, bf16[64,64,128]{2,1,0:T(8,128)(2,1)S(1)}, u32[]{:S(2)}) copy-start(bf16[64,64,128]{2,1,0:T(8,128)(2,1)S(1)} %all-to-all-done.1.mine) | copy-start | bytes 3145732
  182.2 8.6 %collective-permute-start.17 = (bf16[64,64,128]{2,1,0:T(8,128)(2,1)S(1)}, bf16[64,64,128]{2,1,0:T(8,128)(2,1)}, u32[]{:S(2)}, u32[]{:S(2)}) collective-permute-start(bf16[64,64,128]{2,1,0:T(8,128)(2,1)S(1)} %all-to-all-done.1.mine), channel_id=1, source_target_pairs={{0,1},{1,0},{2,3},{3,2},{4,5},{5,4},{6,7},{7,6},{8,9},{9,8},{10,11... | collective-permute-start | bytes 3145736 | tf_op jit(solution)/shard_map/ppermute | solution.py:436
  188.0 0.9 copy-start.7
  188.3 0.9 copy-start.6

commit v5 on v4

--- a/solution.py
+++ b/solution.py
@@ -319,39 +319,38 @@
 
 
 def finish_kernel(scale, core, mine, other, down_q, up_q, down_v, up_v):
-    def write(low, high):
-        for place, half in enumerate((low, high)):
-            for i in range(HEADS // 2):
-                h = place * HEADS // 2 + i
-                for c in range(SHARE):
-                    at = (h * SHARE + c) * HD
-                    up_q[:, at : at + HD] = half[i * UNIT + c].astype(F32) * scale
-                up_v[:, h * HD : (h + 1) * HD] = half[i * UNIT + SHARE].astype(F32) * scale
-            tiles = down_q.shape[1] // HD // 2
-            for i in range(tiles):
-                col = slice((place * tiles + i) * HD, (place * tiles + i + 1) * HD)
-                down_q[:, col] = half[EDGE // 2 + i].astype(F32) * scale
-                down_v[:, col] = half[EDGE // 2 + tiles + i].astype(F32) * scale
-
-    @pl.when(core[0] == 0)
+    def write(half):
+        for i in range(HEADS // 2):
+            for c in range(SHARE):
+                at = (i * SHARE + c) * HD
+                up_q[:, at : at + HD] = half[i * UNIT + c].astype(F32) * scale
+            up_v[:, i * HD : (i + 1) * HD] = half[i * UNIT + SHARE].astype(F32) * scale
+        tiles = down_q.shape[1] // HD
+        for i in range(tiles):
+            col = slice(i * HD, (i + 1) * HD)
+            down_q[:, col] = half[EDGE // 2 + i].astype(F32) * scale
+            down_v[:, col] = half[EDGE // 2 + tiles + i].astype(F32) * scale
+
+    place = pl.program_id(0)
+
+    @pl.when(core[0] == place)
     def _():
-        write(mine, other)
-
-    @pl.when(core[0] != 0)
+        write(mine)
+
+    @pl.when(core[0] != place)
     def _():
-        write(other, mine)
+        write(other)
 
 
 def finish(core, mine, other, tokens, width):
-    vmem = pl.BlockSpec(memory_space=pltpu.VMEM)
-    query = jax.ShapeDtypeStruct((RANK, HEADS * SHARE * HD), F32)
-    down = jax.ShapeDtypeStruct((RANK, width), F32)
-    value = jax.ShapeDtypeStruct((RANK, HEADS * HD), F32)
+    whole = pl.BlockSpec(mine.shape, lambda p: (0, 0, 0))
+    shapes = [(RANK, width), (RANK, HEADS * SHARE * HD), (RANK, width), (RANK, HEADS * HD)]
     return pl.pallas_call(
         functools.partial(finish_kernel, 1.0 / tokens),
-        out_shape=[down, query, down, value],
-        in_specs=[pl.BlockSpec(memory_space=pltpu.SMEM), vmem, vmem],
-        out_specs=[vmem] * 4,
+        out_shape=[jax.ShapeDtypeStruct(shape, F32) for shape in shapes],
+        grid=(2,),
+        in_specs=[pl.BlockSpec(memory_space=pltpu.SMEM), whole, whole],
+        out_specs=[pl.BlockSpec((shape[0], shape[1] // 2), lambda p: (0, p)) for shape in shapes],
         compiler_params=pltpu.CompilerParams(vmem_limit_bytes=VMEM_ASK),
         name="finish",
     )(core, mine, other)
@@ -508,13 +507,13 @@
     keyed = key_mine.astype(F32) + twin(key_other).astype(F32)
     own, one, two = keyed[0], keyed[1].astype(BF), keyed[2].astype(BF)
     lift_near, lift_far, own, one, two = lax.optimization_barrier((lift_near, lift_far, own, one, two))
-    key_near = ahead(one, -1)
+    key_far = ahead(two, -2)
     kept, given = gradients(core[None], lift_q, lifts[0], lift_near, lift_far, normed_input, heads)
     kept = (kept.astype(F32) + twin(given).astype(F32)).astype(BF)
     cores = [list(range(c, devices, 2)) for c in range(2)]
     spread = lax.all_to_all(kept, "ctx", 0, 0, axis_index_groups=cores, tiled=True)
-    key_near, two = lax.optimization_barrier((key_near, two))
-    key_far = ahead(two, -2)
+    key_far, one = lax.optimization_barrier((key_far, one))
+    key_near = ahead(one, -1)
     gathered = lax.all_to_all(sum_and_copy(spread), "ctx", 0, 0, axis_index_groups=cores, tiled=True)
     sums = finish(core[None], gathered, twin(gathered), TOK * devices, normed_input.shape[1])
     key_total = (own + (key_near.astype(F32) + key_far.astype(F32))).reshape(TOK, HEADS, HD)

time: 196 us -> 196 us (level)
  waiting for transfers between devices: 45.4 us -> 35.5 us
  starting transfers between devices: 52.6 us -> 62.3 us
    all_to_all x1, waiting for transfers between devices: 22.2 us -> 12.1 us  [on_device(): lax.all_to_all(kept, 'ctx', 0, 0, axis_index_groups=cores, tiled=True)]
    all_to_all x1, starting transfers between devices: 9.75 us -> 19.4 us  [on_device(): lax.all_to_all(sum_and_copy(spread), 'ctx', 0, 0, axis_index_groups=cores...]
where the time goes in v5:
time: 196 us; the launch traced here: 194 us
  Pallas kernels  78.2 us (40%)
  starting transfers between devices  62.3 us (32%)
  waiting for transfers between devices  35.5 us (18%)
  other arithmetic  8.75 us (4%)
  local copies, waits for them, and re-layouts  5.9 us (3%)
  between operations  3.67 us (2%)
    pallas_call x2, Pallas kernels, attention(): pl.pallas_call(functools.partial(attention_kernel, share, held is None),...  58.8 us
    ppermute x18, starting transfers between devices, moved(): return lax.ppermute(block, 'ctx', route)  32.7 us
    all_to_all x1, starting transfers between devices, on_device(): lax.all_to_all(sum_and_copy(spread), 'ctx', 0, 0, axis_index_groups=cores...  19.4 us
    ppermute x18, waiting for transfers between devices, moved(): return lax.ppermute(block, 'ctx', route)  16.2 us
    all_to_all x1, waiting for transfers between devices, on_device(): lax.all_to_all(kept, 'ctx', 0, 0, axis_index_groups=cores, tiled=True)  12.1 us
    all_to_all x1, starting transfers between devices, on_device(): lax.all_to_all(kept, 'ctx', 0, 0, axis_index_groups=cores, tiled=True)  10.1 us
    pallas_call x1, Pallas kernels, rotate_queries(): pl.pallas_call(rotate_kernel, out_shape=jax.ShapeDtypeStruct(frozen.shape...  7.58 us
    all_to_all x1, waiting for transfers between devices, on_device(): lax.all_to_all(sum_and_copy(spread), 'ctx', 0, 0, axis_index_groups=cores...  7.15 us
  transfers between devices with their start and end apart: 20, of which 10 were waited for; matrix products, arithmetic and copies ran while one was open for 4% of the time, Pallas kernels for 17%

profile of v5, /device:TPU:62, one launch (start us, length us, event | category | flops | bytes accessed | tf_op | source)
XLA Modules:
  0.0 194.3 jit_solution(8867009367067388678)
XLA Ops:
  0.7 1.2 dynamic_slice.3
  2.6 0.8 select_reduce_fusion.1
  3.4 0.5 fusion.2
  4.0 0.9 pad_maximum_fusion
  4.8 4.9 %prepare.1 = (bf16[256,896]{1,0:T(8,128)(2,1)}, bf16[256,1280]{1,0:T(8,128)(2,1)}) custom-call(bf16[256,5120]{1,0:T(8,128)(2,1)} %normed.3, bf16[64,5120]{1,0:T(8,128)(2,1)} %bitcast.38, bf16[64,5120]{1,0:T(8,128)(2,1)} %bitcast.39, bf16[256,1024]{1,0:T(8,128)(2,1)} %keys.1, bf16[256,1024]{1,0:T(8,128)(2,1)} %values.1, bf16[64,1024]{1,0:T(8,128)(2,1)} %vup.5, ...), custom_call_target="tpu_custom_call" | custom-call | tf_op jit(solution)/shard_map/prepare/pallas_call | solution.py:232
  9.7 3.4 %collective-permute-start = (bf16[256,896]{1,0:T(8,128)(2,1)}, bf16[256,896]{1,0:T(8,128)(2,1)S(1)}, u32[]{:S(2)}, u32[]{:S(2)}) collective-permute-start(bf16[256,896]{1,0:T(8,128)(2,1)} %get-tuple-element.42.lora.rest_0_.rest_6_.rest_12_), channel_id=1, source_target_pairs={{0,2},{1,3},{2,4},{3,5},{4,6},{5,7},{6,8},{7,9},{8,10},{9,11},{10,... | collective-permute-start | bytes 1376264 | tf_op jit(solution)/shard_map/ppermute | solution.py:435
  13.1 4.3 %collective-permute-start.1 = (bf16[256,896]{1,0:T(8,128)(2,1)}, bf16[256,896]{1,0:T(8,128)(2,1)S(1)}, u32[]{:S(2)}, u32[]{:S(2)}) collective-permute-start(bf16[256,896]{1,0:T(8,128)(2,1)} %get-tuple-element.42.lora.rest_0_.rest_6_.rest_12_), channel_id=1, source_target_pairs={{0,4},{1,5},{2,6},{3,7},{4,8},{5,9},{6,10},{7,11},{8,12},{9,13},{1... | collective-permute-start | bytes 1376264 | tf_op jit(solution)/shard_map/ppermute | solution.py:435
  17.5 3.7 %collective-permute-start.3 = (bf16[256,1280]{1,0:T(8,128)(2,1)}, bf16[256,1280]{1,0:T(8,128)(2,1)S(1)}, u32[]{:S(2)}, u32[]{:S(2)}) collective-permute-start(bf16[256,1280]{1,0:T(8,128)(2,1)} %get-tuple-element.44.rest_0_.rest_6_), channel_id=1, source_target_pairs={{0,2},{1,3},{2,4},{3,5},{4,6},{5,7},{6,8},{7,9},{8,10},{9,11},{10,... | collective-permute-start | bytes 1966088 | tf_op jit(solution)/shard_map/ppermute | solution.py:435
  21.2 3.1 %collective-permute-start.4 = (bf16[256,1280]{1,0:T(8,128)(2,1)}, bf16[256,1280]{1,0:T(8,128)(2,1)S(1)}, u32[]{:S(2)}, u32[]{:S(2)}) collective-permute-start(bf16[256,1280]{1,0:T(8,128)(2,1)} %get-tuple-element.44.rest_0_.rest_6_), channel_id=1, source_target_pairs={{0,4},{1,5},{2,6},{3,7},{4,8},{5,9},{6,10},{7,11},{8,12},{9,13},{1... | collective-permute-start | bytes 1966088 | tf_op jit(solution)/shard_map/ppermute | solution.py:435
  26.4 0.6 gather_fusion
  27.0 7.6 %rotate_queries.1.query = bf16[256,5120]{1,0:T(8,128)(2,1)} custom-call(bf16[256,5120]{1,0:T(8,128)(2,1)} %frozen.1, bf16[256,896]{1,0:T(8,128)(2,1)} %get-tuple-element.42.lora.rest_0_.rest_6_.rest_12_, bf16[64,5120]{1,0:T(8,128)(2,1)} %qup.5, f32[256,128]{1,0:T(8,128)} %get-tuple-element.91.cos, f32[256,128]{1,0:T(8,128)} %get-tuple-element.92.sin), custom_call_target="tpu_custom_call" | custom-call | tf_op jit(solution)/shard_map/rotate_queries/pallas_call | solution.py:254
  34.7 0.5 collective-permute-start.7
  35.2 0.5 subtract_subtract_fusion.dst
  35.8 0.7 pad_add_fusion.sc
  36.5 0.8 collective-permute-done.7.rest_5_.rest_11_.rest_17_
  37.3 22.8 %attention.2 = (bf16[256,5120]{1,0:T(8,128)(2,1)}, bf16[3,256,1024]{2,1,0:T(8,128)(2,1)}, bf16[3,256,1024]{2,1,0:T(8,128)(2,1)}, bf16[48,64,128]{2,1,0:T(8,128)(...) custom-call(s32[4]{0:T(128)} %pad_add_fusion.sc, bf16[256,5120]{1,0:T(8,128)(2,1)} %rotate_queries.1.query, ...), custom_call_target="tpu_custom_call" | custom-call | flops 6794772480 | bytes 2359296 | tf_op jit(solution)/shard_map/attention/pallas_call | solution.py:414
  60.2 0.4 collective-permute-start.8
  60.6 0.3 collective-permute-start.9
  60.9 1.5 collective-permute-done.8.rest_3_.rest_9_
  62.4 0.9 collective-permute-done.9.rest_5_.rest_11_
  63.3 0.9 copy-done.14
  64.2 35.9 %attention.3 = (bf16[256,5120]{1,0:T(8,128)(2,1)}, bf16[3,256,1024]{2,1,0:T(8,128)(2,1)}, bf16[3,256,1024]{2,1,0:T(8,128)(2,1)}, bf16[48,64,128]{2,1,0:T(8,128)(...) custom-call(s32[4]{0:T(128)} %pad_add_fusion.sc, ...), custom_call_target="tpu_custom_call", output_to_operand_aliasing={{0}: (29, {}), {1}: (30, {}), {2}: (31, {}), {3}: (32, {})} | custom-call | flops 11324620800 | bytes 3932160 | tf_op jit(solution)/shard_map/attention/pallas_call | solution.py:414
  100.1 0.5 collective-permute-start.10
  100.6 1.3 collective-permute-done.10
  101.9 0.4 collective-permute-start.13
  102.3 1.1 fusion.6
  103.3 4.3 %collective-permute-start.11 = (bf16[256,64]{1,0:T(8,128)(2,1)S(1)}, bf16[256,64]{1,0:T(8,128)(2,1)S(1)}, u32[]{:S(2)}, u32[]{:S(2)}) collective-permute-start(bf16[256,64]{1,0:T(8,128)(2,1)S(1)} %get-tuple-element.87), channel_id=1, source_target_pairs={{2,0},{3,1},{4,2},{5,3},{6,4},{7,5},{8,6},{9,7},{10,8},{11,9},{12,... | collective-permute-start | bytes 98312 | tf_op jit(solution)/shard_map/ppermute | solution.py:435
  107.6 5.4 %collective-permute-start.12 = (bf16[256,64]{1,0:T(8,128)(2,1)S(1)}, bf16[256,64]{1,0:T(8,128)(2,1)S(1)}, u32[]{:S(2)}, u32[]{:S(2)}) collective-permute-start(bf16[256,64]{1,0:T(8,128)(2,1)S(1)} %get-tuple-element.86), channel_id=1, source_target_pairs={{4,0},{5,1},{6,2},{7,3},{8,4},{9,5},{10,6},{11,7},{12,8},{13,9},{1... | collective-permute-start | bytes 98312 | tf_op jit(solution)/shard_map/ppermute | solution.py:435
  113.1 0.8 fusion.5
  114.0 0.9 slice_bitcast_fusion.1
  115.1 3.2 %collective-permute-done.12.far = bf16[256,64]{1,0:T(8,128)(2,1)S(1)} collective-permute-done((bf16[256,64]{1,0:T(8,128)(2,1)S(1)}, bf16[256,64]{1,0:T(8,128)(2,1)S(1)}, u32[]{:S(2)}, u32[]{:S(2)}) %collective-permute-start.12) | collective-permute-done | bytes 32800 | tf_op jit(solution)/shard_map/ppermute | solution.py:435
  118.3 0.8 gradients.1
  119.2 2.6 %collective-permute-done.16 = bf16[64,64,128]{2,1,0:T(8,128)(2,1)S(1)} collective-permute-done((bf16[64,64,128]{2,1,0:T(8,128)(2,1)S(1)}, bf16[64,64,128]{2,1,0:T(8,128)(2,1)S(1)}, u32[]{:S(2)}, u32[]{:S(2)}) %collective-permute-start.16) | collective-permute-done | bytes 1048608 | tf_op jit(solution)/shard_map/ppermute | solution.py:435
  121.9 1.4 add_convert_fusion
  123.2 10.1 %all-to-all-start = ((bf16[64,64,128]{2,1,0:T(8,128)(2,1)}), bf16[64,64,128]{2,1,0:T(8,128)(2,1)S(1)}, u32[]{:S(2)}, u32[]{:S(2)}) async-start(bf16[64,64,128]{2,1,0:T(8,128)(2,1)} %add_convert_fusion), calls=%async_computation | async-start | bytes 2097152 | tf_op jit(solution)/shard_map/all_to_all | solution.py:514
  133.4 3.4 %collective-permute-start.14 = (bf16[256,1024]{1,0:T(8,128)(2,1)S(1)}, bf16[256,1024]{1,0:T(8,128)(2,1)S(1)}, u32[]{:S(2)}, u32[]{:S(2)}) collective-permute-start(bf16[256,1024]{1,0:T(8,128)(2,1)S(1)} %get-tuple-element.64), channel_id=1, source_target_pairs={{4,0},{5,1},{6,2},{7,3},{8,4},{9,5},{10,6},{11,7},{12,8},{13,9},{1... | collective-permute-start | bytes 1572872 | tf_op jit(solution)/shard_map/ppermute | solution.py:435
  136.7 12.1 %all-to-all-done.spread = bf16[64,64,128]{2,1,0:T(8,128)(2,1)S(1)} async-done(((bf16[64,64,128]{2,1,0:T(8,128)(2,1)}), bf16[64,64,128]{2,1,0:T(8,128)(2,1)S(1)}, u32[]{:S(2)}, u32[]{:S(2)}) %all-to-all-start) | async-done | bytes 1048608 | tf_op jit(solution)/shard_map/all_to_all | solution.py:514
  148.9 1.0 copy-done.5
  149.8 2.5 %sum_and_copy.1 = bf16[64,64,128]{2,1,0:T(8,128)(2,1)} custom-call(bf16[64,64,128]{2,1,0:T(8,128)(2,1)} %copy-done.5), custom_call_target="tpu_custom_call" | custom-call | tf_op jit(solution)/shard_map/sum_and_copy/pallas_call | solution.py:316
  152.3 19.4 %all-to-all-start.1 = ((bf16[64,64,128]{2,1,0:T(8,128)(2,1)}), bf16[64,64,128]{2,1,0:T(8,128)(2,1)S(1)}, u32[]{:S(2)}, u32[]{:S(2)}) async-start(bf16[64,64,128]{2,1,0:T(8,128)(2,1)} %sum_and_copy.1), calls=%async_computation.1 | async-start | bytes 2097152 | tf_op jit(solution)/shard_map/all_to_all | solution.py:517
  171.7 2.8 %collective-permute-start.15 = (bf16[256,1024]{1,0:T(8,128)(2,1)}, bf16[256,1024]{1,0:T(8,128)(2,1)S(1)}, u32[]{:S(2)}, u32[]{:S(2)}) collective-permute-start(bf16[256,1024]{1,0:T(8,128)(2,1)} %get-tuple-element.66), channel_id=1, source_target_pairs={{2,0},{3,1},{4,2},{5,3},{6,4},{7,5},{8,6},{9,7},{10,8},{11,9},{12,... | collective-permute-start | bytes 1572872 | tf_op jit(solution)/shard_map/ppermute | solution.py:435
  174.5 7.1 %all-to-all-done.1.mine = bf16[64,64,128]{2,1,0:T(8,128)(2,1)S(1)} async-done(((bf16[64,64,128]{2,1,0:T(8,128)(2,1)}), bf16[64,64,128]{2,1,0:T(8,128)(2,1)S(1)}, u32[]{:S(2)}, u32[]{:S(2)}) %all-to-all-start.1) | async-done | bytes 1048608 | tf_op jit(solution)/shard_map/all_to_all | solution.py:517
  181.6 5.6 %collective-permute-done.15 = bf16[256,1024]{1,0:T(8,128)(2,1)S(1)} collective-permute-done((bf16[256,1024]{1,0:T(8,128)(2,1)}, bf16[256,1024]{1,0:T(8,128)(2,1)S(1)}, u32[]{:S(2)}, u32[]{:S(2)}) %collective-permute-start.15) | collective-permute-done | bytes 524320 | tf_op jit(solution)/shard_map/ppermute | solution.py:435
  187.7 0.3 fusion.7
  188.1 0.5 copy-done.7
  188.6 0.4 maximum_multiply_fusion
  189.1 1.5 fusion
  190.5 3.7 %finish.1 = (f32[64,5120]{1,0:T(8,128)}, f32[64,5120]{1,0:T(8,128)}, f32[64,5120]{1,0:T(8,128)}, f32[64,1024]{1,0:T(8,128)}) custom-call(s32[1]{0:T(128)} %bitcast.11.core, bf16[64,64,128]{2,1,0:T(8,128)(2,1)} %copy-done.4, bf16[64,64,128]{2,1,0:T(8,128)(2,1)} %collective-permute-done.17.other), custom_call_target="tpu_custom_call" | custom-call | tf_op jit(solution)/shard_map/finish/pallas_call | solution.py:348
  (62 shorter events, 1.4 us)
Async XLA Ops:
  4.8 21.5 %copy-start.3 = (s32[128]{0:T(128)S(1)}, s32[128]{0:T(128)}, u32[]{:S(2)}) copy-start(s32[128]{0:T(128)} %param.21) | copy-start | bytes 1540
  9.7 24.9 %collective-permute-start = (bf16[256,896]{1,0:T(8,128)(2,1)}, bf16[256,896]{1,0:T(8,128)(2,1)S(1)}, u32[]{:S(2)}, u32[]{:S(2)}) collective-permute-start(bf16[256,896]{1,0:T(8,128)(2,1)} %get-tuple-element.42.lora.rest_0_.rest_6_.rest_12_), channel_id=1, source_target_pairs={{0,2},{1,3},{2,4},{3,5},{4,6},{5,7},{6,8},{7,9},{8,10},{9,11},{10,... | collective-permute-start | bytes 1376264 | tf_op jit(solution)/shard_map/ppermute | solution.py:435
  13.1 21.5 %collective-permute-start.1 = (bf16[256,896]{1,0:T(8,128)(2,1)}, bf16[256,896]{1,0:T(8,128)(2,1)S(1)}, u32[]{:S(2)}, u32[]{:S(2)}) collective-permute-start(bf16[256,896]{1,0:T(8,128)(2,1)} %get-tuple-element.42.lora.rest_0_.rest_6_.rest_12_), channel_id=1, source_target_pairs={{0,4},{1,5},{2,6},{3,7},{4,8},{5,9},{6,10},{7,11},{8,12},{9,13},{1... | collective-permute-start | bytes 1376264 | tf_op jit(solution)/shard_map/ppermute | solution.py:435
  17.4 19.0 %collective-permute-start.5 = (bf16[256,896]{1,0:T(8,128)(2,1)}, bf16[256,896]{1,0:T(8,128)(2,1)}, u32[]{:S(2)}, u32[]{:S(2)}) collective-permute-start(bf16[256,896]{1,0:T(8,128)(2,1)} %get-tuple-element.42.lora.rest_0_.rest_6_.rest_12_), channel_id=1, source_target_pairs={{0,1},{1,0},{2,3},{3,2},{4,5},{5,4},{6,7},{7,6},{8,9},{9,8},{10,11... | collective-permute-start | bytes 1376264 | tf_op jit(solution)/shard_map/ppermute | solution.py:435
  17.5 42.6 %collective-permute-start.3 = (bf16[256,1280]{1,0:T(8,128)(2,1)}, bf16[256,1280]{1,0:T(8,128)(2,1)S(1)}, u32[]{:S(2)}, u32[]{:S(2)}) collective-permute-start(bf16[256,1280]{1,0:T(8,128)(2,1)} %get-tuple-element.44.rest_0_.rest_6_), channel_id=1, source_target_pairs={{0,2},{1,3},{2,4},{3,5},{4,6},{5,7},{6,8},{7,9},{8,10},{9,11},{10,... | collective-permute-start | bytes 1966088 | tf_op jit(solution)/shard_map/ppermute | solution.py:435
  21.2 38.9 %collective-permute-start.4 = (bf16[256,1280]{1,0:T(8,128)(2,1)}, bf16[256,1280]{1,0:T(8,128)(2,1)S(1)}, u32[]{:S(2)}, u32[]{:S(2)}) collective-permute-start(bf16[256,1280]{1,0:T(8,128)(2,1)} %get-tuple-element.44.rest_0_.rest_6_), channel_id=1, source_target_pairs={{0,4},{1,5},{2,6},{3,7},{4,8},{5,9},{6,10},{7,11},{8,12},{9,13},{1... | collective-permute-start | bytes 1966088 | tf_op jit(solution)/shard_map/ppermute | solution.py:435
  27.0 9.4 %copy-start.9 = (bf16[256,1280]{1,0:T(8,128)(2,1)S(1)}, bf16[256,1280]{1,0:T(8,128)(2,1)}, u32[]{:S(2)}) copy-start(bf16[256,1280]{1,0:T(8,128)(2,1)} %get-tuple-element.44.rest_0_.rest_6_) | copy-start | bytes 1966084
  34.6 2.7 %copy-start.15 = (bf16[256,896]{1,0:T(8,128)(2,1)}, bf16[256,896]{1,0:T(8,128)(2,1)S(1)}, u32[]{:S(2)}) copy-start(bf16[256,896]{1,0:T(8,128)(2,1)S(1)} %collective-permute-done.rest_2_.rest_8_.rest_14_) | copy-start | bytes 1376260
  34.6 2.7 %copy-start.16 = (bf16[256,896]{1,0:T(8,128)(2,1)}, bf16[256,896]{1,0:T(8,128)(2,1)S(1)}, u32[]{:S(2)}) copy-start(bf16[256,896]{1,0:T(8,128)(2,1)S(1)} %collective-permute-done.1.rest_4_.rest_10_.rest_16_) | copy-start | bytes 1376260
  34.6 1.9 collective-permute-start.6
  34.7 2.6 %collective-permute-start.7 = (bf16[256,896]{1,0:T(8,128)(2,1)S(1)}, bf16[256,896]{1,0:T(8,128)(2,1)}, u32[]{:S(2)}, u32[]{:S(2)}) collective-permute-start(bf16[256,896]{1,0:T(8,128)(2,1)S(1)} %collective-permute-done.1.rest_4_.rest_10_.rest_16_), channel_id=1, source_target_pairs={{0,1},{1,0},{2,3},{3,2},{4,5},{5,4},{6,7},{7,6},{8,9},{9,8},{10,11... | collective-permute-start | bytes 1376264 | tf_op jit(solution)/shard_map/ppermute | solution.py:435
  36.4 24.5 %collective-permute-start.2 = (bf16[256,1280]{1,0:T(8,128)(2,1)S(1)}, bf16[256,1280]{1,0:T(8,128)(2,1)S(1)}, u32[]{:S(2)}, u32[]{:S(2)}) collective-permute-start(bf16[256,1280]{1,0:T(8,128)(2,1)S(1)} %copy-done.9), channel_id=1, source_target_pairs={{0,1},{1,0},{2,3},{3,2},{4,5},{5,4},{6,7},{7,6},{8,9},{9,8},{10,11... | collective-permute-start | bytes 1966088 | tf_op jit(solution)/shard_map/ppermute | solution.py:435
  36.5 0.8 copy-start.17
  60.2 4.0 %copy-start.10 = (bf16[256,1280]{1,0:T(8,128)(2,1)}, bf16[256,1280]{1,0:T(8,128)(2,1)S(1)}, u32[]{:S(2)}) copy-start(bf16[256,1280]{1,0:T(8,128)(2,1)S(1)} %collective-permute-done.3.rest_2_.rest_8_) | copy-start | bytes 1966084
  60.2 4.0 %copy-start.11 = (bf16[256,1280]{1,0:T(8,128)(2,1)}, bf16[256,1280]{1,0:T(8,128)(2,1)S(1)}, u32[]{:S(2)}) copy-start(bf16[256,1280]{1,0:T(8,128)(2,1)S(1)} %collective-permute-done.4.rest_4_.rest_10_) | copy-start | bytes 1966084
  60.2 2.2 %collective-permute-start.8 = (bf16[256,1280]{1,0:T(8,128)(2,1)S(1)}, bf16[256,1280]{1,0:T(8,128)(2,1)S(1)}, u32[]{:S(2)}, u32[]{:S(2)}) collective-permute-start(bf16[256,1280]{1,0:T(8,128)(2,1)S(1)} %collective-permute-done.3.rest_2_.rest_8_), channel_id=1, source_target_pairs={{0,1},{1,0},{2,3},{3,2},{4,5},{5,4},{6,7},{7,6},{8,9},{9,8},{10,11... | collective-permute-start | bytes 1966088 | tf_op jit(solution)/shard_map/ppermute | solution.py:435
  60.6 2.7 %collective-permute-start.9 = (bf16[256,1280]{1,0:T(8,128)(2,1)S(1)}, bf16[256,1280]{1,0:T(8,128)(2,1)S(1)}, u32[]{:S(2)}, u32[]{:S(2)}) collective-permute-start(bf16[256,1280]{1,0:T(8,128)(2,1)S(1)} %collective-permute-done.4.rest_4_.rest_10_), channel_id=1, source_target_pairs={{0,1},{1,0},{2,3},{3,2},{4,5},{5,4},{6,7},{7,6},{8,9},{9,8},{10,11... | collective-permute-start | bytes 1966088 | tf_op jit(solution)/shard_map/ppermute | solution.py:435
  60.9 3.3 %copy-start.12 = (bf16[256,1280]{1,0:T(8,128)(2,1)}, bf16[256,1280]{1,0:T(8,128)(2,1)S(1)}, u32[]{:S(2)}) copy-start(bf16[256,1280]{1,0:T(8,128)(2,1)S(1)} %collective-permute-done.2.rest_1_.rest_7_) | copy-start | bytes 1966084
  62.4 1.8 copy-start.13
  63.3 0.9 copy-start.14
  100.1 12.9 %copy-start.8 = (bf16[3,256,1024]{2,1,0:T(8,128)(2,1)S(1)}, bf16[3,256,1024]{2,1,0:T(8,128)(2,1)}, u32[]{:S(2)}) copy-start(bf16[3,256,1024]{2,1,0:T(8,128)(2,1)} %get-tuple-element.61) | copy-start | bytes 4718596
  100.1 1.8 collective-permute-start.10
  101.9 11.2 %collective-permute-start.13 = (bf16[3,256,1024]{2,1,0:T(8,128)(2,1)}, bf16[3,256,1024]{2,1,0:T(8,128)(2,1)S(1)}, u32[]{:S(2)}, u32[]{:S(2)}) collective-permute-start(bf16[3,256,1024]{2,1,0:T(8,128)(2,1)} %get-tuple-element.62), channel_id=1, source_target_pairs={{0,1},{1,0},{2,3},{3,2},{4,5},{5,4},{6,7},{7,6},{8,9},{9,8},{10,11... | collective-permute-start | bytes 4718600 | tf_op jit(solution)/shard_map/ppermute | solution.py:435
  103.3 11.7 %collective-permute-start.11 = (bf16[256,64]{1,0:T(8,128)(2,1)S(1)}, bf16[256,64]{1,0:T(8,128)(2,1)S(1)}, u32[]{:S(2)}, u32[]{:S(2)}) collective-permute-start(bf16[256,64]{1,0:T(8,128)(2,1)S(1)} %get-tuple-element.87), channel_id=1, source_target_pairs={{2,0},{3,1},{4,2},{5,3},{6,4},{7,5},{8,6},{9,7},{10,8},{11,9},{12,... | collective-permute-start | bytes 98312 | tf_op jit(solution)/shard_map/ppermute | solution.py:435
  107.6 10.7 %collective-permute-start.12 = (bf16[256,64]{1,0:T(8,128)(2,1)S(1)}, bf16[256,64]{1,0:T(8,128)(2,1)S(1)}, u32[]{:S(2)}, u32[]{:S(2)}) collective-permute-start(bf16[256,64]{1,0:T(8,128)(2,1)S(1)} %get-tuple-element.86), channel_id=1, source_target_pairs={{4,0},{5,1},{6,2},{7,3},{8,4},{9,5},{10,6},{11,7},{12,8},{13,9},{1... | collective-permute-start | bytes 98312 | tf_op jit(solution)/shard_map/ppermute | solution.py:435
  113.9 4.4 %copy-start = (bf16[256,5120]{1,0:T(8,128)(2,1)S(1)}, bf16[256,5120]{1,0:T(8,128)(2,1)}, u32[]{:S(2)}) copy-start(bf16[256,5120]{1,0:T(8,128)(2,1)} %normed.3) | copy-start | bytes 7864324
  113.9 4.4 %copy-start.1 = (bf16[48,64,128]{2,1,0:T(8,128)(2,1)S(1)}, bf16[48,64,128]{2,1,0:T(8,128)(2,1)}, u32[]{:S(2)}) copy-start(bf16[48,64,128]{2,1,0:T(8,128)(2,1)} %get-tuple-element.71.heads) | copy-start | bytes 2359300
  113.9 4.4 %copy-start.2 = (f32[256,64]{1,0:T(8,128)S(1)}, f32[256,64]{1,0:T(8,128)}, u32[]{:S(2)}) copy-start(f32[256,64]{1,0:T(8,128)} %get-tuple-element.68.total_q) | copy-start | bytes 196612
  119.1 2.7 %collective-permute-start.16 = (bf16[64,64,128]{2,1,0:T(8,128)(2,1)S(1)}, bf16[64,64,128]{2,1,0:T(8,128)(2,1)S(1)}, u32[]{:S(2)}, u32[]{:S(2)}) collective-permute-start(bf16[64,64,128]{2,1,0:T(8,128)(2,1)S(1)} %get-tuple-element.73), channel_id=1, source_target_pairs={{0,1},{1,0},{2,3},{3,2},{4,5},{5,4},{6,7},{7,6},{8,9},{9,8},{10,11... | collective-permute-start | bytes 3145736 | tf_op jit(solution)/shard_map/ppermute | solution.py:435
  123.2 25.6 %all-to-all-start = ((bf16[64,64,128]{2,1,0:T(8,128)(2,1)}), bf16[64,64,128]{2,1,0:T(8,128)(2,1)S(1)}, u32[]{:S(2)}, u32[]{:S(2)}) async-start(bf16[64,64,128]{2,1,0:T(8,128)(2,1)} %add_convert_fusion), calls=%async_computation | async-start | bytes 2097152 | tf_op jit(solution)/shard_map/all_to_all | solution.py:514
  133.4 38.4 %collective-permute-start.14 = (bf16[256,1024]{1,0:T(8,128)(2,1)S(1)}, bf16[256,1024]{1,0:T(8,128)(2,1)S(1)}, u32[]{:S(2)}, u32[]{:S(2)}) collective-permute-start(bf16[256,1024]{1,0:T(8,128)(2,1)S(1)} %get-tuple-element.64), channel_id=1, source_target_pairs={{4,0},{5,1},{6,2},{7,3},{8,4},{9,5},{10,6},{11,7},{12,8},{13,9},{1... | collective-permute-start | bytes 1572872 | tf_op jit(solution)/shard_map/ppermute | solution.py:435
  148.9 1.0 copy-start.5
  152.3 29.4 %all-to-all-start.1 = ((bf16[64,64,128]{2,1,0:T(8,128)(2,1)}), bf16[64,64,128]{2,1,0:T(8,128)(2,1)S(1)}, u32[]{:S(2)}, u32[]{:S(2)}) async-start(bf16[64,64,128]{2,1,0:T(8,128)(2,1)} %sum_and_copy.1), calls=%async_computation.1 | async-start | bytes 2097152 | tf_op jit(solution)/shard_map/all_to_all | solution.py:517
  171.7 15.5 %collective-permute-start.15 = (bf16[256,1024]{1,0:T(8,128)(2,1)}, bf16[256,1024]{1,0:T(8,128)(2,1)S(1)}, u32[]{:S(2)}, u32[]{:S(2)}) collective-permute-start(bf16[256,1024]{1,0:T(8,128)(2,1)} %get-tuple-element.66), channel_id=1, source_target_pairs={{2,0},{3,1},{4,2},{5,3},{6,4},{7,5},{8,6},{9,7},{10,8},{11,9},{12,... | collective-permute-start | bytes 1572872 | tf_op jit(solution)/shard_map/ppermute | solution.py:435
  181.6 6.1 %copy-start.4 = (bf16[64,64,128]{2,1,0:T(8,128)(2,1)}, bf16[64,64,128]{2,1,0:T(8,128)(2,1)S(1)}, u32[]{:S(2)}) copy-start(bf16[64,64,128]{2,1,0:T(8,128)(2,1)S(1)} %all-to-all-done.1.mine) | copy-start | bytes 3145732
  181.6 8.9 %collective-permute-start.17 = (bf16[64,64,128]{2,1,0:T(8,128)(2,1)S(1)}, bf16[64,64,128]{2,1,0:T(8,128)(2,1)}, u32[]{:S(2)}, u32[]{:S(2)}) collective-permute-start(bf16[64,64,128]{2,1,0:T(8,128)(2,1)S(1)} %all-to-all-done.1.mine), channel_id=1, source_target_pairs={{0,1},{1,0},{2,3},{3,2},{4,5},{5,4},{6,7},{7,6},{8,9},{9,8},{10,11... | collective-permute-start | bytes 3145736 | tf_op jit(solution)/shard_map/ppermute | solution.py:435
  187.7 0.9 copy-start.7
  188.1 0.9 copy-start.6
